TPU v7x, 512 devices: a whole 4x8x8 slice. The times are simulated.
512 devices in a mesh: grp: 16 (over z_hi, x, core), shard: 32 (over y, z_lo).
Axes of the slice: x: 4, y: 8, z: 8 (z_hi: 2, z_lo: 4; z = z_hi * 4 + z_lo), core: 2. Of those that a mesh axis runs over, the one named last changes fastest.
Arguments:
- query_states: bfloat16 [131072, 512], P(('grp', 'shard')), may hold values from -7.5 to 7.5
- key_states: bfloat16 [131072, 512], P(('grp', 'shard')), may hold values from -7.5 to 7.5
- value_states: bfloat16 [131072, 512], P(('grp', 'shard')), may hold values from -7.5 to 7.5
- valid_mask: int32 [131072], P(('grp', 'shard')), may hold values from 0 to 1, as said below
- attended_grad: bfloat16 [131072, 512], P(('grp', 'shard')), may hold values from -7.5 to 7.5
Outputs:
- attended: bfloat16 [131072, 512], P(('grp', 'shard'))
- query_grad: bfloat16 [131072, 512], P(('grp', 'shard'))
- key_grad: bfloat16 [131072, 512], P(('grp', 'shard'))
- value_grad: bfloat16 [131072, 512], P(('grp', 'shard'))
Inputs may be any that keep to these rules, and one draw needn't show every extreme that they name: `valid_mask`: in each device's run of 256 positions the ones form a prefix of 64 to 256 positions; the first run is all ones and the last has exactly 64.
All inputs are finite; a program needn't handle non-finite values.
Results may differ from a plain program's by a relative error of at most 0.0055.
Values may be sent and summed in bfloat16 or wider, within the bound.
No kernel may reach another device: no remote copies, remote signals or barrier semaphores. Data moves between devices by JAX's collectives and lax.ppermute only.
A program may use at most 128 MiB of HBM per device.

v0:
```python
import jax
import jax.numpy as jnp
from jax import lax
from jax.sharding import PartitionSpec as P

HEADS = 4
HEAD_DIM = 128
BLOCK = 128
COARSE = 64


MASKED = -1e30


def extended(block, sides, width):
    for axis, dim in sides:
        count = lax.axis_size(axis)
        forward = [(i, i + 1) for i in range(count - 1)]
        backward = [(target, source) for source, target in forward]
        low = lax.ppermute(
            lax.slice_in_dim(block, block.shape[dim] - width, None, axis=dim), axis, forward
        )
        high = lax.ppermute(lax.slice_in_dim(block, 0, width, axis=dim), axis, backward)
        block = jnp.concatenate([low, block, high], axis=dim)
    return block


def swapped(block, axis, stride):
    count = lax.axis_size(axis)
    route = []
    for low in range(count):
        high = low | 1 << stride
        if high != low and high < count:
            route += [(low, high), (high, low)]
    return lax.ppermute(block, axis, route)


def as_sent(value):
    return jax.tree.map(lambda a: a.astype(jnp.bfloat16) if a.dtype == jnp.float32 else a, value)


def merge_rows(tiles):
    shape = tiles.shape
    return tiles.reshape(shape[:-3] + (shape[-3] // 2, 2) + shape[-2:]).sum(axis=-3)


def merge_counts(counts):
    shape = counts.shape
    return counts.reshape(shape[:-1] + (shape[-1] // 2, 2)).sum(axis=-1)


def widen_rows(grad):
    shape = grad.shape
    doubled = jnp.broadcast_to(grad[..., :, None, :, :], shape[:-3] + (shape[-3], 2) + shape[-2:])
    return doubled.reshape(shape[:-3] + (2 * shape[-3],) + shape[-2:])


def ordered(sibling_side_flag, first_part, second_part):
    lower_part = jnp.where(sibling_side_flag == 0, first_part, second_part)
    upper_part = jnp.where(sibling_side_flag == 0, second_part, first_part)
    return (lower_part, upper_part)


def climb_level(own_tile, own_count, partner, partner_count, sibling_side_flag):
    lower_tile, upper_tile = ordered(sibling_side_flag, own_tile, partner)
    lower_count, upper_count = ordered(sibling_side_flag, own_count, partner_count)
    merged = merge_rows(jnp.concatenate([lower_tile, upper_tile], axis=0))
    merged_count = merge_counts(jnp.concatenate([lower_count, upper_count], axis=0))
    return (merged, merged_count)


def split_grad(grad_own, sibling_side_flag):
    halves = widen_rows(grad_own)
    row_half = grad_own.shape[0]
    return ordered(sibling_side_flag, halves[:row_half], halves[row_half:])


def body(query_states, key_states, value_states, valid_mask, attended_grad):
    tok_rows, feat_width = query_states.shape
    score_scale = HEAD_DIM ** (-0.5)
    nblocks = tok_rows // BLOCK
    span_len = 2 * BLOCK
    nspans = tok_rows // span_len
    group_size = span_len // COARSE
    leaf_rows = tok_rows // group_size
    shard_bits = lax.axis_size("shard").bit_length() - 1
    grp_bits = lax.axis_size("grp").bit_length() - 1
    mask_float = valid_mask.astype(jnp.float32)
    mask_half = valid_mask.astype(jnp.bfloat16)
    kv_states = jnp.stack([key_states, value_states], axis=1)
    ext_kv, ext_mask = (
        extended(kv_states, ((("grp", "shard"), 0),), BLOCK),
        extended(mask_half, ((("grp", "shard"), 0),), BLOCK),
    )
    leaf_sums = jnp.einsum(
        "rgcw,rg->rcw",
        kv_states.reshape(leaf_rows, group_size, 2, feat_width),
        mask_half.reshape(leaf_rows, group_size),
        preferred_element_type=jnp.float32,
    )
    leaf_count = mask_float.reshape(leaf_rows, group_size).sum(axis=1)
    span_tiles = leaf_sums.reshape(nspans, COARSE, 2, feat_width)
    per_span_counts = leaf_count.reshape(nspans, COARSE)
    own_tile = span_tiles[0]
    own_count = per_span_counts[0]
    cross_sib = []
    cross_cnt = []
    shard_sides = []
    shard_index = lax.axis_index("shard")
    for level_bit in range(shard_bits):
        sibling_side_flag = shard_index >> level_bit & 1
        partner, partner_count = swapped((own_tile, own_count), "shard", level_bit)
        cross_sib.append(partner)
        cross_cnt.append(partner_count)
        shard_sides.append(sibling_side_flag)
        own_tile, own_count = climb_level(
            own_tile, own_count, partner, partner_count, sibling_side_flag
        )
    grp_index = lax.axis_index("grp")
    grp_sides = []
    for level_bit in range(grp_bits):
        sibling_side_flag = grp_index >> level_bit & 1
        partner, partner_count = swapped((own_tile, own_count), "grp", level_bit)
        cross_sib.append(partner)
        cross_cnt.append(partner_count)
        grp_sides.append(sibling_side_flag)
        if level_bit + 1 < grp_bits:
            own_tile, own_count = climb_level(
                own_tile, own_count, partner, partner_count, sibling_side_flag
            )
    cross_tiles = jnp.stack(cross_sib, axis=0).reshape(-1, 2, feat_width)
    cross_count = jnp.stack(cross_cnt, axis=0).reshape(-1)
    far_parts = cross_tiles[None]
    far_counts = cross_count[None]
    far_rows = far_parts.shape[1]
    count_floor = jnp.maximum(far_counts, 1.0)
    far_mean = (far_parts / count_floor[..., None, None]).astype(jnp.bfloat16)
    far_live = far_counts > 0
    far_keys = far_mean[:, :, 0]
    far_vals = far_mean[:, :, 1]
    near_kv = jnp.concatenate(
        [
            ext_kv[:tok_rows].reshape(nblocks, BLOCK, 2, feat_width),
            ext_kv[BLOCK : BLOCK + tok_rows].reshape(nblocks, BLOCK, 2, feat_width),
            ext_kv[2 * BLOCK :].reshape(nblocks, BLOCK, 2, feat_width),
        ],
        axis=1,
    )
    near_mask = jnp.concatenate(
        [
            ext_mask[:tok_rows].reshape(nblocks, BLOCK),
            ext_mask[BLOCK : BLOCK + tok_rows].reshape(nblocks, BLOCK),
            ext_mask[2 * BLOCK :].reshape(nblocks, BLOCK),
        ],
        axis=1,
    )
    near_keys = near_kv[:, :, 0]
    near_vals = near_kv[:, :, 1]
    query_blocks = query_states.reshape(nblocks, BLOCK, feat_width)
    query_spans = query_states.reshape(nspans, span_len, feat_width)
    cot_blocks = attended_grad.reshape(nblocks, BLOCK, feat_width)
    cot_spans = attended_grad.reshape(nspans, span_len, feat_width)
    near_ok = near_mask[:, None, :] > 0
    far_ok = far_live[:, None, :]
    attended_heads = []
    query_heads = []
    near_gk_heads = []
    near_gv_heads = []
    far_gk_heads = []
    far_gv_heads = []
    for head in range(HEADS):
        low = head * HEAD_DIM
        high = low + HEAD_DIM
        query_block_rows = query_blocks[:, :, low:high]
        q_span = query_spans[:, :, low:high]
        coarse_block_rows = cot_blocks[:, :, low:high]
        c_span = cot_spans[:, :, low:high]
        nearby_key_rows = near_keys[:, :, low:high]
        nearby_value_rows = near_vals[:, :, low:high]
        k_far = far_keys[:, :, low:high]
        v_far = far_vals[:, :, low:high]
        near_score = (
            jnp.einsum(
                "pwf,prf->pwr",
                query_block_rows,
                nearby_key_rows,
                preferred_element_type=jnp.float32,
            )
            * score_scale
        )
        near_score = jnp.where(near_ok, near_score, MASKED).reshape(tok_rows, 3 * BLOCK)
        far_score = (
            jnp.einsum("sqd,skd->sqk", q_span, k_far, preferred_element_type=jnp.float32)
            * score_scale
        )
        far_score = jnp.where(far_ok, far_score, MASKED).reshape(tok_rows, far_rows)
        row_max = jnp.maximum(near_score.max(axis=-1), far_score.max(axis=-1))
        near_exp = jnp.exp(near_score - row_max[:, None])
        far_exp = jnp.exp(far_score - row_max[:, None])
        row_total = near_exp.sum(axis=-1) + far_exp.sum(axis=-1)
        near_prob = near_exp / row_total[:, None]
        far_prob = far_exp / row_total[:, None]
        nearby_half_rows = near_prob.astype(jnp.bfloat16).reshape(nblocks, BLOCK, 3 * BLOCK)
        far_half = far_prob.astype(jnp.bfloat16).reshape(nspans, span_len, far_rows)
        out_near = jnp.einsum(
            "pun,pni->pui", nearby_half_rows, nearby_value_rows, preferred_element_type=jnp.float32
        ).reshape(tok_rows, HEAD_DIM)
        out_far = jnp.einsum(
            "sqk,skd->sqd", far_half, v_far, preferred_element_type=jnp.float32
        ).reshape(tok_rows, HEAD_DIM)
        attended_heads.append(out_near + out_far)
        near_dp = jnp.einsum(
            "pwf,prf->pwr", coarse_block_rows, nearby_value_rows, preferred_element_type=jnp.float32
        ).reshape(tok_rows, 3 * BLOCK)
        far_dp = jnp.einsum(
            "sqd,skd->sqk", c_span, v_far, preferred_element_type=jnp.float32
        ).reshape(tok_rows, far_rows)
        row_delta = (near_prob * near_dp).sum(axis=-1) + (far_prob * far_dp).sum(axis=-1)
        nearby_delta_score = (
            (near_prob * (near_dp - row_delta[:, None]))
            .astype(jnp.bfloat16)
            .reshape(nblocks, BLOCK, 3 * BLOCK)
        )
        far_ds = (
            (far_prob * (far_dp - row_delta[:, None]))
            .astype(jnp.bfloat16)
            .reshape(nspans, span_len, far_rows)
        )
        grad_near = jnp.einsum(
            "pun,pni->pui", nearby_delta_score, nearby_key_rows, preferred_element_type=jnp.float32
        ).reshape(tok_rows, HEAD_DIM)
        grad_far = jnp.einsum(
            "sqk,skd->sqd", far_ds, k_far, preferred_element_type=jnp.float32
        ).reshape(tok_rows, HEAD_DIM)
        query_heads.append(score_scale * (grad_near + grad_far))
        near_gk_heads.append(
            score_scale
            * jnp.einsum(
                "gmu,gmw->guw",
                nearby_delta_score,
                query_block_rows,
                preferred_element_type=jnp.float32,
            )
        )
        near_gv_heads.append(
            jnp.einsum(
                "gmu,gmw->guw",
                nearby_half_rows,
                coarse_block_rows,
                preferred_element_type=jnp.float32,
            )
        )
        far_gk_heads.append(
            score_scale
            * jnp.einsum("sqk,sqd->skd", far_ds, q_span, preferred_element_type=jnp.float32)
        )
        far_gv_heads.append(
            jnp.einsum("sqk,sqd->skd", far_half, c_span, preferred_element_type=jnp.float32)
        )
    attended = jnp.concatenate(attended_heads, axis=1).astype(jnp.bfloat16)
    query_grad = jnp.concatenate(query_heads, axis=1).astype(jnp.bfloat16)
    near_gk = jnp.concatenate(near_gk_heads, axis=2)
    near_gv = jnp.concatenate(near_gv_heads, axis=2)
    near_grad = jnp.stack([near_gk, near_gv], axis=2)
    pieces = near_grad.reshape(nblocks, 3, BLOCK, 2, feat_width)
    ext_grad = jnp.pad(pieces[:, 0], ((0, 2), (0, 0), (0, 0), (0, 0)))
    ext_grad = ext_grad + jnp.pad(pieces[:, 1], ((1, 1), (0, 0), (0, 0), (0, 0)))
    ext_grad = ext_grad + jnp.pad(pieces[:, 2], ((2, 0), (0, 0), (0, 0), (0, 0)))
    edge_rows = jnp.concatenate([ext_grad[0], ext_grad[nblocks + 1]], axis=0)
    returned = extended(edge_rows, ((("grp", "shard"), 0),), BLOCK)
    kv_grad = ext_grad[1 : nblocks + 1].reshape(tok_rows, 2, feat_width)
    kv_grad = (
        kv_grad.at[:BLOCK].add(returned[:BLOCK]).at[tok_rows - BLOCK :].add(returned[3 * BLOCK :])
    )
    far_gk = jnp.concatenate(far_gk_heads, axis=2)
    far_gv = jnp.concatenate(far_gv_heads, axis=2)
    far_grad = jnp.stack([far_gk, far_gv], axis=2)
    far_grad = far_grad / count_floor[..., None, None]
    cross_grad = far_grad.sum(axis=0).reshape(shard_bits + grp_bits, COARSE, 2, feat_width)
    grad_own = jnp.zeros((COARSE, 2, feat_width), jnp.float32)
    for level_bit in reversed(range(grp_bits)):
        if level_bit + 1 < grp_bits:
            mine_part, their_part = split_grad(grad_own, grp_sides[level_bit])
        else:
            mine_part = jnp.zeros((COARSE, 2, feat_width), jnp.float32)
            their_part = jnp.zeros((COARSE, 2, feat_width), jnp.float32)
        grad_own = mine_part + swapped(
            as_sent(cross_grad[shard_bits + level_bit] + their_part), "grp", level_bit
        )
    for level_bit in reversed(range(shard_bits)):
        mine_part, their_part = split_grad(grad_own, shard_sides[level_bit])
        grad_own = mine_part + swapped(cross_grad[level_bit] + their_part, "shard", level_bit)
    tile_grad = grad_own[None]
    spread = tile_grad.reshape(leaf_rows, 1, 2, feat_width) * mask_float.reshape(
        leaf_rows, group_size, 1, 1
    )
    kv_grad = kv_grad + spread.reshape(tok_rows, 2, feat_width)
    return (
        attended,
        query_grad,
        kv_grad[:, 0].astype(jnp.bfloat16),
        kv_grad[:, 1].astype(jnp.bfloat16),
    )


def solution(mesh):
    return jax.shard_map(
        body,
        mesh=mesh,
        in_specs=(
            P(("grp", "shard"), None),
            P(("grp", "shard"), None),
            P(("grp", "shard"), None),
            P(("grp", "shard")),
            P(("grp", "shard"), None),
        ),
        out_specs=(
            P(("grp", "shard"), None),
            P(("grp", "shard"), None),
            P(("grp", "shard"), None),
            P(("grp", "shard"), None),
        ),
        check_vma=False,
    )
```

profile of v0, /device:TPU:1, one launch (start us, length us, event | category | flops | bytes accessed | tf_op | source)
XLA Modules:
  0.0 422.9 jit_solution(5062532277438319971)
XLA Ops:
  1.8 4.8 %collective-permute-start.2 = (bf16[128,2,512]{2,0,1:T(8,128)(2,1)S(1)}, bf16[128,2,512]{2,0,1:T(8,128)(2,1)S(1)}, u32[]{:S(2)}, u32[]{:S(2)}) collective-permute-start(bf16[128,2,512]{2,0,1:T(8,128)(2,1)S(1)} %get-tuple-element.69), channel_id=1, source_target_pairs={{0,1},{1,2},{2,3},{3,4},{4,5},{5,6},{6,7},{7,8},{8,9},{9,10},{10,1... | collective-permute-start | bytes 786440 | tf_op jit(solution)/shard_map/ppermute | solution.py:20
  6.6 9.0 %collective-permute-start.3 = (bf16[128,2,512]{2,0,1:T(8,128)(2,1)S(1)}, bf16[128,2,512]{2,0,1:T(8,128)(2,1)S(1)}, u32[]{:S(2)}, u32[]{:S(2)}) collective-permute-start(bf16[128,2,512]{2,0,1:T(8,128)(2,1)S(1)} %get-tuple-element.70), channel_id=1, source_target_pairs={{1,0},{2,1},{3,2},{4,3},{5,4},{6,5},{7,6},{8,7},{9,8},{10,9},{11,1... | collective-permute-start | bytes 786440 | tf_op jit(solution)/shard_map/ppermute | solution.py:23
  18.3 7.5 %collective-permute-start.1 = (bf16[128]{0:T(256)(128)(2,1)S(1)}, bf16[128]{0:T(256)(128)(2,1)S(1)}, u32[]{:S(2)}, u32[]{:S(2)}) collective-permute-start(bf16[128]{0:T(256)(128)(2,1)S(1)} %get-tuple-element.108), channel_id=1, source_target_pairs={{1,0},{2,1},{3,2},{4,3},{5,4},{6,5},{7,6},{8,7},{9,8},{10,9},{11,1... | collective-permute-start | bytes 776 | tf_op jit(solution)/shard_map/ppermute | solution.py:23
  33.0 3.2 collective-permute-done.5
  38.7 2.4 collective-permute-done.6
  41.5 2.1 collective-permute-start.7
  43.7 3.2 collective-permute-done.7
  47.3 3.6 collective-permute-start.8
  50.9 4.6 %collective-permute-done.8 = f32[64]{0:T(128)S(1)} collective-permute-done((f32[64]{0:T(128)S(1)}, f32[64]{0:T(128)S(1)}, u32[]{:S(2)}, u32[]{:S(2)}) %collective-permute-start.8) | collective-permute-done | bytes 288 | tf_op jit(solution)/shard_map/ppermute | solution.py:35
  56.0 5.0 %collective-permute-start.9 = (f32[64]{0:T(128)S(1)}, f32[64]{0:T(128)S(1)}, u32[]{:S(2)}, u32[]{:S(2)}) collective-permute-start(f32[64]{0:T(128)S(1)} %maximum_reduce_fusion.4), channel_id=1, source_target_pairs={{0,32},{32,0},{64,96},{96,64},{128,160},{160,128},{192,224},{224,1... | collective-permute-start | bytes 776 | tf_op jit(solution)/shard_map/ppermute | solution.py:35
  61.8 2.7 collective-permute-start.13
  65.0 6.2 %collective-permute-start.10 = (f32[64]{0:T(128)S(1)}, f32[64]{0:T(128)S(1)}, u32[]{:S(2)}, u32[]{:S(2)}) collective-permute-start(f32[64]{0:T(128)S(1)} %maximum_reduce_fusion.5), channel_id=1, source_target_pairs={{0,64},{64,0},{32,96},{96,32},{128,192},{192,128},{160,224},{224,1... | collective-permute-start | bytes 776 | tf_op jit(solution)/shard_map/ppermute | solution.py:35
  72.6 5.2 %collective-permute-start.11 = (f32[64]{0:T(128)S(1)}, f32[64]{0:T(128)S(1)}, u32[]{:S(2)}, u32[]{:S(2)}) collective-permute-start(f32[64]{0:T(128)S(1)} %maximum_reduce_fusion.6), channel_id=1, source_target_pairs={{0,128},{128,0},{32,160},{160,32},{64,192},{192,64},{96,224},{224,... | collective-permute-start | bytes 776 | tf_op jit(solution)/shard_map/ppermute | solution.py:35
  79.2 10.3 %collective-permute-start.12 = (f32[64]{0:T(128)S(1)}, f32[64]{0:T(128)S(1)}, u32[]{:S(2)}, u32[]{:S(2)}) collective-permute-start(f32[64]{0:T(128)S(1)} %maximum_reduce_fusion.7), channel_id=1, source_target_pairs={{0,256},{256,0},{32,288},{288,32},{64,320},{320,64},{96,352},{352,... | collective-permute-start | bytes 776 | tf_op jit(solution)/shard_map/ppermute | solution.py:35
  94.5 13.4 %collective-permute-done.14 = f32[64,2,512]{2,0,1:T(8,128)S(1)} collective-permute-done((f32[64,2,512]{2,0,1:T(8,128)S(1)}, f32[64,2,512]{2,0,1:T(8,128)S(1)}, u32[]{:S(2)}, u32[]{:S(2)}) %collective-permute-start.14) | collective-permute-done | bytes 262176 | tf_op jit(solution)/shard_map/ppermute | solution.py:35
  112.6 5.2 %collective-permute-done.15 = f32[64,2,512]{2,0,1:T(8,128)S(1)} collective-permute-done((f32[64,2,512]{2,0,1:T(8,128)S(1)}, f32[64,2,512]{2,0,1:T(8,128)S(1)}, u32[]{:S(2)}, u32[]{:S(2)}) %collective-permute-start.15) | collective-permute-done | bytes 262176 | tf_op jit(solution)/shard_map/ppermute | solution.py:35
  123.2 12.2 %collective-permute-done.16 = f32[64,2,512]{2,0,1:T(8,128)S(1)} collective-permute-done((f32[64,2,512]{2,0,1:T(8,128)S(1)}, f32[64,2,512]{2,0,1:T(8,128)S(1)}, u32[]{:S(2)}, u32[]{:S(2)}) %collective-permute-start.16) | collective-permute-done | bytes 262176 | tf_op jit(solution)/shard_map/ppermute | solution.py:35
  136.4 5.0 %collective-permute-start.17 = (f32[64,2,512]{2,0,1:T(8,128)S(1)}, f32[64,2,512]{2,0,1:T(8,128)S(1)}, u32[]{:S(2)}, u32[]{:S(2)}) collective-permute-start(f32[64,2,512]{2,0,1:T(8,128)S(1)} %reduce_sum.345), channel_id=1, source_target_pairs={{0,16},{16,0},{1,17},{17,1},{2,18},{18,2},{3,19},{19,3},{4,20},{20... | collective-permute-start | bytes 786440 | tf_op jit(solution)/shard_map/ppermute | solution.py:35
  143.8 12.3 %collective-permute-done.17 = f32[64,2,512]{2,0,1:T(8,128)S(1)} collective-permute-done((f32[64,2,512]{2,0,1:T(8,128)S(1)}, f32[64,2,512]{2,0,1:T(8,128)S(1)}, u32[]{:S(2)}, u32[]{:S(2)}) %collective-permute-start.17) | collective-permute-done | bytes 262176 | tf_op jit(solution)/shard_map/ppermute | solution.py:35
  157.8 2.4 collective-permute-start.18
  164.7 2.1 reshape.951
  166.8 2.4 reduce_sum.347
  169.2 2.3 collective-permute-start.19
  173.4 5.8 %collective-permute-done.19 = f32[64,2,512]{2,0,1:T(8,128)S(1)} collective-permute-done((f32[64,2,512]{2,0,1:T(8,128)}, f32[64,2,512]{2,0,1:T(8,128)S(1)}, u32[]{:S(2)}, u32[]{:S(2)}) %collective-permute-start.19) | collective-permute-done | bytes 262176 | tf_op jit(solution)/shard_map/ppermute | solution.py:35
  181.8 2.1 reshape.952
  183.9 2.4 reduce_sum.348
  186.3 3.5 collective-permute-start.20
  191.7 5.2 %collective-permute-done.20 = f32[64,2,512]{2,0,1:T(8,128)S(1)} collective-permute-done((f32[64,2,512]{2,0,1:T(8,128)}, f32[64,2,512]{2,0,1:T(8,128)S(1)}, u32[]{:S(2)}, u32[]{:S(2)}) %collective-permute-start.20) | collective-permute-done | bytes 262176 | tf_op jit(solution)/shard_map/ppermute | solution.py:35
  199.4 2.1 reshape.953
  201.6 2.4 reduce_sum.349
  203.9 6.7 %collective-permute-start.21 = (f32[64,2,512]{2,0,1:T(8,128)}, f32[64,2,512]{2,0,1:T(8,128)S(1)}, u32[]{:S(2)}, u32[]{:S(2)}) collective-permute-start(f32[64,2,512]{2,0,1:T(8,128)} %reduce_sum.349), channel_id=1, source_target_pairs={{0,256},{256,0},{32,288},{288,32},{64,320},{320,64},{96,352},{352,... | collective-permute-start | bytes 786440 | tf_op jit(solution)/shard_map/ppermute | solution.py:35
  212.6 9.5 %collective-permute-done.21 = f32[64,2,512]{2,0,1:T(8,128)S(1)} collective-permute-done((f32[64,2,512]{2,0,1:T(8,128)}, f32[64,2,512]{2,0,1:T(8,128)S(1)}, u32[]{:S(2)}, u32[]{:S(2)}) %collective-permute-start.21) | collective-permute-done | bytes 262176 | tf_op jit(solution)/shard_map/ppermute | solution.py:35
  254.6 2.0 fusion.23
  276.7 4.2 collective-permute-start.24
  282.8 5.3 %collective-permute-done.24 = bf16[64,2,512]{2,0,1:T(8,128)(2,1)S(1)} collective-permute-done((bf16[64,2,512]{2,0,1:T(8,128)(2,1)S(1)}, bf16[64,2,512]{2,0,1:T(8,128)(2,1)S(1)}, u32[]{:S(2)}, u32[]{:S(2)}) %collective-permute-start.24) | collective-permute-done | bytes 131104 | tf_op jit(solution)/shard_map/ppermute | solution.py:35
  293.0 3.8 collective-permute-start.25
  307.3 2.2 collective-permute-start.26
  309.5 2.3 pad_maximum_fusion.1
  315.3 5.2 %collective-permute-start.27 = (bf16[64,2,512]{2,0,1:T(8,128)(2,1)}, bf16[64,2,512]{2,0,1:T(8,128)(2,1)}, u32[]{:S(2)}, u32[]{:S(2)}) collective-permute-start(bf16[64,2,512]{2,0,1:T(8,128)(2,1)} %fusion.70), channel_id=1, source_target_pairs={{0,32},{32,0},{64,96},{96,64},{128,160},{160,128},{192,224},{224,1... | collective-permute-start | bytes 393224 | tf_op jit(solution)/shard_map/ppermute | solution.py:35
  320.5 3.6 fusion.32
  332.1 4.2 collective-permute-start.28
  336.3 2.1 pad_add_fusion
  338.6 2.5 fusion.21
  341.4 7.7 %collective-permute-done.28 = f32[64,2,512]{2,0,1:T(8,128)} collective-permute-done((f32[64,2,512]{2,0,1:T(8,128)}, f32[64,2,512]{2,0,1:T(8,128)}, u32[]{:S(2)}, u32[]{:S(2)}) %collective-permute-start.28) | collective-permute-done | bytes 262176 | tf_op jit(solution)/shard_map/ppermute | solution.py:35
  354.7 10.1 %collective-permute-done.29 = f32[64,2,512]{2,0,1:T(8,128)} collective-permute-done((f32[64,2,512]{2,0,1:T(8,128)S(1)}, f32[64,2,512]{2,0,1:T(8,128)}, u32[]{:S(2)}, u32[]{:S(2)}) %collective-permute-start.29) | collective-permute-done | bytes 262176 | tf_op jit(solution)/shard_map/ppermute | solution.py:35
  376.4 7.7 %collective-permute-start.23 = (f32[128,2,512]{2,0,1:T(8,128)}, f32[128,2,512]{2,0,1:T(8,128)}, u32[]{:S(2)}, u32[]{:S(2)}) collective-permute-start(f32[128,2,512]{2,0,1:T(8,128)} %get-tuple-element.43), channel_id=1, source_target_pairs={{1,0},{2,1},{3,2},{4,3},{5,4},{6,5},{7,6},{8,7},{9,8},{10,9},{11,1... | collective-permute-start | bytes 1572872 | tf_op jit(solution)/shard_map/ppermute | solution.py:23
  394.0 17.7 %collective-permute-done.31 = f32[64,2,512]{2,0,1:T(8,128)S(1)} collective-permute-done((f32[64,2,512]{2,0,1:T(8,128)}, f32[64,2,512]{2,0,1:T(8,128)S(1)}, u32[]{:S(2)}, u32[]{:S(2)}) %collective-permute-start.31) | collective-permute-done | bytes 262176 | tf_op jit(solution)/shard_map/ppermute | solution.py:35
  416.5 4.8 %collective-permute-done.32 = f32[64,2,512]{2,0,1:T(8,128)S(1)} collective-permute-done((f32[64,2,512]{2,0,1:T(8,128)S(1)}, f32[64,2,512]{2,0,1:T(8,128)S(1)}, u32[]{:S(2)}, u32[]{:S(2)}) %collective-permute-start.32) | collective-permute-done | bytes 262176 | tf_op jit(solution)/shard_map/ppermute | solution.py:35
  (461 shorter events, 168.2 us)
Async XLA Ops:
  1.8 92.5 %collective-permute-start.2 = (bf16[128,2,512]{2,0,1:T(8,128)(2,1)S(1)}, bf16[128,2,512]{2,0,1:T(8,128)(2,1)S(1)}, u32[]{:S(2)}, u32[]{:S(2)}) collective-permute-start(bf16[128,2,512]{2,0,1:T(8,128)(2,1)S(1)} %get-tuple-element.69), channel_id=1, source_target_pairs={{0,1},{1,2},{2,3},{3,4},{4,5},{5,6},{6,7},{7,8},{8,9},{9,10},{10,1... | collective-permute-start | bytes 786440 | tf_op jit(solution)/shard_map/ppermute | solution.py:20
  6.6 87.7 %collective-permute-start.3 = (bf16[128,2,512]{2,0,1:T(8,128)(2,1)S(1)}, bf16[128,2,512]{2,0,1:T(8,128)(2,1)S(1)}, u32[]{:S(2)}, u32[]{:S(2)}) collective-permute-start(bf16[128,2,512]{2,0,1:T(8,128)(2,1)S(1)} %get-tuple-element.70), channel_id=1, source_target_pairs={{1,0},{2,1},{3,2},{4,3},{5,4},{6,5},{7,6},{8,7},{9,8},{10,9},{11,1... | collective-permute-start | bytes 786440 | tf_op jit(solution)/shard_map/ppermute | solution.py:23
  16.4 48.5 %copy-start.55 = (f32[256]{0:T(256)}, f32[256]{0:T(256)S(1)}, u32[]{:S(2)}) copy-start(f32[256]{0:T(256)S(1)} %get-tuple-element.103) | copy-start | bytes 3076
  16.4 48.6 %collective-permute-start = (bf16[128]{0:T(256)(128)(2,1)S(1)}, bf16[128]{0:T(256)(128)(2,1)S(1)}, u32[]{:S(2)}, u32[]{:S(2)}) collective-permute-start(bf16[128]{0:T(256)(128)(2,1)S(1)} %get-tuple-element.107), channel_id=1, source_target_pairs={{0,1},{1,2},{2,3},{3,4},{4,5},{5,6},{6,7},{7,8},{8,9},{9,10},{10,1... | collective-permute-start | bytes 776 | tf_op jit(solution)/shard_map/ppermute | solution.py:20
  18.3 52.9 %collective-permute-start.1 = (bf16[128]{0:T(256)(128)(2,1)S(1)}, bf16[128]{0:T(256)(128)(2,1)S(1)}, u32[]{:S(2)}, u32[]{:S(2)}) collective-permute-start(bf16[128]{0:T(256)(128)(2,1)S(1)} %get-tuple-element.108), channel_id=1, source_target_pairs={{1,0},{2,1},{3,2},{4,3},{5,4},{6,5},{7,6},{8,7},{9,8},{10,9},{11,1... | collective-permute-start | bytes 776 | tf_op jit(solution)/shard_map/ppermute | solution.py:23
  26.1 4.5 %collective-permute-start.4 = (f32[64]{0:T(128)S(1)}, f32[64]{0:T(128)S(1)}, u32[]{:S(2)}, u32[]{:S(2)}) collective-permute-start(f32[64]{0:T(128)S(1)} %reduce_sum.333), channel_id=1, source_target_pairs={{0,1},{1,0},{2,3},{3,2},{4,5},{5,4},{6,7},{7,6},{8,9},{9,8},{10,11... | collective-permute-start | bytes 776 | tf_op jit(solution)/shard_map/ppermute | solution.py:35
  31.1 5.2 %collective-permute-start.5 = (f32[64]{0:T(128)S(1)}, f32[64]{0:T(128)S(1)}, u32[]{:S(2)}, u32[]{:S(2)}) collective-permute-start(f32[64]{0:T(128)S(1)} %maximum_reduce_fusion), channel_id=1, source_target_pairs={{0,2},{2,0},{1,3},{3,1},{4,6},{6,4},{5,7},{7,5},{8,10},{10,8},{9,1... | collective-permute-start | bytes 776 | tf_op jit(solution)/shard_map/ppermute | solution.py:35
  36.8 4.3 %collective-permute-start.6 = (f32[64]{0:T(128)S(1)}, f32[64]{0:T(128)S(1)}, u32[]{:S(2)}, u32[]{:S(2)}) collective-permute-start(f32[64]{0:T(128)S(1)} %maximum_reduce_fusion.1), channel_id=1, source_target_pairs={{0,4},{4,0},{1,5},{5,1},{2,6},{6,2},{3,7},{7,3},{8,12},{12,8},{9,1... | collective-permute-start | bytes 776 | tf_op jit(solution)/shard_map/ppermute | solution.py:35
  41.5 52.8 %copy-start.3 = (bf16[256,512]{1,0:T(8,128)(2,1)S(1)}, bf16[256,512]{1,0:T(8,128)(2,1)}, u32[]{:S(2)}) copy-start(bf16[256,512]{1,0:T(8,128)(2,1)} %param.10) | copy-start | bytes 786436
  41.5 52.8 %copy-start.4 = (bf16[256,512]{1,0:T(8,128)(2,1)S(1)}, bf16[256,512]{1,0:T(8,128)(2,1)}, u32[]{:S(2)}) copy-start(bf16[256,512]{1,0:T(8,128)(2,1)} %param.11) | copy-start | bytes 786436
  41.5 5.3 %collective-permute-start.7 = (f32[64]{0:T(128)S(1)}, f32[64]{0:T(128)S(1)}, u32[]{:S(2)}, u32[]{:S(2)}) collective-permute-start(f32[64]{0:T(128)S(1)} %maximum_reduce_fusion.2), channel_id=1, source_target_pairs={{0,8},{8,0},{1,9},{9,1},{2,10},{10,2},{3,11},{11,3},{4,12},{12,4},... | collective-permute-start | bytes 776 | tf_op jit(solution)/shard_map/ppermute | solution.py:35
  47.3 8.2 %collective-permute-start.8 = (f32[64]{0:T(128)S(1)}, f32[64]{0:T(128)S(1)}, u32[]{:S(2)}, u32[]{:S(2)}) collective-permute-start(f32[64]{0:T(128)S(1)} %maximum_reduce_fusion.3), channel_id=1, source_target_pairs={{0,16},{16,0},{1,17},{17,1},{2,18},{18,2},{3,19},{19,3},{4,20},{20... | collective-permute-start | bytes 776 | tf_op jit(solution)/shard_map/ppermute | solution.py:35
  56.0 5.8 %collective-permute-start.9 = (f32[64]{0:T(128)S(1)}, f32[64]{0:T(128)S(1)}, u32[]{:S(2)}, u32[]{:S(2)}) collective-permute-start(f32[64]{0:T(128)S(1)} %maximum_reduce_fusion.4), channel_id=1, source_target_pairs={{0,32},{32,0},{64,96},{96,64},{128,160},{160,128},{192,224},{224,1... | collective-permute-start | bytes 776 | tf_op jit(solution)/shard_map/ppermute | solution.py:35
  61.8 28.9 %collective-permute-start.13 = (f32[64,2,512]{2,0,1:T(8,128)S(1)}, f32[64,2,512]{2,0,1:T(8,128)S(1)}, u32[]{:S(2)}, u32[]{:S(2)}) collective-permute-start(f32[64,2,512]{2,0,1:T(8,128)S(1)} %bitcast.466), channel_id=1, source_target_pairs={{0,1},{1,0},{2,3},{3,2},{4,5},{5,4},{6,7},{7,6},{8,9},{9,8},{10,11... | collective-permute-start | bytes 786440 | tf_op jit(solution)/shard_map/ppermute | solution.py:35
  65.0 7.1 %collective-permute-start.10 = (f32[64]{0:T(128)S(1)}, f32[64]{0:T(128)S(1)}, u32[]{:S(2)}, u32[]{:S(2)}) collective-permute-start(f32[64]{0:T(128)S(1)} %maximum_reduce_fusion.5), channel_id=1, source_target_pairs={{0,64},{64,0},{32,96},{96,32},{128,192},{192,128},{160,224},{224,1... | collective-permute-start | bytes 776 | tf_op jit(solution)/shard_map/ppermute | solution.py:35
  72.6 6.1 %collective-permute-start.11 = (f32[64]{0:T(128)S(1)}, f32[64]{0:T(128)S(1)}, u32[]{:S(2)}, u32[]{:S(2)}) collective-permute-start(f32[64]{0:T(128)S(1)} %maximum_reduce_fusion.6), channel_id=1, source_target_pairs={{0,128},{128,0},{32,160},{160,32},{64,192},{192,64},{96,224},{224,... | collective-permute-start | bytes 776 | tf_op jit(solution)/shard_map/ppermute | solution.py:35
  79.2 11.3 %collective-permute-start.12 = (f32[64]{0:T(128)S(1)}, f32[64]{0:T(128)S(1)}, u32[]{:S(2)}, u32[]{:S(2)}) collective-permute-start(f32[64]{0:T(128)S(1)} %maximum_reduce_fusion.7), channel_id=1, source_target_pairs={{0,256},{256,0},{32,288},{288,32},{64,320},{320,64},{96,352},{352,... | collective-permute-start | bytes 776 | tf_op jit(solution)/shard_map/ppermute | solution.py:35
  90.7 131.8 %copy-start.75 = (pred[576]{0:T(1024)(128)(4,1)}, pred[576]{0:T(1024)(128)(4,1)S(1)}, u32[]{:S(2)}) copy-start(pred[576]{0:T(1024)(128)(4,1)S(1)} %gt.30) | copy-start | bytes 1732
  92.4 15.6 %collective-permute-start.14 = (f32[64,2,512]{2,0,1:T(8,128)S(1)}, f32[64,2,512]{2,0,1:T(8,128)S(1)}, u32[]{:S(2)}, u32[]{:S(2)}) collective-permute-start(f32[64,2,512]{2,0,1:T(8,128)S(1)} %reduce_sum.342), channel_id=1, source_target_pairs={{0,2},{2,0},{1,3},{3,1},{4,6},{6,4},{5,7},{7,5},{8,10},{10,8},{9,1... | collective-permute-start | bytes 786440 | tf_op jit(solution)/shard_map/ppermute | solution.py:35
  109.6 8.1 %collective-permute-start.15 = (f32[64,2,512]{2,0,1:T(8,128)S(1)}, f32[64,2,512]{2,0,1:T(8,128)S(1)}, u32[]{:S(2)}, u32[]{:S(2)}) collective-permute-start(f32[64,2,512]{2,0,1:T(8,128)S(1)} %reduce_sum.343), channel_id=1, source_target_pairs={{0,4},{4,0},{1,5},{5,1},{2,6},{6,2},{3,7},{7,3},{8,12},{12,8},{9,1... | collective-permute-start | bytes 786440 | tf_op jit(solution)/shard_map/ppermute | solution.py:35
  118.8 16.6 %collective-permute-start.16 = (f32[64,2,512]{2,0,1:T(8,128)S(1)}, f32[64,2,512]{2,0,1:T(8,128)S(1)}, u32[]{:S(2)}, u32[]{:S(2)}) collective-permute-start(f32[64,2,512]{2,0,1:T(8,128)S(1)} %reduce_sum.344), channel_id=1, source_target_pairs={{0,8},{8,0},{1,9},{9,1},{2,10},{10,2},{3,11},{11,3},{4,12},{12,4},... | collective-permute-start | bytes 786440 | tf_op jit(solution)/shard_map/ppermute | solution.py:35
  136.4 19.6 %collective-permute-start.17 = (f32[64,2,512]{2,0,1:T(8,128)S(1)}, f32[64,2,512]{2,0,1:T(8,128)S(1)}, u32[]{:S(2)}, u32[]{:S(2)}) collective-permute-start(f32[64,2,512]{2,0,1:T(8,128)S(1)} %reduce_sum.345), channel_id=1, source_target_pairs={{0,16},{16,0},{1,17},{17,1},{2,18},{18,2},{3,19},{19,3},{4,20},{20... | collective-permute-start | bytes 786440 | tf_op jit(solution)/shard_map/ppermute | solution.py:35
  143.8 103.8 %copy-start.12 = (f32[2,128,384]{1,2,0:T(8,128)}, f32[2,128,384]{1,2,0:T(8,128)S(1)}, u32[]{:S(2)}) copy-start(f32[2,128,384]{1,2,0:T(8,128)S(1)} %get-tuple-element.122) | copy-start | bytes 1179652
  157.8 4.3 %collective-permute-start.18 = (f32[64,2,512]{2,0,1:T(8,128)}, f32[64,2,512]{2,0,1:T(8,128)S(1)}, u32[]{:S(2)}, u32[]{:S(2)}) collective-permute-start(f32[64,2,512]{2,0,1:T(8,128)} %reduce_sum.346), channel_id=1, source_target_pairs={{0,32},{32,0},{64,96},{96,64},{128,160},{160,128},{192,224},{224,1... | collective-permute-start | bytes 786440 | tf_op jit(solution)/shard_map/ppermute | solution.py:35
  169.2 10.0 %collective-permute-start.19 = (f32[64,2,512]{2,0,1:T(8,128)}, f32[64,2,512]{2,0,1:T(8,128)S(1)}, u32[]{:S(2)}, u32[]{:S(2)}) collective-permute-start(f32[64,2,512]{2,0,1:T(8,128)} %reduce_sum.347), channel_id=1, source_target_pairs={{0,64},{64,0},{32,96},{96,32},{128,192},{192,128},{160,224},{224,1... | collective-permute-start | bytes 786440 | tf_op jit(solution)/shard_map/ppermute | solution.py:35
  186.3 10.6 %collective-permute-start.20 = (f32[64,2,512]{2,0,1:T(8,128)}, f32[64,2,512]{2,0,1:T(8,128)S(1)}, u32[]{:S(2)}, u32[]{:S(2)}) collective-permute-start(f32[64,2,512]{2,0,1:T(8,128)} %reduce_sum.348), channel_id=1, source_target_pairs={{0,128},{128,0},{32,160},{160,32},{64,192},{192,64},{96,224},{224,... | collective-permute-start | bytes 786440 | tf_op jit(solution)/shard_map/ppermute | solution.py:35
  203.9 18.1 %collective-permute-start.21 = (f32[64,2,512]{2,0,1:T(8,128)}, f32[64,2,512]{2,0,1:T(8,128)S(1)}, u32[]{:S(2)}, u32[]{:S(2)}) collective-permute-start(f32[64,2,512]{2,0,1:T(8,128)} %reduce_sum.349), channel_id=1, source_target_pairs={{0,256},{256,0},{32,288},{288,32},{64,320},{320,64},{96,352},{352,... | collective-permute-start | bytes 786440 | tf_op jit(solution)/shard_map/ppermute | solution.py:35
  223.6 24.9 %copy-start.61 = (f32[256]{0:T(256)}, f32[256]{0:T(256)S(1)}, u32[]{:S(2)}) copy-start(f32[256]{0:T(256)S(1)} %bitcast_add_fusion.8) | copy-start | bytes 3076
  224.6 24.9 %copy-start.9 = (f32[576,256]{1,0:T(8,128)}, f32[576,256]{1,0:T(8,128)S(1)}, u32[]{:S(2)}) copy-start(f32[576,256]{1,0:T(8,128)S(1)} %get-tuple-element.116) | copy-start | bytes 1769476
  224.6 24.9 %copy-start.51 = (f32[256]{0:T(256)}, f32[256]{0:T(256)S(1)}, u32[]{:S(2)}) copy-start(f32[256]{0:T(256)S(1)} %bitcast_maximum_fusion.2) | copy-start | bytes 3076
  224.9 24.6 %copy-start.63 = (f32[256]{0:T(256)}, f32[256]{0:T(256)S(1)}, u32[]{:S(2)}) copy-start(f32[256]{0:T(256)S(1)} %bitcast_add_fusion.10) | copy-start | bytes 3076
  225.2 31.6 %copy-start.8 = (f32[576,256]{1,0:T(8,128)}, f32[576,256]{1,0:T(8,128)S(1)}, u32[]{:S(2)}) copy-start(f32[576,256]{1,0:T(8,128)S(1)} %get-tuple-element.120) | copy-start | bytes 1769476
  225.5 25.0 %copy-start.59 = (f32[256]{0:T(256)}, f32[256]{0:T(256)S(1)}, u32[]{:S(2)}) copy-start(f32[256]{0:T(256)S(1)} %bitcast_add_fusion.12) | copy-start | bytes 3076
  225.8 49.1 %copy-start.7 = (f32[576,256]{1,0:T(8,128)}, f32[576,256]{1,0:T(8,128)S(1)}, u32[]{:S(2)}) copy-start(f32[576,256]{1,0:T(8,128)S(1)} %get-tuple-element.124) | copy-start | bytes 1769476
  226.1 25.4 %copy-start.57 = (f32[256]{0:T(256)}, f32[256]{0:T(256)S(1)}, u32[]{:S(2)}) copy-start(f32[256]{0:T(256)S(1)} %bitcast_add_fusion.14) | copy-start | bytes 3076
  276.7 53.7 %copy-start.2 = (f32[1,576,2,512]{3,1,2,0:T(8,128)}, f32[1,576,2,512]{3,1,2,0:T(8,128)S(1)}, u32[]{:S(2)}) copy-start(f32[1,576,2,512]{3,1,2,0:T(8,128)S(1)} %maximum_divide_fusion) | copy-start | bytes 7077892
  276.7 11.3 %collective-permute-start.24 = (bf16[64,2,512]{2,0,1:T(8,128)(2,1)S(1)}, bf16[64,2,512]{2,0,1:T(8,128)(2,1)S(1)}, u32[]{:S(2)}, u32[]{:S(2)}) collective-permute-start(bf16[64,2,512]{2,0,1:T(8,128)(2,1)S(1)} %fusion.99), channel_id=1, source_target_pairs={{0,256},{256,0},{32,288},{288,32},{64,320},{320,64},{96,352},{352,... | collective-permute-start | bytes 393224 | tf_op jit(solution)/shard_map/ppermute | solution.py:35
  293.0 8.3 %collective-permute-start.25 = (bf16[64,2,512]{2,0,1:T(8,128)(2,1)}, bf16[64,2,512]{2,0,1:T(8,128)(2,1)}, u32[]{:S(2)}, u32[]{:S(2)}) collective-permute-start(bf16[64,2,512]{2,0,1:T(8,128)(2,1)} %fusion.74), channel_id=1, source_target_pairs={{0,128},{128,0},{32,160},{160,32},{64,192},{192,64},{96,224},{224,... | collective-permute-start | bytes 393224 | tf_op jit(solution)/shard_map/ppermute | solution.py:35
  307.3 6.0 %collective-permute-start.26 = (bf16[64,2,512]{2,0,1:T(8,128)(2,1)}, bf16[64,2,512]{2,0,1:T(8,128)(2,1)}, u32[]{:S(2)}, u32[]{:S(2)}) collective-permute-start(bf16[64,2,512]{2,0,1:T(8,128)(2,1)} %fusion.72), channel_id=1, source_target_pairs={{0,64},{64,0},{32,96},{96,32},{128,192},{192,128},{160,224},{224,1... | collective-permute-start | bytes 393224 | tf_op jit(solution)/shard_map/ppermute | solution.py:35
  315.3 11.4 %collective-permute-start.27 = (bf16[64,2,512]{2,0,1:T(8,128)(2,1)}, bf16[64,2,512]{2,0,1:T(8,128)(2,1)}, u32[]{:S(2)}, u32[]{:S(2)}) collective-permute-start(bf16[64,2,512]{2,0,1:T(8,128)(2,1)} %fusion.70), channel_id=1, source_target_pairs={{0,32},{32,0},{64,96},{96,64},{128,160},{160,128},{192,224},{224,1... | collective-permute-start | bytes 393224 | tf_op jit(solution)/shard_map/ppermute | solution.py:35
  332.1 17.0 %collective-permute-start.28 = (f32[64,2,512]{2,0,1:T(8,128)}, f32[64,2,512]{2,0,1:T(8,128)}, u32[]{:S(2)}, u32[]{:S(2)}) collective-permute-start(f32[64,2,512]{2,0,1:T(8,128)} %fusion.68), channel_id=1, source_target_pairs={{0,16},{16,0},{1,17},{17,1},{2,18},{18,2},{3,19},{19,3},{4,20},{20... | collective-permute-start | bytes 786440 | tf_op jit(solution)/shard_map/ppermute | solution.py:35
  338.4 36.3 %copy-start = (f32[4,128,2,512]{3,1,0,2:T(8,128)}, f32[4,128,2,512]{3,1,0,2:T(8,128)S(1)}, u32[]{:S(2)}) copy-start(f32[4,128,2,512]{3,1,0,2:T(8,128)S(1)} %pad_add_fusion) | copy-start | bytes 6291460
  351.4 13.4 %collective-permute-start.29 = (f32[64,2,512]{2,0,1:T(8,128)S(1)}, f32[64,2,512]{2,0,1:T(8,128)}, u32[]{:S(2)}, u32[]{:S(2)}) collective-permute-start(f32[64,2,512]{2,0,1:T(8,128)S(1)} %fusion.67), channel_id=1, source_target_pairs={{0,8},{8,0},{1,9},{9,1},{2,10},{10,2},{3,11},{11,3},{4,12},{12,4},... | collective-permute-start | bytes 786440 | tf_op jit(solution)/shard_map/ppermute | solution.py:35
  367.8 18.2 %collective-permute-start.30 = (f32[64,2,512]{2,0,1:T(8,128)}, f32[64,2,512]{2,0,1:T(8,128)}, u32[]{:S(2)}, u32[]{:S(2)}) collective-permute-start(f32[64,2,512]{2,0,1:T(8,128)} %fusion.66), channel_id=1, source_target_pairs={{0,4},{4,0},{1,5},{5,1},{2,6},{6,2},{3,7},{7,3},{8,12},{12,8},{9,1... | collective-permute-start | bytes 786440 | tf_op jit(solution)/shard_map/ppermute | solution.py:35
  370.9 21.6 %collective-permute-start.22 = (f32[128,2,512]{2,0,1:T(8,128)}, f32[128,2,512]{2,0,1:T(8,128)}, u32[]{:S(2)}, u32[]{:S(2)}) collective-permute-start(f32[128,2,512]{2,0,1:T(8,128)} %get-tuple-element.44), channel_id=1, source_target_pairs={{0,1},{1,2},{2,3},{3,4},{4,5},{5,6},{6,7},{7,8},{8,9},{9,10},{10,1... | collective-permute-start | bytes 1572872 | tf_op jit(solution)/shard_map/ppermute | solution.py:20
  376.4 38.6 %collective-permute-start.23 = (f32[128,2,512]{2,0,1:T(8,128)}, f32[128,2,512]{2,0,1:T(8,128)}, u32[]{:S(2)}, u32[]{:S(2)}) collective-permute-start(f32[128,2,512]{2,0,1:T(8,128)} %get-tuple-element.43), channel_id=1, source_target_pairs={{1,0},{2,1},{3,2},{4,3},{5,4},{6,5},{7,6},{8,7},{9,8},{10,9},{11,1... | collective-permute-start | bytes 1572872 | tf_op jit(solution)/shard_map/ppermute | solution.py:23
  390.7 21.1 %collective-permute-start.31 = (f32[64,2,512]{2,0,1:T(8,128)}, f32[64,2,512]{2,0,1:T(8,128)S(1)}, u32[]{:S(2)}, u32[]{:S(2)}) collective-permute-start(f32[64,2,512]{2,0,1:T(8,128)} %fusion.65), channel_id=1, source_target_pairs={{0,2},{2,0},{1,3},{3,1},{4,6},{6,4},{5,7},{7,5},{8,10},{10,8},{9,1... | collective-permute-start | bytes 786440 | tf_op jit(solution)/shard_map/ppermute | solution.py:35
  413.1 8.2 %collective-permute-start.32 = (f32[64,2,512]{2,0,1:T(8,128)S(1)}, f32[64,2,512]{2,0,1:T(8,128)S(1)}, u32[]{:S(2)}, u32[]{:S(2)}) collective-permute-start(f32[64,2,512]{2,0,1:T(8,128)S(1)} %fusion.64), channel_id=1, source_target_pairs={{0,1},{1,0},{2,3},{3,2},{4,5},{5,4},{6,7},{7,6},{8,9},{9,8},{10,11... | collective-permute-start | bytes 786440 | tf_op jit(solution)/shard_map/ppermute | solution.py:35
  (64 other events, 363.5 us)
where the time goes:
time: 427 us; the launch traced here: 423 us
  starting transfers between devices  127 us (30%)
  waiting for transfers between devices  127 us (30%)
  other arithmetic  62 us (15%)
  local copies, waits for them, and re-layouts  53.4 us (13%)
  matrix products  51 us (12%)
    ppermute x27, waiting for transfers between devices, swapped(): return lax.ppermute(block, axis, route)  127 us
    ppermute x27, starting transfers between devices, swapped(): return lax.ppermute(block, axis, route)  93.6 us
    ppermute x3, starting transfers between devices, extended(): lax.ppermute(lax.slice_in_dim(block, 0, width, axis=dim), axis, backward)  24.2 us
    unnamed x166, local copies, waits for them, and re-layouts  13.7 us
    reduce_sum x8, other arithmetic, merge_rows(): tiles.reshape(shape[:-3] + (shape[-3] // 2, 2) + shape[-2:]).sum(axis=-3)  10.9 us
    ppermute x3, starting transfers between devices, extended(): lax.ppermute(lax.slice_in_dim(block, block.shape[dim] - width, None, axis...  8.67 us
  transfers between devices with their start and end apart: 33, of which 21 were waited for; matrix products, arithmetic and copies ran while one was open for 14% of the time, Pallas kernels for 0%

commit v1 on v0

v1 whole, which is shorter than its diff:
```python
import jax
import jax.numpy as jnp
from jax import lax
from jax.experimental import pallas as pl
from jax.experimental.pallas import tpu as pltpu
from jax.sharding import PartitionSpec as P

HEADS = 4
HEAD_DIM = 128
BLOCK = 128
COARSE = 64
LEVELS = 9
LANES = 128
MASKED = -1e30
VMEM_BYTES = 56 * 1024 * 1024

f32 = jnp.float32
bf16 = jnp.bfloat16


def rows_of(shape):
    return lax.broadcasted_iota(jnp.int32, shape, 0)


def call(kernel, outs, scratch, index, *operands, flops=0, name=None):
    size = sum(o.size * o.dtype.itemsize for o in operands)
    size += sum(o.size * o.dtype.itemsize for o in outs)
    in_specs = [pl.BlockSpec(memory_space=pltpu.SMEM)]
    in_specs += [pl.BlockSpec(memory_space=pltpu.VMEM) for _ in operands]
    return pl.pallas_call(
        kernel,
        out_shape=outs,
        in_specs=in_specs,
        out_specs=[pl.BlockSpec(memory_space=pltpu.VMEM) for _ in outs],
        scratch_shapes=scratch,
        compiler_params=pltpu.CompilerParams(vmem_limit_bytes=VMEM_BYTES),
        cost_estimate=pl.CostEstimate(flops=flops, bytes_accessed=size, transcendentals=0),
        name=name,
    )(index, *operands)


def shape(rows, width, dtype=bf16):
    return jax.ShapeDtypeStruct((rows, width), dtype)


def by_lanes(column, width):
    return jnp.concatenate([column] * (width // LANES), axis=1)


def decode_count(code):
    lane = lax.broadcasted_iota(jnp.int32, code.shape, 1)
    part = jnp.where(lane < LANES // 2, 8.0 * code, code)
    return part + pltpu.roll(part, LANES // 2, 1)


def encode_count(count):
    lane = lax.broadcasted_iota(jnp.int32, count.shape, 1)
    high = jnp.floor(count * 0.125)
    return jnp.where(lane < LANES // 2, high, count - 8.0 * high)


def local_kernel(width, peers):
    def kernel(index, mask, key, value, sib, oth, gather):
        parity = index[0]
        tokens = key.shape[0]
        length = jnp.sum(mask[...], axis=1, keepdims=True)
        live = (rows_of((tokens, LANES)) < length).astype(bf16)
        for ref, block in ((sib, 1 - parity), (oth, parity)):
            start = pl.multiple_of(block * BLOCK, BLOCK)
            ref[pl.ds(0, BLOCK), pl.ds(0, width)] = key[pl.ds(start, BLOCK)]
            ref[pl.ds(0, BLOCK), pl.ds(width, width)] = value[pl.ds(start, BLOCK)]
            place = rows_of((BLOCK, LANES)) + start
            ref[pl.ds(0, BLOCK), pl.ds(2 * width, LANES)] = (place < length).astype(f32).astype(bf16)

        def means(rows):
            group = tokens // rows
            row = rows_of((rows, tokens))
            place = lax.broadcasted_iota(jnp.int32, (rows, tokens), 1)
            member = (row * group <= place) & (place < row * group + group) & (place < length)
            member = member.astype(f32).astype(bf16)
            first = rows_of((rows, LANES)) * group
            count = jnp.clip(length - first, 0, group).astype(f32)
            inverse = by_lanes(1.0 / jnp.maximum(count, 1.0), width)
            k_sum = jnp.dot(member, key[...], preferred_element_type=f32)
            v_sum = jnp.dot(member, value[...], preferred_element_type=f32)
            return (k_sum * inverse).astype(bf16), (v_sum * inverse).astype(bf16), count.astype(bf16)

        k_mean, v_mean, count = means(COARSE)
        sib[pl.ds(BLOCK, COARSE), pl.ds(0, width)] = k_mean
        sib[pl.ds(BLOCK, COARSE), pl.ds(width, width)] = v_mean
        sib[pl.ds(BLOCK, COARSE), pl.ds(2 * width, LANES)] = count
        few = gather.shape[1]
        k_mean, v_mean, count = means(few)
        for peer in range(peers):
            gather[peer, :, pl.ds(0, width)] = k_mean
            gather[peer, :, pl.ds(width, width)] = v_mean
            gather[peer, :, pl.ds(2 * width, LANES)] = count

    return kernel


def store_means(out, first, sums, count, scale_width):
    inverse = by_lanes(1.0 / jnp.maximum(count, 1.0), scale_width)
    rows = count.shape[0]
    out[pl.ds(first, rows), pl.ds(0, scale_width)] = (sums * inverse).astype(bf16)
    out[pl.ds(first, rows), pl.ds(scale_width, LANES)] = count.astype(bf16)


def load_sums(ref, first, rows, sums, counts, at, coded=False):
    width = sums.shape[0] * LANES
    count = ref[pl.ds(first, rows), pl.ds(width, LANES)].astype(f32)
    if coded:
        count = decode_count(count)
    counts[pl.ds(at, rows)] = count
    for tile in range(sums.shape[0]):
        mean = ref[pl.ds(first, rows), pl.ds(tile * LANES, LANES)].astype(f32)
        sums[tile, pl.ds(at, rows)] = mean * count


def climb_kernel(first_own, first_other, bit):
    def kernel(index, own, other, out, sums, counts):
        side = index[bit]
        at_own = pl.multiple_of(side * COARSE, COARSE)
        at_other = pl.multiple_of((1 - side) * COARSE, COARSE)
        load_sums(own, first_own, COARSE, sums, counts, at_own)
        load_sums(other, first_other, COARSE, sums, counts, at_other)
        store_means(
            out, 0, pooled(sums, COARSE, 2), pooled(counts, COARSE, 2), sums.shape[0] * LANES
        )

    return kernel


def pooled(ref, rows, step):
    if len(ref.shape) == 3:
        return jnp.concatenate(
            [pooled(ref.at[tile], rows, step) for tile in range(ref.shape[0])], axis=1
        )
    total = ref[pl.ds(0, rows, stride=step)]
    for i in range(1, step):
        total = total + ref[pl.ds(i, rows, stride=step)]
    return total


def group_kernel(groups):
    def kernel(index, recv, six, seven, wide, sums, counts):
        width = sums.shape[0] * LANES
        total = recv.shape[0]
        load_sums(recv, 0, total, sums, counts, 0)
        quarter = total // COARSE
        store_means(six, 0, pooled(sums, COARSE, quarter), pooled(counts, COARSE, quarter), width)
        half = COARSE // 2
        store_means(
            seven, 0, pooled(sums, half, 2 * quarter), pooled(counts, half, 2 * quarter), width
        )
        few = wide.shape[1]
        step = total // few
        count = pooled(counts, few, step)
        inverse = by_lanes(1.0 / jnp.maximum(count, 1.0), width)
        mean = (pooled(sums, few, step) * inverse).astype(bf16)
        code = encode_count(count).astype(bf16)
        for peer in range(groups):
            wide[peer, :, pl.ds(0, width)] = mean
            wide[peer, :, pl.ds(width, LANES)] = code

    return kernel


def attention_kernel(width, shard_rows, group_rows):
    far_rows = LEVELS * COARSE
    scale = HEAD_DIM**-0.5
    main_rows = far_rows + 2 * BLOCK
    key_rows = main_rows + BLOCK
    half = COARSE // 2

    def kernel(
        index, query, cot, sib, oth, sib_in, oth_in, two_in, three_in, shard_in, six_in,
        seven_a, seven_b, group_in,
        attended, query_grad, own_grad, sib_grad, oth_grad, low_grad, three_out,
        shard_part, six_out, seven_a_out, seven_b_out, group_out,
        keys, bias, inverse, sums, counts, score, weight, grads,
    ):
        parity, octet, half_shard, quad_group, half_group = (
            index[0], index[4], index[5], index[6], index[7]
        )
        packed = 2 * width

        def take(at, ref, first, rows):
            keys[pl.ds(at, rows)] = ref[pl.ds(first, rows), pl.ds(0, packed)]
            count = ref[pl.ds(first, rows), pl.ds(packed, LANES)].astype(f32)
            bias[pl.ds(at, rows)] = jnp.where(count > 0, 0.0, MASKED)
            if at < far_rows:
                inverse[pl.ds(at, rows)] = 1.0 / jnp.maximum(count, 1.0)

        def take_pooled(at):
            count = pooled(counts, COARSE, 2)
            inv = 1.0 / jnp.maximum(count, 1.0)
            keys[pl.ds(at, COARSE)] = (pooled(sums, COARSE, 2) * by_lanes(inv, packed)).astype(bf16)
            bias[pl.ds(at, COARSE)] = jnp.where(count > 0, 0.0, MASKED)
            inverse[pl.ds(at, COARSE)] = inv

        octet_at = pl.multiple_of(octet * COARSE, COARSE)
        half_shard_at = pl.multiple_of(half_shard * 2 * COARSE, 2 * COARSE)
        quad_at = pl.multiple_of(quad_group * COARSE, COARSE)
        half_group_at = pl.multiple_of(half_group * 2 * COARSE, 2 * COARSE)
        take(0, sib_in, BLOCK, COARSE)
        take(COARSE, two_in, 0, COARSE)
        take(2 * COARSE, three_in, 0, COARSE)
        take(3 * COARSE, shard_in, octet_at, COARSE)
        load_sums(shard_in, half_shard_at, 2 * COARSE, sums, counts, 0)
        take_pooled(4 * COARSE)
        take(5 * COARSE, six_in, 0, COARSE)
        take(6 * COARSE, seven_a, 0, half)
        take(6 * COARSE + half, seven_b, 0, half)
        at = 7 * COARSE
        keys[pl.ds(at, COARSE)] = group_in[pl.ds(quad_at, COARSE), pl.ds(0, packed)]
        count = decode_count(group_in[pl.ds(quad_at, COARSE), pl.ds(packed, LANES)].astype(f32))
        bias[pl.ds(at, COARSE)] = jnp.where(count > 0, 0.0, MASKED)
        inverse[pl.ds(at, COARSE)] = 1.0 / jnp.maximum(count, 1.0)
        load_sums(group_in, half_group_at, 2 * COARSE, sums, counts, 0, coded=True)
        take_pooled(8 * COARSE)
        take(far_rows, sib, 0, BLOCK)
        take(far_rows + BLOCK, oth, 0, BLOCK)
        take(main_rows, sib_in, 0, BLOCK)
        take(main_rows + BLOCK, oth_in, 0, BLOCK)

        own_rows = (
            pl.ds(pl.multiple_of((1 - parity) * BLOCK, BLOCK), BLOCK),
            pl.ds(pl.multiple_of(parity * BLOCK, BLOCK), BLOCK),
        )
        nt = (((1,), (1,)), ((), ()))
        tn = (((0,), (0,)), ((), ()))
        segments = [(at, 64) for at in range(0, main_rows, 64)]
        halo_segments = [(at, 64) for at in range(0, BLOCK, 64)]

        def one_head(head):
            key_cols = pl.ds(pl.multiple_of(head * HEAD_DIM, HEAD_DIM), HEAD_DIM)
            value_cols = pl.ds(pl.multiple_of(width + head * HEAD_DIM, HEAD_DIM), HEAD_DIM)
            q = jnp.concatenate([query[r, key_cols] for r in own_rows], axis=0)
            c = jnp.concatenate([cot[r, key_cols] for r in own_rows], axis=0)

            def dots(cols, side):
                return (
                    lax.dot_general(keys[pl.ds(0, main_rows), cols], side, nt, preferred_element_type=f32),
                    lax.dot_general(
                        keys[pl.ds(main_rows, BLOCK), cols], side[:BLOCK], nt, preferred_element_type=f32
                    ),
                    lax.dot_general(
                        keys[pl.ds(main_rows + BLOCK, BLOCK), cols], side[BLOCK:], nt,
                        preferred_element_type=f32,
                    ),
                )

            main, near_sib, near_oth = dots(key_cols, q)
            score[pl.ds(0, main_rows)] = main * scale + by_lanes(bias[pl.ds(0, main_rows)], 2 * BLOCK)
            score[pl.ds(main_rows, BLOCK)] = jnp.concatenate(
                [
                    near_sib * scale + bias[pl.ds(main_rows, BLOCK)],
                    near_oth * scale + bias[pl.ds(main_rows + BLOCK, BLOCK)],
                ],
                axis=1,
            )
            main, near_sib, near_oth = dots(value_cols, c)
            grads[pl.ds(0, main_rows)] = main
            grads[pl.ds(main_rows, BLOCK)] = jnp.concatenate([near_sib, near_oth], axis=1)
            top = jnp.full((8, 2 * BLOCK), -jnp.inf, f32)
            for at in range(0, key_rows, 64):
                part = score[pl.ds(at, 64)]
                top = jnp.maximum(top, jnp.max(part.reshape(8, 8, 2 * BLOCK), axis=0))
            top = jnp.max(top, axis=0, keepdims=True)
            total = jnp.zeros((8, 2 * BLOCK), f32)
            mixed = jnp.zeros((8, 2 * BLOCK), f32)
            for at in range(0, key_rows, 64):
                e = jnp.exp(score[pl.ds(at, 64)] - top)
                score[pl.ds(at, 64)] = e
                total = total + jnp.sum(e.reshape(8, 8, 2 * BLOCK), axis=0)
                mixed = mixed + jnp.sum((e * grads[pl.ds(at, 64)]).reshape(8, 8, 2 * BLOCK), axis=0)
            total = 1.0 / jnp.sum(total, axis=0, keepdims=True)
            delta = jnp.sum(mixed, axis=0, keepdims=True) * total
            for at in range(0, key_rows, 64):
                prob = score[pl.ds(at, 64)] * total
                weight[pl.ds(at, 64), pl.ds(0, 2 * BLOCK)] = prob.astype(bf16)
                ds = prob * (grads[pl.ds(at, 64)] - delta)
                weight[pl.ds(at, 64), pl.ds(2 * BLOCK, 2 * BLOCK)] = ds.astype(bf16)

            def back(offset, cols):
                out = lax.dot_general(
                    weight[pl.ds(0, main_rows), pl.ds(offset, 2 * BLOCK)],
                    keys[pl.ds(0, main_rows), cols], tn, preferred_element_type=f32,
                )
                near = []
                for i in range(2):
                    near.append(
                        lax.dot_general(
                            weight[pl.ds(main_rows, BLOCK), pl.ds(offset + i * BLOCK, BLOCK)],
                            keys[pl.ds(main_rows + i * BLOCK, BLOCK), cols], tn,
                            preferred_element_type=f32,
                        )
                    )
                return out + jnp.concatenate(near, axis=0)

            out = back(0, value_cols)
            grad = back(2 * BLOCK, key_cols) * scale
            for i, r in enumerate(own_rows):
                attended[r, key_cols] = out[i * BLOCK : (i + 1) * BLOCK].astype(bf16)
                query_grad[r, key_cols] = grad[i * BLOCK : (i + 1) * BLOCK].astype(bf16)

            for offset, cols, side, factor in (
                (2 * BLOCK, key_cols, q, scale), (0, value_cols, c, None)
            ):
                res = jnp.dot(
                    weight[pl.ds(0, main_rows), pl.ds(offset, 2 * BLOCK)], side,
                    preferred_element_type=f32,
                )
                if factor is not None:
                    res = res * factor
                far = res[:far_rows] * inverse[...]
                own_grad[:, cols] = res[far_rows:]
                low_grad[:, cols] = far[: 2 * COARSE]
                three_out[:, cols] = far[2 * COARSE : 3 * COARSE].astype(bf16)
                shard_part[pl.ds(0, 2 * COARSE), cols] = far[3 * COARSE : 5 * COARSE]
                six_out[:, cols] = far[5 * COARSE : 6 * COARSE].astype(bf16)
                seven_a_out[:, cols] = far[6 * COARSE : 6 * COARSE + half].astype(bf16)
                seven_b_out[:, cols] = far[6 * COARSE + half : 7 * COARSE].astype(bf16)
                sums[head + (0 if offset else HEADS)] = far[7 * COARSE :]
                for i, out_ref in enumerate((sib_grad, oth_grad)):
                    near = jnp.dot(
                        weight[pl.ds(main_rows, BLOCK), pl.ds(offset + i * BLOCK, BLOCK)],
                        side[i * BLOCK : (i + 1) * BLOCK], preferred_element_type=f32,
                    )
                    if factor is not None:
                        near = near * factor
                    out_ref[:, cols] = near.astype(bf16)

        def step(head, carry):
            one_head(head)
            return carry

        lax.fori_loop(0, HEADS, step, 0)
        group_out[...] = jnp.zeros_like(group_out)
        for tile in range(sums.shape[0]):
            cols = pl.ds(tile * LANES, LANES)
            group_out[pl.ds(quad_at, COARSE), cols] = sums[tile, pl.ds(0, COARSE)].astype(bf16)
            wide = widen(sums[tile, pl.ds(COARSE, COARSE)], 2)
            group_out[pl.ds(half_group_at, 2 * COARSE), cols] = wide.astype(bf16)

    scratch = [
        pltpu.VMEM((key_rows + BLOCK, 2 * width), bf16),
        pltpu.VMEM((key_rows + BLOCK, LANES), f32),
        pltpu.VMEM((far_rows, LANES), f32),
        pltpu.VMEM((2 * width // LANES, 2 * COARSE, LANES), f32),
        pltpu.VMEM((2 * COARSE, LANES), f32),
        pltpu.VMEM((key_rows, 2 * BLOCK), f32),
        pltpu.VMEM((key_rows, 4 * BLOCK), bf16),
        pltpu.VMEM((key_rows, 2 * BLOCK), f32),
    ]
    outs = [
        shape(2 * BLOCK, width), shape(2 * BLOCK, width), shape(2 * BLOCK, 2 * width, f32),
        shape(BLOCK, 2 * width), shape(BLOCK, 2 * width), shape(2 * COARSE, 2 * width, f32),
        shape(COARSE, 2 * width), shape(2 * COARSE, 2 * width, f32), shape(COARSE, 2 * width),
        shape(half, 2 * width), shape(half, 2 * width), shape(group_rows, 2 * width),
    ]
    return kernel, outs, scratch


def widen(rows, times):
    count, width = rows.shape
    return jnp.broadcast_to(rows[:, None], (count, times, width)).reshape(count * times, width)


def shard_back_kernel(index, part, six, seven_a, seven_b, group, out, acc):
    octet, half_shard = index[4], index[5]
    tile = six[...].astype(f32) + widen(seven_a[...].astype(f32) + seven_b[...].astype(f32), 2)
    few = COARSE // 4
    total = group[pl.ds(0, few)].astype(f32)
    for i in range(1, group.shape[0] // few):
        total = total + group[pl.ds(i * few, few)].astype(f32)
    tile = tile + widen(total, 4)
    acc[...] = widen(tile, out.shape[0] // COARSE)
    octet_at = pl.ds(pl.multiple_of(octet * COARSE, COARSE), COARSE)
    half_at = pl.ds(pl.multiple_of(half_shard * 2 * COARSE, 2 * COARSE), 2 * COARSE)
    acc[octet_at] = acc[octet_at] + part[pl.ds(0, COARSE)]
    acc[half_at] = acc[half_at] + widen(part[pl.ds(COARSE, COARSE)], 2)
    out[...] = acc[...].astype(bf16)


def two_back_kernel(index, three, low, out):
    side = index[1]
    half = COARSE // 2
    theirs = three[pl.ds(pl.multiple_of((1 - side) * half, half), half)].astype(f32)
    out[...] = (low[pl.ds(COARSE, COARSE)] + widen(theirs, 2)).astype(bf16)


def one_back_kernel(index, three, two, low, sib_grad, out, mine, tile):
    side, low_side = index[1], index[0]
    half = COARSE // 2
    upper = three[pl.ds(pl.multiple_of(side * half, half), half)].astype(f32)
    tile[...] = widen(upper, 2) + two[...].astype(f32)
    theirs = tile[pl.ds(pl.multiple_of((1 - low_side) * half, half), half)]
    out[pl.ds(0, BLOCK)] = sib_grad[...]
    out[pl.ds(BLOCK, COARSE)] = (low[pl.ds(0, COARSE)] + widen(theirs, 2)).astype(bf16)
    mine[...] = tile[pl.ds(pl.multiple_of(low_side * half, half), half)]


def final_kernel(width):
    def kernel(index, mask, own, sib_back, oth_back, mine, shard, key_grad, value_grad, spread):
        parity = index[0]
        tokens = key_grad.shape[0]
        length = jnp.sum(mask[...], axis=1, keepdims=True)
        few = shard.shape[1]
        total = shard[0].astype(f32)
        for i in range(1, shard.shape[0]):
            total = total + shard[i].astype(f32)
        tile = widen(total, COARSE // few) + widen(mine[...], 2)
        tile = tile + sib_back[pl.ds(BLOCK, COARSE)].astype(f32)
        spread[...] = widen(tile, tokens // COARSE)
        for i, (block, near) in enumerate(((1 - parity, sib_back), (parity, oth_back))):
            start = pl.multiple_of(block * BLOCK, BLOCK)
            live = (rows_of((BLOCK, LANES)) + start < length).astype(f32)
            grad = own[pl.ds(i * BLOCK, BLOCK)] + near[pl.ds(0, BLOCK)].astype(f32)
            grad = grad + spread[pl.ds(start, BLOCK)] * by_lanes(live, 2 * width)
            key_grad[pl.ds(start, BLOCK)] = grad[:, :width].astype(bf16)
            value_grad[pl.ds(start, BLOCK)] = grad[:, width:].astype(bf16)

    return kernel


def flip(count, bits):
    return [(i, i ^ bits) for i in range(count)]


def body(query_states, key_states, value_states, valid_mask, attended_grad):
    tokens, width = query_states.shape
    shards = lax.axis_size("shard")
    groups = lax.axis_size("grp")
    total = shards * groups
    packed = 2 * width
    row = packed + LANES
    half = COARSE // 2
    s = lax.axis_index("shard")
    g = lax.axis_index("grp")
    index = jnp.stack(
        [s & 1, s >> 1 & 1, s >> 2 & 1, s, s >> 3 ^ 1, s >> 4 ^ 1, g >> 2 ^ 1, g >> 3 ^ 1]
    ).astype(jnp.int32)
    mask = valid_mask.reshape(1, tokens)
    pairs = [(2 * i - 1, 2 * i) for i in range(1, total // 2)]
    pairs = pairs + [(high, low) for low, high in pairs]

    def on_shard(x, bits):
        return lax.ppermute(x, "shard", flip(shards, bits))

    def on_group(x, bits):
        return lax.ppermute(x, "grp", flip(groups, bits))

    few_shard = 2 * COARSE // 16
    few_group = COARSE // 4
    sib, oth, gather = call(
        local_kernel(width, shards),
        [
            shape(BLOCK + COARSE, row), shape(BLOCK, row),
            jax.ShapeDtypeStruct((shards, few_shard, row), bf16),
        ],
        [], index, mask, key_states, value_states, name="local",
    )
    sib_in = on_shard(sib, 1)
    oth_in = lax.ppermute(oth, ("grp", "shard"), pairs)
    shard_in = lax.all_to_all(gather, "shard", 0, 0, tiled=True).reshape(shards * few_shard, row)
    tile_scratch = [
        pltpu.VMEM((packed // LANES, 2 * COARSE, LANES), f32),
        pltpu.VMEM((2 * COARSE, LANES), f32),
    ]
    (two,) = call(
        climb_kernel(BLOCK, BLOCK, 0), [shape(COARSE, row)], tile_scratch, index, sib, sib_in, name="climb_two"
    )
    two_in = on_shard(two, 2)
    six, seven, wide = call(
        group_kernel(groups),
        [shape(COARSE, row), shape(half, row), jax.ShapeDtypeStruct((groups, few_group, row), bf16)],
        [
            pltpu.VMEM((packed // LANES, shards * few_shard, LANES), f32),
            pltpu.VMEM((shards * few_shard, LANES), f32),
        ],
        index, shard_in, name="climb_six",
    )
    six_in = on_group(six, 1)
    seven_a = on_group(seven, 2)
    seven_b = on_group(seven, 3)
    group_in = lax.all_to_all(wide, "grp", 0, 0, tiled=True).reshape(groups * few_group, row)
    (three,) = call(
        climb_kernel(0, 0, 1), [shape(COARSE, row)], tile_scratch, index, two, two_in, name="climb_three"
    )
    three_in = on_shard(three, 4)
    kernel, outs, scratch = attention_kernel(width, shards * few_shard, groups * few_group)
    (
        attended, query_grad, own_grad, sib_grad, oth_grad, low_grad, three_out, shard_part,
        six_out, seven_a_out, seven_b_out, group_out,
    ) = call(
        kernel, outs, scratch, index, query_states, attended_grad, sib, oth, sib_in, oth_in,
        two_in, three_in, shard_in, six_in, seven_a, seven_b, group_in,
        flops=1_600_000_000, name="attention",
    )
    six_back = on_group(six_out, 1)
    seven_a_back = on_group(seven_a_out, 2)
    seven_b_back = on_group(seven_b_out, 3)
    three_back = on_shard(three_out, 4)
    oth_back = lax.ppermute(oth_grad, ("grp", "shard"), pairs)
    group_back = lax.all_to_all(group_out, "grp", 0, 0, tiled=True)
    (two_out,) = call(
        two_back_kernel, [shape(COARSE, packed)], [], index, three_back, low_grad, name="back_two"
    )
    two_back = on_shard(two_out, 2)
    (shard_out,) = call(
        shard_back_kernel, [shape(shards * few_shard, packed)],
        [pltpu.VMEM((shards * few_shard, packed), f32)],
        index, shard_part, six_back, seven_a_back, seven_b_back, group_back, name="back_six",
    )
    sib_out, mine = call(
        one_back_kernel, [shape(BLOCK + COARSE, packed), shape(half, packed, f32)],
        [pltpu.VMEM((COARSE, packed), f32)],
        index, three_back, two_back, low_grad, sib_grad, name="back_one",
    )
    sib_back = on_shard(sib_out, 1)
    shard_back = lax.all_to_all(shard_out, "shard", 0, 0, tiled=True)
    key_grad, value_grad = call(
        final_kernel(width), [shape(tokens, width), shape(tokens, width)],
        [pltpu.VMEM((tokens, packed), f32)],
        index, mask, own_grad, sib_back, oth_back, mine,
        shard_back.reshape(shards, few_shard, packed), name="final",
    )
    return attended, query_grad, key_grad, value_grad


def solution(mesh):
    whole = P(("grp", "shard"), None)
    return jax.shard_map(
        body,
        mesh=mesh,
        in_specs=(whole, whole, whole, P(("grp", "shard")), whole),
        out_specs=(whole, whole, whole, whole),
        check_vma=False,
    )
```

time: 427 us -> 211 us (0.49)
  waiting for transfers between devices: 127 us -> 59.6 us
  other arithmetic: 62 us -> 0 us
  matrix products: 51 us -> 0 us
  local copies, waits for them, and re-layouts: 53.4 us -> 6.06 us
  starting transfers between devices: 127 us -> 81.6 us
  blocking collectives: 0 us -> 31.6 us
  Pallas kernels: 0 us -> 29.7 us
    ppermute x33 -> x14, waiting for transfers between devices: 127 us -> 54.8 us  [the longest x6 41.2 us: on_shard(): return lax.ppermute(x, 'shard', flip(shards, bits))]
    ppermute x33 -> x14, starting transfers between devices: 127 us -> 55 us  [the longest x6 24.1 us: on_group(): return lax.ppermute(x, 'grp', flip(groups, bits))]
    dot_general x49 -> x0, matrix products: 51 us -> none  [the longest x4 8.28 us: body(): jnp.einsum('sqk,skd->sqd', far_half, v_far, preferred_element_type=jnp.fl...]
    all_to_all x0 -> x1, blocking collectives: none -> 31.6 us  [body(): lax.all_to_all(gather, 'shard', 0, 0, tiled=True)]
    pallas_call x0 -> x9, Pallas kernels: none -> 29.7 us  [call(): pl.pallas_call(kernel, out_shape=outs, in_specs=in_specs, out_specs=[pl.B...]
    all_to_all x0 -> x3, starting transfers between devices: none -> 26.5 us  [the longest x1 12.7 us: body(): lax.all_to_all(wide, 'grp', 0, 0, tiled=True)]
    add x30 -> x0, other arithmetic: 18.1 us -> none  [the longest x5 7.06 us: body(): cross_grad[level_bit] + their_part]
    select_n x16 -> x0, local copies, waits for them, and re-layouts: 13 us -> none  [the longest x8 7.35 us: ordered(): upper_part = jnp.where(sibling_side_flag == 0, second_part, first_part)]
  transfers between devices with their start and end apart: 33 -> 17, of which waited for: 21 -> 10; matrix products, arithmetic and copies ran while one was open for 14% -> 0% of each run, Pallas kernels for 0% -> 4%
where the time goes in v1:
time: 211 us; the launch traced here: 210 us
  starting transfers between devices  81.6 us (39%)
  waiting for transfers between devices  59.6 us (28%)
  blocking collectives  31.6 us (15%)
  Pallas kernels  29.7 us (14%)
  local copies, waits for them, and re-layouts  6.06 us (3%)
    ppermute x6, waiting for transfers between devices, on_shard(): return lax.ppermute(x, 'shard', flip(shards, bits))  41.2 us
    all_to_all x1, blocking collectives, body(): lax.all_to_all(gather, 'shard', 0, 0, tiled=True)  31.6 us
    pallas_call x9, Pallas kernels, call(): pl.pallas_call(kernel, out_shape=outs, in_specs=in_specs, out_specs=[pl.B...  29.7 us
    ppermute x6, starting transfers between devices, on_group(): return lax.ppermute(x, 'grp', flip(groups, bits))  24.1 us
    ppermute x6, starting transfers between devices, on_shard(): return lax.ppermute(x, 'shard', flip(shards, bits))  17.3 us
    all_to_all x1, starting transfers between devices, body(): lax.all_to_all(wide, 'grp', 0, 0, tiled=True)  12.7 us
    ppermute x1, starting transfers between devices, body(): oth_back = lax.ppermute(oth_grad, ('grp', 'shard'), pairs)  9.96 us
    all_to_all x1, starting transfers between devices, body(): group_back = lax.all_to_all(group_out, 'grp', 0, 0, tiled=True)  9.46 us
  transfers between devices with their start and end apart: 17, of which 10 were waited for; matrix products, arithmetic and copies ran while one was open for 0% of the time, Pallas kernels for 4%

profile of v1, /device:TPU:1, one launch (start us, length us, event | category | flops | bytes accessed | tf_op | source)
XLA Modules:
  0.0 209.6 jit_solution(2913201359332204803)
XLA Ops:
  0.6 0.6 stack.35.index
  1.2 2.4 %local.1 = (bf16[192,1152]{1,0:T(8,128)(2,1)}, bf16[128,1152]{1,0:T(8,128)(2,1)}, bf16[32,8,1152]{2,1,0:T(8,128)(2,1)}) custom-call(s32[8]{0:T(128)} %stack.35.index, s32[1,256]{1,0:T(1,128)} %bitcast.20, bf16[256,512]{1,0:T(8,128)(2,1)} %key.1, bf16[256,512]{1,0:T(8,128)(2,1)} %value.1), custom_call_target="tpu_custom_call" | custom-call | bytes 1852416 | tf_op jit(solution)/shard_map/local/pallas_call | solution.py:30
  3.6 31.6 %all_to_all.30 = bf16[32,8,1152]{2,1,0:T(8,128)(2,1)} all-to-all(bf16[32,8,1152]{2,1,0:T(8,128)(2,1)} %get-tuple-element.28), channel_id=1, replica_groups=mesh['grp'=16,'shard'=32] {'shard'}, dimensions={0} | all-to-all | bytes 1179648 | tf_op jit(solution)/shard_map/all_to_all | solution.py:467
  35.3 2.6 %climb_six.1 = (bf16[64,1152]{1,0:T(8,128)(2,1)}, bf16[32,1152]{1,0:T(8,128)(2,1)}, bf16[16,16,1152]{2,1,0:T(8,128)(2,1)}) custom-call(s32[8]{0:T(128)} %stack.35.index, bf16[256,1152]{1,0:T(8,128)(2,1)} %bitcast.14), custom_call_target="tpu_custom_call" | custom-call | bytes 1400832 | tf_op jit(solution)/shard_map/climb_six/pallas_call | solution.py:30
  37.9 12.7 %all-to-all-start.1 = ((bf16[16,16,1152]{2,1,0:T(8,128)(2,1)}), bf16[16,16,1152]{2,1,0:T(8,128)(2,1)S(1)}, u32[]{:S(2)}, u32[]{:S(2)}) async-start(bf16[16,16,1152]{2,1,0:T(8,128)(2,1)} %get-tuple-element.31), calls=%async_computation.1 | async-start | bytes 1179648 | tf_op jit(solution)/shard_map/all_to_all | solution.py:488
  50.6 2.2 %collective-permute-start = (bf16[192,1152]{1,0:T(8,128)(2,1)S(1)}, bf16[192,1152]{1,0:T(8,128)(2,1)S(1)}, u32[]{:S(2)}, u32[]{:S(2)}) collective-permute-start(bf16[192,1152]{1,0:T(8,128)(2,1)S(1)} %copy-done.4), channel_id=1, source_target_pairs={{0,1},{1,0},{2,3},{3,2},{4,5},{5,4},{6,7},{7,6},{8,9},{9,8},{10,11... | collective-permute-start | bytes 1327112 | tf_op jit(solution)/shard_map/ppermute | solution.py:450
  52.8 21.3 %collective-permute-done.other.sib_in = bf16[192,1152]{1,0:T(8,128)(2,1)S(1)} collective-permute-done((bf16[192,1152]{1,0:T(8,128)(2,1)S(1)}, bf16[192,1152]{1,0:T(8,128)(2,1)S(1)}, u32[]{:S(2)}, u32[]{:S(2)}) %collective-permute-start) | collective-permute-done | bytes 442400 | tf_op jit(solution)/shard_map/ppermute | solution.py:450
  74.1 0.8 copy-done.5
  74.8 1.9 climb_two.1.own
  76.7 4.0 %collective-permute-start.2 = (bf16[64,1152]{1,0:T(8,128)(2,1)}, bf16[64,1152]{1,0:T(8,128)(2,1)S(1)}, u32[]{:S(2)}, u32[]{:S(2)}) collective-permute-start(bf16[64,1152]{1,0:T(8,128)(2,1)} %climb_two.1.own), channel_id=1, source_target_pairs={{0,2},{1,3},{2,0},{3,1},{4,6},{5,7},{6,4},{7,5},{8,10},{9,11},{10,... | collective-permute-start | bytes 442376 | tf_op jit(solution)/shard_map/ppermute | solution.py:450
  80.8 3.7 %collective-permute-start.1 = (bf16[128,1152]{1,0:T(8,128)(2,1)S(1)}, bf16[128,1152]{1,0:T(8,128)(2,1)S(1)}, u32[]{:S(2)}, u32[]{:S(2)}) collective-permute-start(bf16[128,1152]{1,0:T(8,128)(2,1)S(1)} %copy-done.13), channel_id=1, source_target_pairs={{1,2},{3,4},{5,6},{7,8},{9,10},{11,12},{13,14},{15,16},{17,18},{19... | collective-permute-start | bytes 884744 | tf_op jit(solution)/shard_map/ppermute | solution.py:466
  84.5 3.2 %collective-permute-done.2.other.two_in = bf16[64,1152]{1,0:T(8,128)(2,1)S(1)} collective-permute-done((bf16[64,1152]{1,0:T(8,128)(2,1)}, bf16[64,1152]{1,0:T(8,128)(2,1)S(1)}, u32[]{:S(2)}, u32[]{:S(2)}) %collective-permute-start.2) | collective-permute-done | bytes 147488 | tf_op jit(solution)/shard_map/ppermute | solution.py:450
  87.7 0.7 copy-done.8
  88.4 1.7 climb_three.1
  90.1 2.2 %collective-permute-start.3 = (bf16[64,1152]{1,0:T(8,128)(2,1)}, bf16[64,1152]{1,0:T(8,128)(2,1)S(1)}, u32[]{:S(2)}, u32[]{:S(2)}) collective-permute-start(bf16[64,1152]{1,0:T(8,128)(2,1)} %climb_three.1), channel_id=1, source_target_pairs={{0,4},{1,5},{2,6},{3,7},{4,0},{5,1},{6,2},{7,3},{8,12},{9,13},{10,... | collective-permute-start | bytes 442376 | tf_op jit(solution)/shard_map/ppermute | solution.py:450
  92.3 11.0 %collective-permute-start.4 = (bf16[64,1152]{1,0:T(8,128)(2,1)S(1)}, bf16[64,1152]{1,0:T(8,128)(2,1)S(1)}, u32[]{:S(2)}, u32[]{:S(2)}) collective-permute-start(bf16[64,1152]{1,0:T(8,128)(2,1)S(1)} %copy-done.16), channel_id=1, source_target_pairs={{0,32},{32,0},{64,96},{96,64},{128,160},{160,128},{192,224},{224,1... | collective-permute-start | bytes 442376 | tf_op jit(solution)/shard_map/ppermute | solution.py:453
  103.3 3.2 %collective-permute-start.6 = (bf16[32,1152]{1,0:T(8,128)(2,1)S(1)}, bf16[32,1152]{1,0:T(8,128)(2,1)S(1)}, u32[]{:S(2)}, u32[]{:S(2)}) collective-permute-start(bf16[32,1152]{1,0:T(8,128)(2,1)S(1)} %copy-done.21), channel_id=1, source_target_pairs={{0,96},{32,64},{64,32},{96,0},{128,224},{160,192},{192,160},{224,1... | collective-permute-start | bytes 221192 | tf_op jit(solution)/shard_map/ppermute | solution.py:453
  106.5 2.0 collective-permute-start.5
  108.6 0.5 collective-permute-done.6.seven_b
  109.1 2.5 %collective-permute-done.5.seven_a = bf16[32,1152]{1,0:T(8,128)(2,1)S(1)} collective-permute-done((bf16[32,1152]{1,0:T(8,128)(2,1)S(1)}, bf16[32,1152]{1,0:T(8,128)(2,1)S(1)}, u32[]{:S(2)}, u32[]{:S(2)}) %collective-permute-start.5) | collective-permute-done | bytes 73760 | tf_op jit(solution)/shard_map/ppermute | solution.py:453
  111.6 0.6 copy-done.23
  112.3 0.2 copy-done.2
  112.5 10.7 %attention.1 = (bf16[256,512]{1,0:T(8,128)(2,1)}, bf16[256,512]{1,0:T(8,128)(2,1)}, f32[256,1024]{1,0:T(8,128)}, bf16[128,1024]{1,0:T(8,128)(2,1)}, bf16[128,102...) custom-call(s32[8]{0:T(128)} %stack.35.index, ...), custom_call_target="tpu_custom_call" | custom-call | flops 1600000000 | bytes 7831552 | tf_op jit(solution)/shard_map/attention/pallas_call | solution.py:30
  123.3 9.5 %all-to-all-start.2 = ((bf16[16,16,1024]{2,1,0:T(8,128)(2,1)}), bf16[16,16,1024]{2,1,0:T(8,128)(2,1)S(1)}, u32[]{:S(2)}, u32[]{:S(2)}) async-start(bf16[16,16,1024]{2,1,0:T(8,128)(2,1)} %bitcast.19), calls=%async_computation.2 | async-start | bytes 1048576 | tf_op jit(solution)/shard_map/all_to_all | solution.py:507
  132.7 2.0 collective-permute-start.11
  134.8 3.5 %collective-permute-start.12 = (bf16[32,1024]{1,0:T(8,128)(2,1)S(1)}, bf16[32,1024]{1,0:T(8,128)(2,1)S(1)}, u32[]{:S(2)}, u32[]{:S(2)}) collective-permute-start(bf16[32,1024]{1,0:T(8,128)(2,1)S(1)} %copy-done.25), channel_id=1, source_target_pairs={{0,64},{32,96},{64,0},{96,32},{128,192},{160,224},{192,128},{224,1... | collective-permute-start | bytes 196616 | tf_op jit(solution)/shard_map/ppermute | solution.py:453
  138.3 2.3 %collective-permute-start.13 = (bf16[32,1024]{1,0:T(8,128)(2,1)S(1)}, bf16[32,1024]{1,0:T(8,128)(2,1)S(1)}, u32[]{:S(2)}, u32[]{:S(2)}) collective-permute-start(bf16[32,1024]{1,0:T(8,128)(2,1)S(1)} %copy-done.24), channel_id=1, source_target_pairs={{0,96},{32,64},{64,32},{96,0},{128,224},{160,192},{192,160},{224,1... | collective-permute-start | bytes 196616 | tf_op jit(solution)/shard_map/ppermute | solution.py:453
  140.6 0.3 collective-permute-done.12.seven_a
  140.9 3.8 %collective-permute-done.13.seven_b = bf16[32,1024]{1,0:T(8,128)(2,1)S(1)} collective-permute-done((bf16[32,1024]{1,0:T(8,128)(2,1)S(1)}, bf16[32,1024]{1,0:T(8,128)(2,1)S(1)}, u32[]{:S(2)}, u32[]{:S(2)}) %collective-permute-start.13) | collective-permute-done | bytes 65568 | tf_op jit(solution)/shard_map/ppermute | solution.py:453
  144.7 4.8 %all-to-all-done.2 = bf16[16,16,1024]{2,1,0:T(8,128)(2,1)S(1)} async-done(((bf16[16,16,1024]{2,1,0:T(8,128)(2,1)}), bf16[16,16,1024]{2,1,0:T(8,128)(2,1)S(1)}, u32[]{:S(2)}, u32[]{:S(2)}) %all-to-all-start.2) | async-done | bytes 524320 | tf_op jit(solution)/shard_map/all_to_all | solution.py:507
  149.5 0.8 copy-done.1
  150.3 3.0 %back_six.1 = bf16[256,1024]{1,0:T(8,128)(2,1)} custom-call(s32[8]{0:T(128)} %stack.35.index, f32[128,1024]{1,0:T(8,128)} %get-tuple-element.41.part, bf16[64,1024]{1,0:T(8,128)(2,1)} %copy-done.9, bf16[32,1024]{1,0:T(8,128)(2,1)} %copy-done.11, bf16[32,1024]{1,0:T(8,128)(2,1)} %copy-done.12, bf16[256,1024]{1,0:T(8,128)(2,1)} %bitcast.17), custom_call_target="tpu_custom_call" | custom-call | bytes 1835008 | tf_op jit(solution)/shard_map/back_six/pallas_call | solution.py:30
  153.3 4.4 %all-to-all-start.3 = ((bf16[32,8,1024]{2,1,0:T(8,128)(2,1)}), bf16[32,8,1024]{2,1,0:T(8,128)(2,1)S(1)}, u32[]{:S(2)}, u32[]{:S(2)}) async-start(bf16[32,8,1024]{2,1,0:T(8,128)(2,1)} %bitcast.16), calls=%async_computation.3 | async-start | bytes 1048576 | tf_op jit(solution)/shard_map/all_to_all | solution.py:523
  157.7 3.1 %collective-permute-start.7 = (bf16[64,1024]{1,0:T(8,128)(2,1)S(1)}, bf16[64,1024]{1,0:T(8,128)(2,1)S(1)}, u32[]{:S(2)}, u32[]{:S(2)}) collective-permute-start(bf16[64,1024]{1,0:T(8,128)(2,1)S(1)} %copy-done.19), channel_id=1, source_target_pairs={{0,4},{1,5},{2,6},{3,7},{4,0},{5,1},{6,2},{7,3},{8,12},{9,13},{10,... | collective-permute-start | bytes 393224 | tf_op jit(solution)/shard_map/ppermute | solution.py:450
  160.8 11.8 %collective-permute-done.7.three = bf16[64,1024]{1,0:T(8,128)(2,1)S(1)} collective-permute-done((bf16[64,1024]{1,0:T(8,128)(2,1)S(1)}, bf16[64,1024]{1,0:T(8,128)(2,1)S(1)}, u32[]{:S(2)}, u32[]{:S(2)}) %collective-permute-start.7) | collective-permute-done | bytes 131104 | tf_op jit(solution)/shard_map/ppermute | solution.py:450
  172.6 0.7 copy-done.3
  173.3 1.9 back_two.1
  175.2 3.9 %collective-permute-start.8 = (bf16[64,1024]{1,0:T(8,128)(2,1)}, bf16[64,1024]{1,0:T(8,128)(2,1)S(1)}, u32[]{:S(2)}, u32[]{:S(2)}) collective-permute-start(bf16[64,1024]{1,0:T(8,128)(2,1)} %back_two.1), channel_id=1, source_target_pairs={{0,2},{1,3},{2,0},{3,1},{4,6},{5,7},{6,4},{7,5},{8,10},{9,11},{10,... | collective-permute-start | bytes 393224 | tf_op jit(solution)/shard_map/ppermute | solution.py:450
  179.1 4.8 %collective-permute-done.8.two = bf16[64,1024]{1,0:T(8,128)(2,1)S(1)} collective-permute-done((bf16[64,1024]{1,0:T(8,128)(2,1)}, bf16[64,1024]{1,0:T(8,128)(2,1)S(1)}, u32[]{:S(2)}, u32[]{:S(2)}) %collective-permute-start.8) | collective-permute-done | bytes 131104 | tf_op jit(solution)/shard_map/ppermute | solution.py:450
  183.9 0.6 copy-done.10
  184.6 2.4 %back_one.1 = (bf16[192,1024]{1,0:T(8,128)(2,1)}, f32[32,1024]{1,0:T(8,128)}) custom-call(s32[8]{0:T(128)} %stack.35.index, bf16[64,1024]{1,0:T(8,128)(2,1)} %copy-done.3, bf16[64,1024]{1,0:T(8,128)(2,1)} %copy-done.10, f32[128,1024]{1,0:T(8,128)} %get-tuple-element.36.low, bf16[128,1024]{1,0:T(8,128)(2,1)} %get-tuple-element.37.sib_grad), custom_call_target="tpu_custom_call" | custom-call | bytes 1572864 | tf_op jit(solution)/shard_map/back_one/pallas_call | solution.py:30
  187.0 1.9 collective-permute-start.9
  188.9 10.0 %collective-permute-start.10 = (bf16[128,1024]{1,0:T(8,128)(2,1)S(1)}, bf16[128,1024]{1,0:T(8,128)(2,1)S(1)}, u32[]{:S(2)}, u32[]{:S(2)}) collective-permute-start(bf16[128,1024]{1,0:T(8,128)(2,1)S(1)} %copy-done.15), channel_id=1, source_target_pairs={{1,2},{3,4},{5,6},{7,8},{9,10},{11,12},{13,14},{15,16},{17,18},{19... | collective-permute-start | bytes 786440 | tf_op jit(solution)/shard_map/ppermute | solution.py:506
  198.9 6.6 %collective-permute-done.10.oth_back = bf16[128,1024]{1,0:T(8,128)(2,1)S(1)} collective-permute-done((bf16[128,1024]{1,0:T(8,128)(2,1)S(1)}, bf16[128,1024]{1,0:T(8,128)(2,1)S(1)}, u32[]{:S(2)}, u32[]{:S(2)}) %collective-permute-start.10) | collective-permute-done | bytes 262176 | tf_op jit(solution)/shard_map/ppermute | solution.py:506
  205.5 0.7 copy-done.7
  206.1 0.1 copy-done.6
  206.3 0.2 copy-done
  206.5 3.1 %final.1 = (bf16[256,512]{1,0:T(8,128)(2,1)}, bf16[256,512]{1,0:T(8,128)(2,1)}) custom-call(s32[8]{0:T(128)} %stack.35.index, s32[1,256]{1,0:T(1,128)} %bitcast.21, f32[256,1024]{1,0:T(8,128)} %get-tuple-element.34.own, bf16[192,1024]{1,0:T(8,128)(2,1)} %copy-done.6, bf16[128,1024]{1,0:T(8,128)(2,1)} %copy-done.7, f32[32,1024]{1,0:T(8,128)} %get-tuple-element.40.mine, ...), custom_call_target="tpu_custom_call" | custom-call | bytes 2884608 | tf_op jit(solution)/shard_map/final/pallas_call | solution.py:30
  (49 shorter events, 0.2 us)
Async XLA Ops:
  37.9 12.7 %copy-start.4 = (bf16[192,1152]{1,0:T(8,128)(2,1)S(1)}, bf16[192,1152]{1,0:T(8,128)(2,1)}, u32[]{:S(2)}) copy-start(bf16[192,1152]{1,0:T(8,128)(2,1)} %get-tuple-element.26.own.sib) | copy-start | bytes 1327108
  37.9 73.7 %all-to-all-start.1 = ((bf16[16,16,1152]{2,1,0:T(8,128)(2,1)}), bf16[16,16,1152]{2,1,0:T(8,128)(2,1)S(1)}, u32[]{:S(2)}, u32[]{:S(2)}) async-start(bf16[16,16,1152]{2,1,0:T(8,128)(2,1)} %get-tuple-element.31), calls=%async_computation.1 | async-start | bytes 1179648 | tf_op jit(solution)/shard_map/all_to_all | solution.py:488
  50.5 30.2 %copy-start.13 = (bf16[128,1152]{1,0:T(8,128)(2,1)S(1)}, bf16[128,1152]{1,0:T(8,128)(2,1)}, u32[]{:S(2)}) copy-start(bf16[128,1152]{1,0:T(8,128)(2,1)} %get-tuple-element.27.oth) | copy-start | bytes 884740
  50.6 23.5 %collective-permute-start = (bf16[192,1152]{1,0:T(8,128)(2,1)S(1)}, bf16[192,1152]{1,0:T(8,128)(2,1)S(1)}, u32[]{:S(2)}, u32[]{:S(2)}) collective-permute-start(bf16[192,1152]{1,0:T(8,128)(2,1)S(1)} %copy-done.4), channel_id=1, source_target_pairs={{0,1},{1,0},{2,3},{3,2},{4,5},{5,4},{6,7},{7,6},{8,9},{9,8},{10,11... | collective-permute-start | bytes 1327112 | tf_op jit(solution)/shard_map/ppermute | solution.py:450
  74.1 0.8 copy-start.5
  76.7 11.0 %collective-permute-start.2 = (bf16[64,1152]{1,0:T(8,128)(2,1)}, bf16[64,1152]{1,0:T(8,128)(2,1)S(1)}, u32[]{:S(2)}, u32[]{:S(2)}) collective-permute-start(bf16[64,1152]{1,0:T(8,128)(2,1)} %climb_two.1.own), channel_id=1, source_target_pairs={{0,2},{1,3},{2,0},{3,1},{4,6},{5,7},{6,4},{7,5},{8,10},{9,11},{10,... | collective-permute-start | bytes 442376 | tf_op jit(solution)/shard_map/ppermute | solution.py:450
  80.8 11.5 %copy-start.16 = (bf16[64,1152]{1,0:T(8,128)(2,1)S(1)}, bf16[64,1152]{1,0:T(8,128)(2,1)}, u32[]{:S(2)}) copy-start(bf16[64,1152]{1,0:T(8,128)(2,1)} %get-tuple-element.29) | copy-start | bytes 442372
  80.8 22.6 %copy-start.21 = (bf16[32,1152]{1,0:T(8,128)(2,1)S(1)}, bf16[32,1152]{1,0:T(8,128)(2,1)}, u32[]{:S(2)}) copy-start(bf16[32,1152]{1,0:T(8,128)(2,1)} %get-tuple-element.30) | copy-start | bytes 221188
  80.8 27.7 %collective-permute-start.1 = (bf16[128,1152]{1,0:T(8,128)(2,1)S(1)}, bf16[128,1152]{1,0:T(8,128)(2,1)S(1)}, u32[]{:S(2)}, u32[]{:S(2)}) collective-permute-start(bf16[128,1152]{1,0:T(8,128)(2,1)S(1)} %copy-done.13), channel_id=1, source_target_pairs={{1,2},{3,4},{5,6},{7,8},{9,10},{11,12},{13,14},{15,16},{17,18},{19... | collective-permute-start | bytes 884744 | tf_op jit(solution)/shard_map/ppermute | solution.py:466
  87.7 0.7 copy-start.8
  90.1 18.5 %collective-permute-start.3 = (bf16[64,1152]{1,0:T(8,128)(2,1)}, bf16[64,1152]{1,0:T(8,128)(2,1)S(1)}, u32[]{:S(2)}, u32[]{:S(2)}) collective-permute-start(bf16[64,1152]{1,0:T(8,128)(2,1)} %climb_three.1), channel_id=1, source_target_pairs={{0,4},{1,5},{2,6},{3,7},{4,0},{5,1},{6,2},{7,3},{8,12},{9,13},{10,... | collective-permute-start | bytes 442376 | tf_op jit(solution)/shard_map/ppermute | solution.py:450
  92.3 19.3 %collective-permute-start.4 = (bf16[64,1152]{1,0:T(8,128)(2,1)S(1)}, bf16[64,1152]{1,0:T(8,128)(2,1)S(1)}, u32[]{:S(2)}, u32[]{:S(2)}) collective-permute-start(bf16[64,1152]{1,0:T(8,128)(2,1)S(1)} %copy-done.16), channel_id=1, source_target_pairs={{0,32},{32,0},{64,96},{96,64},{128,160},{160,128},{192,224},{224,1... | collective-permute-start | bytes 442376 | tf_op jit(solution)/shard_map/ppermute | solution.py:453
  103.3 5.8 %collective-permute-start.6 = (bf16[32,1152]{1,0:T(8,128)(2,1)S(1)}, bf16[32,1152]{1,0:T(8,128)(2,1)S(1)}, u32[]{:S(2)}, u32[]{:S(2)}) collective-permute-start(bf16[32,1152]{1,0:T(8,128)(2,1)S(1)} %copy-done.21), channel_id=1, source_target_pairs={{0,96},{32,64},{64,32},{96,0},{128,224},{160,192},{192,160},{224,1... | collective-permute-start | bytes 221192 | tf_op jit(solution)/shard_map/ppermute | solution.py:453
  106.5 5.1 %collective-permute-start.5 = (bf16[32,1152]{1,0:T(8,128)(2,1)S(1)}, bf16[32,1152]{1,0:T(8,128)(2,1)S(1)}, u32[]{:S(2)}, u32[]{:S(2)}) collective-permute-start(bf16[32,1152]{1,0:T(8,128)(2,1)S(1)} %copy-done.21), channel_id=1, source_target_pairs={{0,64},{32,96},{64,0},{96,32},{128,192},{160,224},{192,128},{224,1... | collective-permute-start | bytes 221192 | tf_op jit(solution)/shard_map/ppermute | solution.py:453
  108.5 3.1 %copy-start.14 = (bf16[128,1152]{1,0:T(8,128)(2,1)}, bf16[128,1152]{1,0:T(8,128)(2,1)S(1)}, u32[]{:S(2)}) copy-start(bf16[128,1152]{1,0:T(8,128)(2,1)S(1)} %collective-permute-done.1.oth_in) | copy-start | bytes 884740
  108.6 3.1 %copy-start.17 = (bf16[64,1152]{1,0:T(8,128)(2,1)}, bf16[64,1152]{1,0:T(8,128)(2,1)S(1)}, u32[]{:S(2)}) copy-start(bf16[64,1152]{1,0:T(8,128)(2,1)S(1)} %collective-permute-done.3.three_in) | copy-start | bytes 442372
  109.1 2.5 %copy-start.22 = (bf16[32,1152]{1,0:T(8,128)(2,1)}, bf16[32,1152]{1,0:T(8,128)(2,1)S(1)}, u32[]{:S(2)}) copy-start(bf16[32,1152]{1,0:T(8,128)(2,1)S(1)} %collective-permute-done.6.seven_b) | copy-start | bytes 221188
  111.6 0.6 copy-start.23
  111.6 0.7 copy-start.18
  111.6 0.9 copy-start.2
  123.2 9.5 %copy-start.20 = (bf16[64,1024]{1,0:T(8,128)(2,1)S(1)}, bf16[64,1024]{1,0:T(8,128)(2,1)}, u32[]{:S(2)}) copy-start(bf16[64,1024]{1,0:T(8,128)(2,1)} %get-tuple-element.42) | copy-start | bytes 393220
  123.2 11.5 %copy-start.25 = (bf16[32,1024]{1,0:T(8,128)(2,1)S(1)}, bf16[32,1024]{1,0:T(8,128)(2,1)}, u32[]{:S(2)}) copy-start(bf16[32,1024]{1,0:T(8,128)(2,1)} %get-tuple-element.43) | copy-start | bytes 196612
  123.2 15.1 %copy-start.24 = (bf16[32,1024]{1,0:T(8,128)(2,1)S(1)}, bf16[32,1024]{1,0:T(8,128)(2,1)}, u32[]{:S(2)}) copy-start(bf16[32,1024]{1,0:T(8,128)(2,1)} %get-tuple-element.44) | copy-start | bytes 196612
  123.3 26.2 %all-to-all-start.2 = ((bf16[16,16,1024]{2,1,0:T(8,128)(2,1)}), bf16[16,16,1024]{2,1,0:T(8,128)(2,1)S(1)}, u32[]{:S(2)}, u32[]{:S(2)}) async-start(bf16[16,16,1024]{2,1,0:T(8,128)(2,1)} %bitcast.19), calls=%async_computation.2 | async-start | bytes 1048576 | tf_op jit(solution)/shard_map/all_to_all | solution.py:507
  132.7 11.9 %collective-permute-start.11 = (bf16[64,1024]{1,0:T(8,128)(2,1)S(1)}, bf16[64,1024]{1,0:T(8,128)(2,1)S(1)}, u32[]{:S(2)}, u32[]{:S(2)}) collective-permute-start(bf16[64,1024]{1,0:T(8,128)(2,1)S(1)} %copy-done.20), channel_id=1, source_target_pairs={{0,32},{32,0},{64,96},{96,64},{128,160},{160,128},{192,224},{224,1... | collective-permute-start | bytes 393224 | tf_op jit(solution)/shard_map/ppermute | solution.py:453
  134.8 6.1 %collective-permute-start.12 = (bf16[32,1024]{1,0:T(8,128)(2,1)S(1)}, bf16[32,1024]{1,0:T(8,128)(2,1)S(1)}, u32[]{:S(2)}, u32[]{:S(2)}) collective-permute-start(bf16[32,1024]{1,0:T(8,128)(2,1)S(1)} %copy-done.25), channel_id=1, source_target_pairs={{0,64},{32,96},{64,0},{96,32},{128,192},{160,224},{192,128},{224,1... | collective-permute-start | bytes 196616 | tf_op jit(solution)/shard_map/ppermute | solution.py:453
  138.3 6.3 %collective-permute-start.13 = (bf16[32,1024]{1,0:T(8,128)(2,1)S(1)}, bf16[32,1024]{1,0:T(8,128)(2,1)S(1)}, u32[]{:S(2)}, u32[]{:S(2)}) collective-permute-start(bf16[32,1024]{1,0:T(8,128)(2,1)S(1)} %copy-done.24), channel_id=1, source_target_pairs={{0,96},{32,64},{64,32},{96,0},{128,224},{160,192},{192,160},{224,1... | collective-permute-start | bytes 196616 | tf_op jit(solution)/shard_map/ppermute | solution.py:453
  140.9 8.6 %copy-start.11 = (bf16[32,1024]{1,0:T(8,128)(2,1)}, bf16[32,1024]{1,0:T(8,128)(2,1)S(1)}, u32[]{:S(2)}) copy-start(bf16[32,1024]{1,0:T(8,128)(2,1)S(1)} %collective-permute-done.12.seven_a) | copy-start | bytes 196612
  144.7 4.8 %copy-start.12 = (bf16[32,1024]{1,0:T(8,128)(2,1)}, bf16[32,1024]{1,0:T(8,128)(2,1)S(1)}, u32[]{:S(2)}) copy-start(bf16[32,1024]{1,0:T(8,128)(2,1)S(1)} %collective-permute-done.13.seven_b) | copy-start | bytes 196612
  144.7 4.8 %copy-start.9 = (bf16[64,1024]{1,0:T(8,128)(2,1)}, bf16[64,1024]{1,0:T(8,128)(2,1)S(1)}, u32[]{:S(2)}) copy-start(bf16[64,1024]{1,0:T(8,128)(2,1)S(1)} %collective-permute-done.11.six) | copy-start | bytes 393220
  149.5 0.8 copy-start.1
  153.2 4.4 %copy-start.19 = (bf16[64,1024]{1,0:T(8,128)(2,1)S(1)}, bf16[64,1024]{1,0:T(8,128)(2,1)}, u32[]{:S(2)}) copy-start(bf16[64,1024]{1,0:T(8,128)(2,1)} %get-tuple-element.35) | copy-start | bytes 393220
  153.3 52.2 %all-to-all-start.3 = ((bf16[32,8,1024]{2,1,0:T(8,128)(2,1)}), bf16[32,8,1024]{2,1,0:T(8,128)(2,1)S(1)}, u32[]{:S(2)}, u32[]{:S(2)}) async-start(bf16[32,8,1024]{2,1,0:T(8,128)(2,1)} %bitcast.16), calls=%async_computation.3 | async-start | bytes 1048576 | tf_op jit(solution)/shard_map/all_to_all | solution.py:523
  157.7 14.9 %collective-permute-start.7 = (bf16[64,1024]{1,0:T(8,128)(2,1)S(1)}, bf16[64,1024]{1,0:T(8,128)(2,1)S(1)}, u32[]{:S(2)}, u32[]{:S(2)}) collective-permute-start(bf16[64,1024]{1,0:T(8,128)(2,1)S(1)} %copy-done.19), channel_id=1, source_target_pairs={{0,4},{1,5},{2,6},{3,7},{4,0},{5,1},{6,2},{7,3},{8,12},{9,13},{10,... | collective-permute-start | bytes 393224 | tf_op jit(solution)/shard_map/ppermute | solution.py:450
  172.6 0.7 copy-start.3
  175.2 8.7 %collective-permute-start.8 = (bf16[64,1024]{1,0:T(8,128)(2,1)}, bf16[64,1024]{1,0:T(8,128)(2,1)S(1)}, u32[]{:S(2)}, u32[]{:S(2)}) collective-permute-start(bf16[64,1024]{1,0:T(8,128)(2,1)} %back_two.1), channel_id=1, source_target_pairs={{0,2},{1,3},{2,0},{3,1},{4,6},{5,7},{6,4},{7,5},{8,10},{9,11},{10,... | collective-permute-start | bytes 393224 | tf_op jit(solution)/shard_map/ppermute | solution.py:450
  183.9 0.7 copy-start.10
  184.6 4.3 %copy-start.15 = (bf16[128,1024]{1,0:T(8,128)(2,1)S(1)}, bf16[128,1024]{1,0:T(8,128)(2,1)}, u32[]{:S(2)}) copy-start(bf16[128,1024]{1,0:T(8,128)(2,1)} %get-tuple-element.39) | copy-start | bytes 786436
  187.0 18.5 %collective-permute-start.9 = (bf16[192,1024]{1,0:T(8,128)(2,1)}, bf16[192,1024]{1,0:T(8,128)(2,1)S(1)}, u32[]{:S(2)}, u32[]{:S(2)}) collective-permute-start(bf16[192,1024]{1,0:T(8,128)(2,1)} %get-tuple-element.38), channel_id=1, source_target_pairs={{0,1},{1,0},{2,3},{3,2},{4,5},{5,4},{6,7},{7,6},{8,9},{9,8},{10,11... | collective-permute-start | bytes 1179656 | tf_op jit(solution)/shard_map/ppermute | solution.py:450
  188.9 16.5 %collective-permute-start.10 = (bf16[128,1024]{1,0:T(8,128)(2,1)S(1)}, bf16[128,1024]{1,0:T(8,128)(2,1)S(1)}, u32[]{:S(2)}, u32[]{:S(2)}) collective-permute-start(bf16[128,1024]{1,0:T(8,128)(2,1)S(1)} %copy-done.15), channel_id=1, source_target_pairs={{1,2},{3,4},{5,6},{7,8},{9,10},{11,12},{13,14},{15,16},{17,18},{19... | collective-permute-start | bytes 786440 | tf_op jit(solution)/shard_map/ppermute | solution.py:506
  205.4 0.7 copy-start.7
  205.4 0.8 copy-start.6
  205.4 1.0 copy-start

commit v2 on v1

--- a/solution.py
+++ b/solution.py
@@ -60,11 +60,10 @@
 
 
 def local_kernel(width, peers):
-    def kernel(index, mask, key, value, sib, oth, gather):
+    def kernel(index, mask, key, value, sib, oth, pair, gather):
         parity = index[0]
         tokens = key.shape[0]
         length = jnp.sum(mask[...], axis=1, keepdims=True)
-        live = (rows_of((tokens, LANES)) < length).astype(bf16)
         for ref, block in ((sib, 1 - parity), (oth, parity)):
             start = pl.multiple_of(block * BLOCK, BLOCK)
             ref[pl.ds(0, BLOCK), pl.ds(0, width)] = key[pl.ds(start, BLOCK)]
@@ -89,6 +88,10 @@
         sib[pl.ds(BLOCK, COARSE), pl.ds(0, width)] = k_mean
         sib[pl.ds(BLOCK, COARSE), pl.ds(width, width)] = v_mean
         sib[pl.ds(BLOCK, COARSE), pl.ds(2 * width, LANES)] = count
+        k_mean, v_mean, count = means(COARSE // 2)
+        pair[:, pl.ds(0, width)] = k_mean
+        pair[:, pl.ds(width, width)] = v_mean
+        pair[:, pl.ds(2 * width, LANES)] = count
         few = gather.shape[1]
         k_mean, v_mean, count = means(few)
         for peer in range(peers):
@@ -117,33 +120,26 @@
         sums[tile, pl.ds(at, rows)] = mean * count
 
 
-def climb_kernel(first_own, first_other, bit):
-    def kernel(index, own, other, out, sums, counts):
-        side = index[bit]
-        at_own = pl.multiple_of(side * COARSE, COARSE)
-        at_other = pl.multiple_of((1 - side) * COARSE, COARSE)
-        load_sums(own, first_own, COARSE, sums, counts, at_own)
-        load_sums(other, first_other, COARSE, sums, counts, at_other)
-        store_means(
-            out, 0, pooled(sums, COARSE, 2), pooled(counts, COARSE, 2), sums.shape[0] * LANES
-        )
-
-    return kernel
-
-
-def pooled(ref, rows, step):
+def pooled(ref, rows, step, base=0):
     if len(ref.shape) == 3:
         return jnp.concatenate(
-            [pooled(ref.at[tile], rows, step) for tile in range(ref.shape[0])], axis=1
+            [pooled(ref.at[tile], rows, step, base) for tile in range(ref.shape[0])], axis=1
         )
-    total = ref[pl.ds(0, rows, stride=step)]
+    total = ref[pl.ds(base, rows, stride=step)]
     for i in range(1, step):
-        total = total + ref[pl.ds(i, rows, stride=step)]
+        total = total + ref[pl.ds(base + i, rows, stride=step)]
     return total
 
 
-def group_kernel(groups):
-    def kernel(index, recv, six, seven, wide, sums, counts):
+def quarter_at(index, flip_bits):
+    few = COARSE // 4
+    return pl.multiple_of(((index[3] & 3) ^ flip_bits) * few, few)
+
+
+def climb_kernel(groups):
+    def kernel(
+        index, sib_in, pair, pair_a, pair_b, recv, three, six, seven, wide, sums, counts
+    ):
         width = sums.shape[0] * LANES
         total = recv.shape[0]
         load_sums(recv, 0, total, sums, counts, 0)
@@ -162,6 +158,17 @@
         for peer in range(groups):
             wide[peer, :, pl.ds(0, width)] = mean
             wide[peer, :, pl.ds(width, LANES)] = code
+        few = COARSE // 4
+        for ref, first, rows, bits in (
+            (pair, 0, half, 0), (sib_in, BLOCK, COARSE, 1), (pair_a, 0, half, 2), (pair_b, 0, half, 3)
+        ):
+            base = bits * COARSE
+            load_sums(ref, first, rows, sums, counts, base)
+            step = rows // few
+            store_means(
+                three, quarter_at(index, bits), pooled(sums, few, step, base),
+                pooled(counts, few, step, base), width,
+            )
 
     return kernel
 
@@ -174,7 +181,7 @@
     half = COARSE // 2
 
     def kernel(
-        index, query, cot, sib, oth, sib_in, oth_in, two_in, three_in, shard_in, six_in,
+        index, query, cot, sib, oth, sib_in, oth_in, pair_a, pair_b, three_in, shard_in, six_in,
         seven_a, seven_b, group_in,
         attended, query_grad, own_grad, sib_grad, oth_grad, low_grad, three_out,
         shard_part, six_out, seven_a_out, seven_b_out, group_out,
@@ -204,7 +211,8 @@
         quad_at = pl.multiple_of(quad_group * COARSE, COARSE)
         half_group_at = pl.multiple_of(half_group * 2 * COARSE, 2 * COARSE)
         take(0, sib_in, BLOCK, COARSE)
-        take(COARSE, two_in, 0, COARSE)
+        take(COARSE, pair_a, 0, half)
+        take(COARSE + half, pair_b, 0, half)
         take(2 * COARSE, three_in, 0, COARSE)
         take(3 * COARSE, shard_in, octet_at, COARSE)
         load_sums(shard_in, half_shard_at, 2 * COARSE, sums, counts, 0)
@@ -368,7 +376,10 @@
     return jnp.broadcast_to(rows[:, None], (count, times, width)).reshape(count * times, width)
 
 
-def shard_back_kernel(index, part, six, seven_a, seven_b, group, out, acc):
+def back_kernel(
+    index, part, six, seven_a, seven_b, group, three, low, sib_grad,
+    out, sib_out, pair_a, pair_b, mine, acc,
+):
     octet, half_shard = index[4], index[5]
     tile = six[...].astype(f32) + widen(seven_a[...].astype(f32) + seven_b[...].astype(f32), 2)
     few = COARSE // 4
@@ -382,28 +393,23 @@
     acc[octet_at] = acc[octet_at] + part[pl.ds(0, COARSE)]
     acc[half_at] = acc[half_at] + widen(part[pl.ds(COARSE, COARSE)], 2)
     out[...] = acc[...].astype(bf16)
-
-
-def two_back_kernel(index, three, low, out):
-    side = index[1]
     half = COARSE // 2
-    theirs = three[pl.ds(pl.multiple_of((1 - side) * half, half), half)].astype(f32)
-    out[...] = (low[pl.ds(COARSE, COARSE)] + widen(theirs, 2)).astype(bf16)
-
-
-def one_back_kernel(index, three, two, low, sib_grad, out, mine, tile):
-    side, low_side = index[1], index[0]
-    half = COARSE // 2
-    upper = three[pl.ds(pl.multiple_of(side * half, half), half)].astype(f32)
-    tile[...] = widen(upper, 2) + two[...].astype(f32)
-    theirs = tile[pl.ds(pl.multiple_of((1 - low_side) * half, half), half)]
-    out[pl.ds(0, BLOCK)] = sib_grad[...]
-    out[pl.ds(BLOCK, COARSE)] = (low[pl.ds(0, COARSE)] + widen(theirs, 2)).astype(bf16)
-    mine[...] = tile[pl.ds(pl.multiple_of(low_side * half, half), half)]
+
+    def quarter(bits):
+        return three[pl.ds(quarter_at(index, bits), few)].astype(f32)
+
+    sib_out[pl.ds(0, BLOCK)] = sib_grad[...]
+    sib_out[pl.ds(BLOCK, COARSE)] = (low[pl.ds(0, COARSE)] + widen(quarter(1), 4)).astype(bf16)
+    pair_a[...] = (low[pl.ds(COARSE, half)] + widen(quarter(2), 2)).astype(bf16)
+    pair_b[...] = (low[pl.ds(COARSE + half, half)] + widen(quarter(3), 2)).astype(bf16)
+    mine[...] = quarter(0)
 
 
 def final_kernel(width):
-    def kernel(index, mask, own, sib_back, oth_back, mine, shard, key_grad, value_grad, spread):
+    def kernel(
+        index, mask, own, sib_back, oth_back, pair_a, pair_b, mine, shard,
+        key_grad, value_grad, spread,
+    ):
         parity = index[0]
         tokens = key_grad.shape[0]
         length = jnp.sum(mask[...], axis=1, keepdims=True)
@@ -411,7 +417,8 @@
         total = shard[0].astype(f32)
         for i in range(1, shard.shape[0]):
             total = total + shard[i].astype(f32)
-        tile = widen(total, COARSE // few) + widen(mine[...], 2)
+        tile = widen(total, COARSE // few) + widen(mine[...], 4)
+        tile = tile + widen(pair_a[...].astype(f32) + pair_b[...].astype(f32), 2)
         tile = tile + sib_back[pl.ds(BLOCK, COARSE)].astype(f32)
         spread[...] = widen(tile, tokens // COARSE)
         for i, (block, near) in enumerate(((1 - parity, sib_back), (parity, oth_back))):
@@ -454,49 +461,43 @@
 
     few_shard = 2 * COARSE // 16
     few_group = COARSE // 4
-    sib, oth, gather = call(
+    sib, oth, pair, gather = call(
         local_kernel(width, shards),
         [
-            shape(BLOCK + COARSE, row), shape(BLOCK, row),
+            shape(BLOCK + COARSE, row), shape(BLOCK, row), shape(half, row),
             jax.ShapeDtypeStruct((shards, few_shard, row), bf16),
         ],
         [], index, mask, key_states, value_states, name="local",
     )
     sib_in = on_shard(sib, 1)
+    pair_a = on_shard(pair, 2)
+    pair_b = on_shard(pair, 3)
     oth_in = lax.ppermute(oth, ("grp", "shard"), pairs)
     shard_in = lax.all_to_all(gather, "shard", 0, 0, tiled=True).reshape(shards * few_shard, row)
-    tile_scratch = [
-        pltpu.VMEM((packed // LANES, 2 * COARSE, LANES), f32),
-        pltpu.VMEM((2 * COARSE, LANES), f32),
-    ]
-    (two,) = call(
-        climb_kernel(BLOCK, BLOCK, 0), [shape(COARSE, row)], tile_scratch, index, sib, sib_in, name="climb_two"
-    )
-    two_in = on_shard(two, 2)
-    six, seven, wide = call(
-        group_kernel(groups),
-        [shape(COARSE, row), shape(half, row), jax.ShapeDtypeStruct((groups, few_group, row), bf16)],
+    three, six, seven, wide = call(
+        climb_kernel(groups),
+        [
+            shape(COARSE, row), shape(COARSE, row), shape(half, row),
+            jax.ShapeDtypeStruct((groups, few_group, row), bf16),
+        ],
         [
             pltpu.VMEM((packed // LANES, shards * few_shard, LANES), f32),
             pltpu.VMEM((shards * few_shard, LANES), f32),
         ],
-        index, shard_in, name="climb_six",
+        index, sib_in, pair, pair_a, pair_b, shard_in, name="climb",
     )
     six_in = on_group(six, 1)
     seven_a = on_group(seven, 2)
     seven_b = on_group(seven, 3)
+    three_in = on_shard(three, 4)
     group_in = lax.all_to_all(wide, "grp", 0, 0, tiled=True).reshape(groups * few_group, row)
-    (three,) = call(
-        climb_kernel(0, 0, 1), [shape(COARSE, row)], tile_scratch, index, two, two_in, name="climb_three"
-    )
-    three_in = on_shard(three, 4)
     kernel, outs, scratch = attention_kernel(width, shards * few_shard, groups * few_group)
     (
         attended, query_grad, own_grad, sib_grad, oth_grad, low_grad, three_out, shard_part,
         six_out, seven_a_out, seven_b_out, group_out,
     ) = call(
         kernel, outs, scratch, index, query_states, attended_grad, sib, oth, sib_in, oth_in,
-        two_in, three_in, shard_in, six_in, seven_a, seven_b, group_in,
+        pair_a, pair_b, three_in, shard_in, six_in, seven_a, seven_b, group_in,
         flops=1_600_000_000, name="attention",
     )
     six_back = on_group(six_out, 1)
@@ -505,26 +506,24 @@
     three_back = on_shard(three_out, 4)
     oth_back = lax.ppermute(oth_grad, ("grp", "shard"), pairs)
     group_back = lax.all_to_all(group_out, "grp", 0, 0, tiled=True)
-    (two_out,) = call(
-        two_back_kernel, [shape(COARSE, packed)], [], index, three_back, low_grad, name="back_two"
-    )
-    two_back = on_shard(two_out, 2)
-    (shard_out,) = call(
-        shard_back_kernel, [shape(shards * few_shard, packed)],
+    shard_out, sib_out, pair_a_out, pair_b_out, mine = call(
+        back_kernel,
+        [
+            shape(shards * few_shard, packed), shape(BLOCK + COARSE, packed),
+            shape(half, packed), shape(half, packed), shape(few_group, packed, f32),
+        ],
         [pltpu.VMEM((shards * few_shard, packed), f32)],
-        index, shard_part, six_back, seven_a_back, seven_b_back, group_back, name="back_six",
-    )
-    sib_out, mine = call(
-        one_back_kernel, [shape(BLOCK + COARSE, packed), shape(half, packed, f32)],
-        [pltpu.VMEM((COARSE, packed), f32)],
-        index, three_back, two_back, low_grad, sib_grad, name="back_one",
+        index, shard_part, six_back, seven_a_back, seven_b_back, group_back, three_back,
+        low_grad, sib_grad, name="back",
     )
     sib_back = on_shard(sib_out, 1)
+    pair_a_back = on_shard(pair_a_out, 2)
+    pair_b_back = on_shard(pair_b_out, 3)
     shard_back = lax.all_to_all(shard_out, "shard", 0, 0, tiled=True)
     key_grad, value_grad = call(
         final_kernel(width), [shape(tokens, width), shape(tokens, width)],
         [pltpu.VMEM((tokens, packed), f32)],
-        index, mask, own_grad, sib_back, oth_back, mine,
+        index, mask, own_grad, sib_back, oth_back, pair_a_back, pair_b_back, mine,
         shard_back.reshape(shards, few_shard, packed), name="final",
     )
     return attended, query_grad, key_grad, value_grad

time: 211 us -> 170 us (0.81)
  blocking collectives: 31.6 us -> 0 us
  waiting for transfers between devices: 59.6 us -> 47.5 us
  starting transfers between devices: 81.6 us -> 93.1 us
  Pallas kernels: 29.7 us -> 22.8 us
    all_to_all x1 -> x0, blocking collectives: 31.6 us -> none  [body(): lax.all_to_all(gather, 'shard', 0, 0, tiled=True)]
    ppermute x6 -> x8, waiting for transfers between devices: 41.2 us -> 23.9 us  [on_shard(): return lax.ppermute(x, 'shard', flip(shards, bits))]
    all_to_all x0 -> x1, starting transfers between devices: none -> 13.6 us  [body(): lax.all_to_all(gather, 'shard', 0, 0, tiled=True)]
    all_to_all x1, starting transfers between devices: 4.43 us -> 13.7 us  [body(): shard_back = lax.all_to_all(shard_out, 'shard', 0, 0, tiled=True)]
    ppermute x6, starting transfers between devices: 24.1 us -> 15.9 us  [on_group(): return lax.ppermute(x, 'grp', flip(groups, bits))]
    pallas_call x9 -> x5, Pallas kernels: 29.7 us -> 22.8 us  [call(): pl.pallas_call(kernel, out_shape=outs, in_specs=in_specs, out_specs=[pl.B...]
    all_to_all x1, waiting for transfers between devices: 0.01 us -> 6.95 us  [body(): lax.all_to_all(wide, 'grp', 0, 0, tiled=True)]
    all_to_all x1, starting transfers between devices: 9.46 us -> 4.55 us  [body(): group_back = lax.all_to_all(group_out, 'grp', 0, 0, tiled=True)]
  transfers between devices with their start and end apart: 17 -> 20, of which waited for: 10 -> 8; matrix products, arithmetic and copies ran while one was open for 0% -> 0% of each run, Pallas kernels for 4% -> 0%
where the time goes in v2:
time: 170 us; the launch traced here: 169 us
  starting transfers between devices  93.1 us (55%)
  waiting for transfers between devices  47.5 us (28%)
  Pallas kernels  22.8 us (13%)
  local copies, waits for them, and re-layouts  4.28 us (3%)
    ppermute x8, waiting for transfers between devices, on_shard(): return lax.ppermute(x, 'shard', flip(shards, bits))  23.9 us
    pallas_call x5, Pallas kernels, call(): pl.pallas_call(kernel, out_shape=outs, in_specs=in_specs, out_specs=[pl.B...  22.8 us
    ppermute x8, starting transfers between devices, on_shard(): return lax.ppermute(x, 'shard', flip(shards, bits))  21 us
    ppermute x6, starting transfers between devices, on_group(): return lax.ppermute(x, 'grp', flip(groups, bits))  15.9 us
    all_to_all x1, starting transfers between devices, body(): shard_back = lax.all_to_all(shard_out, 'shard', 0, 0, tiled=True)  13.7 us
    all_to_all x1, starting transfers between devices, body(): lax.all_to_all(gather, 'shard', 0, 0, tiled=True)  13.6 us
    all_to_all x1, starting transfers between devices, body(): lax.all_to_all(wide, 'grp', 0, 0, tiled=True)  11.9 us
    ppermute x1, waiting for transfers between devices, body(): oth_back = lax.ppermute(oth_grad, ('grp', 'shard'), pairs)  8.92 us
  transfers between devices with their start and end apart: 20, of which 8 were waited for; matrix products, arithmetic and copies ran while one was open for 0% of the time, Pallas kernels for 0%

profile of v2, /device:TPU:1, one launch (start us, length us, event | category | flops | bytes accessed | tf_op | source)
XLA Modules:
  0.0 168.9 jit_solution(2365162253255743798)
XLA Ops:
  0.6 0.6 stack.35.index
  1.2 2.5 %local.1 = (bf16[192,1152]{1,0:T(8,128)(2,1)}, bf16[128,1152]{1,0:T(8,128)(2,1)}, bf16[32,1152]{1,0:T(8,128)(2,1)}, bf16[32,8,1152]{2,1,0:T(8,128)(2,1)}) custom-call(s32[8]{0:T(128)} %stack.35.index, s32[1,256]{1,0:T(1,128)} %bitcast.20, bf16[256,512]{1,0:T(8,128)(2,1)} %key.1, bf16[256,512]{1,0:T(8,128)(2,1)} %value.1), custom_call_target="tpu_custom_call" | custom-call | bytes 1926144 | tf_op jit(solution)/shard_map/local/pallas_call | solution.py:30
  3.7 13.6 %all-to-all-start = ((bf16[32,8,1152]{2,1,0:T(8,128)(2,1)}), bf16[32,8,1152]{2,1,0:T(8,128)(2,1)S(1)}, u32[]{:S(2)}, u32[]{:S(2)}) async-start(bf16[32,8,1152]{2,1,0:T(8,128)(2,1)} %get-tuple-element.34), calls=%async_computation | async-start | bytes 1179648 | tf_op jit(solution)/shard_map/all_to_all | solution.py:476
  17.3 3.1 %collective-permute-start = (bf16[192,1152]{1,0:T(8,128)(2,1)S(1)}, bf16[192,1152]{1,0:T(8,128)(2,1)S(1)}, u32[]{:S(2)}, u32[]{:S(2)}) collective-permute-start(bf16[192,1152]{1,0:T(8,128)(2,1)S(1)} %copy-done.16), channel_id=1, source_target_pairs={{0,1},{1,0},{2,3},{3,2},{4,5},{5,4},{6,7},{7,6},{8,9},{9,8},{10,11... | collective-permute-start | bytes 1327112 | tf_op jit(solution)/shard_map/ppermute | solution.py:457
  20.5 4.0 %collective-permute-start.3 = (bf16[32,1152]{1,0:T(8,128)(2,1)S(1)}, bf16[32,1152]{1,0:T(8,128)(2,1)S(1)}, u32[]{:S(2)}, u32[]{:S(2)}) collective-permute-start(bf16[32,1152]{1,0:T(8,128)(2,1)S(1)} %copy-done.11), channel_id=1, source_target_pairs={{0,3},{1,2},{2,1},{3,0},{4,7},{5,6},{6,5},{7,4},{8,11},{9,10},{10,... | collective-permute-start | bytes 221192 | tf_op jit(solution)/shard_map/ppermute | solution.py:457
  24.5 1.9 %collective-permute-start.2 = (bf16[32,1152]{1,0:T(8,128)(2,1)S(1)}, bf16[32,1152]{1,0:T(8,128)(2,1)S(1)}, u32[]{:S(2)}, u32[]{:S(2)}) collective-permute-start(bf16[32,1152]{1,0:T(8,128)(2,1)S(1)} %copy-done.11), channel_id=1, source_target_pairs={{0,2},{1,3},{2,0},{3,1},{4,6},{5,7},{6,4},{7,5},{8,10},{9,11},{10,... | collective-permute-start | bytes 221192 | tf_op jit(solution)/shard_map/ppermute | solution.py:457
  26.4 16.0 %collective-permute-done.3.pair_b = bf16[32,1152]{1,0:T(8,128)(2,1)S(1)} collective-permute-done((bf16[32,1152]{1,0:T(8,128)(2,1)S(1)}, bf16[32,1152]{1,0:T(8,128)(2,1)S(1)}, u32[]{:S(2)}, u32[]{:S(2)}) %collective-permute-start.3) | collective-permute-done | bytes 73760 | tf_op jit(solution)/shard_map/ppermute | solution.py:457
  42.4 0.6 copy-done.9
  43.0 0.0 copy-done.10
  43.1 0.2 copy-done.4
  43.2 0.2 copy-done
  43.4 2.9 %climb.1 = (bf16[64,1152]{1,0:T(8,128)(2,1)}, bf16[64,1152]{1,0:T(8,128)(2,1)}, bf16[32,1152]{1,0:T(8,128)(2,1)}, bf16[16,16,1152]{2,1,0:T(8,128)(2,1)}) custom-call(s32[8]{0:T(128)} %stack.35.index, bf16[192,1152]{1,0:T(8,128)(2,1)} %copy-done.4, bf16[32,1152]{1,0:T(8,128)(2,1)} %get-tuple-element.33.pair, bf16[32,1152]{1,0:T(8,128)(2,1)} %copy-done.10, ...), custom_call_target="tpu_custom_call" | custom-call | bytes 2211840 | tf_op jit(solution)/shard_map/climb/pallas_call | solution.py:30
  46.3 0.0 copy-start.29
  46.3 11.9 %all-to-all-start.1 = ((bf16[16,16,1152]{2,1,0:T(8,128)(2,1)}), bf16[16,16,1152]{2,1,0:T(8,128)(2,1)S(1)}, u32[]{:S(2)}, u32[]{:S(2)}) async-start(bf16[16,16,1152]{2,1,0:T(8,128)(2,1)} %get-tuple-element.38), calls=%async_computation.1 | async-start | bytes 1179648 | tf_op jit(solution)/shard_map/all_to_all | solution.py:493
  58.2 5.2 %collective-permute-start.1 = (bf16[128,1152]{1,0:T(8,128)(2,1)S(1)}, bf16[128,1152]{1,0:T(8,128)(2,1)S(1)}, u32[]{:S(2)}, u32[]{:S(2)}) collective-permute-start(bf16[128,1152]{1,0:T(8,128)(2,1)S(1)} %copy-done.18), channel_id=1, source_target_pairs={{1,2},{3,4},{5,6},{7,8},{9,10},{11,12},{13,14},{15,16},{17,18},{19... | collective-permute-start | bytes 884744 | tf_op jit(solution)/shard_map/ppermute | solution.py:475
  63.4 1.9 %collective-permute-start.4 = (bf16[64,1152]{1,0:T(8,128)(2,1)S(1)}, bf16[64,1152]{1,0:T(8,128)(2,1)S(1)}, u32[]{:S(2)}, u32[]{:S(2)}) collective-permute-start(bf16[64,1152]{1,0:T(8,128)(2,1)S(1)} %copy-done.24), channel_id=1, source_target_pairs={{0,4},{1,5},{2,6},{3,7},{4,0},{5,1},{6,2},{7,3},{8,12},{9,13},{10,... | collective-permute-start | bytes 442376 | tf_op jit(solution)/shard_map/ppermute | solution.py:457
  65.4 1.9 %collective-permute-start.5 = (bf16[64,1152]{1,0:T(8,128)(2,1)S(1)}, bf16[64,1152]{1,0:T(8,128)(2,1)S(1)}, u32[]{:S(2)}, u32[]{:S(2)}) collective-permute-start(bf16[64,1152]{1,0:T(8,128)(2,1)S(1)} %copy-done.23), channel_id=1, source_target_pairs={{0,32},{32,0},{64,96},{96,64},{128,160},{160,128},{192,224},{224,1... | collective-permute-start | bytes 442376 | tf_op jit(solution)/shard_map/ppermute | solution.py:460
  67.3 3.9 %collective-permute-start.7 = (bf16[32,1152]{1,0:T(8,128)(2,1)S(1)}, bf16[32,1152]{1,0:T(8,128)(2,1)S(1)}, u32[]{:S(2)}, u32[]{:S(2)}) collective-permute-start(bf16[32,1152]{1,0:T(8,128)(2,1)S(1)} %copy-done.29), channel_id=1, source_target_pairs={{0,96},{32,64},{64,32},{96,0},{128,224},{160,192},{192,160},{224,1... | collective-permute-start | bytes 221192 | tf_op jit(solution)/shard_map/ppermute | solution.py:460
  71.2 1.9 %collective-permute-start.6 = (bf16[32,1152]{1,0:T(8,128)(2,1)S(1)}, bf16[32,1152]{1,0:T(8,128)(2,1)S(1)}, u32[]{:S(2)}, u32[]{:S(2)}) collective-permute-start(bf16[32,1152]{1,0:T(8,128)(2,1)S(1)} %copy-done.29), channel_id=1, source_target_pairs={{0,64},{32,96},{64,0},{96,32},{128,192},{160,224},{192,128},{224,1... | collective-permute-start | bytes 221192 | tf_op jit(solution)/shard_map/ppermute | solution.py:460
  73.2 1.1 collective-permute-done.7.seven_b
  74.3 2.8 %collective-permute-done.6.seven_a = bf16[32,1152]{1,0:T(8,128)(2,1)S(1)} collective-permute-done((bf16[32,1152]{1,0:T(8,128)(2,1)S(1)}, bf16[32,1152]{1,0:T(8,128)(2,1)S(1)}, u32[]{:S(2)}, u32[]{:S(2)}) %collective-permute-start.6) | collective-permute-done | bytes 73760 | tf_op jit(solution)/shard_map/ppermute | solution.py:460
  77.0 6.9 %all-to-all-done.1 = bf16[16,16,1152]{2,1,0:T(8,128)(2,1)S(1)} async-done(((bf16[16,16,1152]{2,1,0:T(8,128)(2,1)}), bf16[16,16,1152]{2,1,0:T(8,128)(2,1)S(1)}, u32[]{:S(2)}, u32[]{:S(2)}) %all-to-all-start.1) | async-done | bytes 589856 | tf_op jit(solution)/shard_map/all_to_all | solution.py:493
  84.0 0.8 copy-done.3
  84.8 10.8 %attention.1 = (bf16[256,512]{1,0:T(8,128)(2,1)}, bf16[256,512]{1,0:T(8,128)(2,1)}, f32[256,1024]{1,0:T(8,128)}, bf16[128,1024]{1,0:T(8,128)(2,1)}, bf16[128,102...) custom-call(s32[8]{0:T(128)} %stack.35.index, ...), custom_call_target="tpu_custom_call" | custom-call | flops 1600000000 | bytes 7831552 | tf_op jit(solution)/shard_map/attention/pallas_call | solution.py:30
  95.6 4.6 %all-to-all-start.2 = ((bf16[16,16,1024]{2,1,0:T(8,128)(2,1)}), bf16[16,16,1024]{2,1,0:T(8,128)(2,1)S(1)}, u32[]{:S(2)}, u32[]{:S(2)}) async-start(bf16[16,16,1024]{2,1,0:T(8,128)(2,1)} %bitcast.18), calls=%async_computation.2 | async-start | bytes 1048576 | tf_op jit(solution)/shard_map/all_to_all | solution.py:508
  100.2 2.0 %collective-permute-start.8 = (bf16[64,1024]{1,0:T(8,128)(2,1)S(1)}, bf16[64,1024]{1,0:T(8,128)(2,1)S(1)}, u32[]{:S(2)}, u32[]{:S(2)}) collective-permute-start(bf16[64,1024]{1,0:T(8,128)(2,1)S(1)} %copy-done.26), channel_id=1, source_target_pairs={{0,32},{32,0},{64,96},{96,64},{128,160},{160,128},{192,224},{224,1... | collective-permute-start | bytes 393224 | tf_op jit(solution)/shard_map/ppermute | solution.py:460
  102.2 3.1 %collective-permute-start.11 = (bf16[64,1024]{1,0:T(8,128)(2,1)S(1)}, bf16[64,1024]{1,0:T(8,128)(2,1)S(1)}, u32[]{:S(2)}, u32[]{:S(2)}) collective-permute-start(bf16[64,1024]{1,0:T(8,128)(2,1)S(1)} %copy-done.25), channel_id=1, source_target_pairs={{0,4},{1,5},{2,6},{3,7},{4,0},{5,1},{6,2},{7,3},{8,12},{9,13},{10,... | collective-permute-start | bytes 393224 | tf_op jit(solution)/shard_map/ppermute | solution.py:457
  105.3 3.5 %collective-permute-start.9 = (bf16[32,1024]{1,0:T(8,128)(2,1)S(1)}, bf16[32,1024]{1,0:T(8,128)(2,1)S(1)}, u32[]{:S(2)}, u32[]{:S(2)}) collective-permute-start(bf16[32,1024]{1,0:T(8,128)(2,1)S(1)} %copy-done.31), channel_id=1, source_target_pairs={{0,64},{32,96},{64,0},{96,32},{128,192},{160,224},{192,128},{224,1... | collective-permute-start | bytes 196616 | tf_op jit(solution)/shard_map/ppermute | solution.py:460
  108.9 2.6 %collective-permute-start.10 = (bf16[32,1024]{1,0:T(8,128)(2,1)S(1)}, bf16[32,1024]{1,0:T(8,128)(2,1)S(1)}, u32[]{:S(2)}, u32[]{:S(2)}) collective-permute-start(bf16[32,1024]{1,0:T(8,128)(2,1)S(1)} %copy-done.30), channel_id=1, source_target_pairs={{0,96},{32,64},{64,32},{96,0},{128,224},{160,192},{192,160},{224,1... | collective-permute-start | bytes 196616 | tf_op jit(solution)/shard_map/ppermute | solution.py:460
  111.5 0.9 collective-permute-done.9.seven_a
  112.4 3.0 %collective-permute-done.10.seven_b = bf16[32,1024]{1,0:T(8,128)(2,1)S(1)} collective-permute-done((bf16[32,1024]{1,0:T(8,128)(2,1)S(1)}, bf16[32,1024]{1,0:T(8,128)(2,1)S(1)}, u32[]{:S(2)}, u32[]{:S(2)}) %collective-permute-start.10) | collective-permute-done | bytes 65568 | tf_op jit(solution)/shard_map/ppermute | solution.py:460
  115.5 0.6 copy-done.14
  116.1 0.1 copy-done.7
  116.1 0.0 copy-done.8
  116.2 0.2 copy-done.1
  116.4 3.4 %back.1 = (bf16[256,1024]{1,0:T(8,128)(2,1)}, bf16[192,1024]{1,0:T(8,128)(2,1)}, bf16[32,1024]{1,0:T(8,128)(2,1)}, bf16[32,1024]{1,0:T(8,128)(2,1)}, f32[16,1024]{1,0:T(8,128)}) custom-call(s32[8]{0:T(128)} %stack.35.index, f32[128,1024]{1,0:T(8,128)} %get-tuple-element.42.part, bf16[64,1024]{1,0:T(8,128)(2,1)} %copy-done.7, bf16[32,1024]{1,0:T(8,128)(2,1)} %copy-done.12, ...), custom_call_target="tpu_custom_call" | custom-call | bytes 3342336 | tf_op jit(solution)/shard_map/back/pallas_call | solution.py:30
  119.8 13.7 %all-to-all-start.3 = ((bf16[32,8,1024]{2,1,0:T(8,128)(2,1)}), bf16[32,8,1024]{2,1,0:T(8,128)(2,1)S(1)}, u32[]{:S(2)}, u32[]{:S(2)}) async-start(bf16[32,8,1024]{2,1,0:T(8,128)(2,1)} %bitcast.19), calls=%async_computation.3 | async-start | bytes 1048576 | tf_op jit(solution)/shard_map/all_to_all | solution.py:522
  133.5 3.1 %collective-permute-start.12 = (bf16[192,1024]{1,0:T(8,128)(2,1)S(1)}, bf16[192,1024]{1,0:T(8,128)(2,1)S(1)}, u32[]{:S(2)}, u32[]{:S(2)}) collective-permute-start(bf16[192,1024]{1,0:T(8,128)(2,1)S(1)} %copy-done.17), channel_id=1, source_target_pairs={{0,1},{1,0},{2,3},{3,2},{4,5},{5,4},{6,7},{7,6},{8,9},{9,8},{10,11... | collective-permute-start | bytes 1179656 | tf_op jit(solution)/shard_map/ppermute | solution.py:457
  136.7 7.3 %collective-permute-start.13 = (bf16[128,1024]{1,0:T(8,128)(2,1)S(1)}, bf16[128,1024]{1,0:T(8,128)(2,1)S(1)}, u32[]{:S(2)}, u32[]{:S(2)}) collective-permute-start(bf16[128,1024]{1,0:T(8,128)(2,1)S(1)} %copy-done.20), channel_id=1, source_target_pairs={{1,2},{3,4},{5,6},{7,8},{9,10},{11,12},{13,14},{15,16},{17,18},{19... | collective-permute-start | bytes 786440 | tf_op jit(solution)/shard_map/ppermute | solution.py:507
  144.0 1.9 %collective-permute-start.14 = (bf16[32,1024]{1,0:T(8,128)(2,1)S(1)}, bf16[32,1024]{1,0:T(8,128)(2,1)S(1)}, u32[]{:S(2)}, u32[]{:S(2)}) collective-permute-start(bf16[32,1024]{1,0:T(8,128)(2,1)S(1)} %copy-done.33), channel_id=1, source_target_pairs={{0,2},{1,3},{2,0},{3,1},{4,6},{5,7},{6,4},{7,5},{8,10},{9,11},{10,... | collective-permute-start | bytes 196616 | tf_op jit(solution)/shard_map/ppermute | solution.py:457
  145.9 1.9 %collective-permute-start.15 = (bf16[32,1024]{1,0:T(8,128)(2,1)S(1)}, bf16[32,1024]{1,0:T(8,128)(2,1)S(1)}, u32[]{:S(2)}, u32[]{:S(2)}) collective-permute-start(bf16[32,1024]{1,0:T(8,128)(2,1)S(1)} %copy-done.32), channel_id=1, source_target_pairs={{0,3},{1,2},{2,1},{3,0},{4,7},{5,6},{6,5},{7,4},{8,11},{9,10},{10,... | collective-permute-start | bytes 196616 | tf_op jit(solution)/shard_map/ppermute | solution.py:457
  147.9 8.9 %collective-permute-done.13.oth_back = bf16[128,1024]{1,0:T(8,128)(2,1)S(1)} collective-permute-done((bf16[128,1024]{1,0:T(8,128)(2,1)S(1)}, bf16[128,1024]{1,0:T(8,128)(2,1)S(1)}, u32[]{:S(2)}, u32[]{:S(2)}) %collective-permute-start.13) | collective-permute-done | bytes 262176 | tf_op jit(solution)/shard_map/ppermute | solution.py:507
  156.8 7.9 %collective-permute-done.14.pair_a = bf16[32,1024]{1,0:T(8,128)(2,1)S(1)} collective-permute-done((bf16[32,1024]{1,0:T(8,128)(2,1)S(1)}, bf16[32,1024]{1,0:T(8,128)(2,1)S(1)}, u32[]{:S(2)}, u32[]{:S(2)}) %collective-permute-start.14) | collective-permute-done | bytes 65568 | tf_op jit(solution)/shard_map/ppermute | solution.py:457
  164.7 0.6 copy-done.13
  165.3 0.0 copy-done.15
  165.3 0.2 copy-done.5
  165.5 0.2 copy-done.2
  165.6 3.2 %final.1 = (bf16[256,512]{1,0:T(8,128)(2,1)}, bf16[256,512]{1,0:T(8,128)(2,1)}) custom-call(s32[8]{0:T(128)} %stack.35.index, s32[1,256]{1,0:T(1,128)} %bitcast.21, f32[256,1024]{1,0:T(8,128)} %get-tuple-element.41.own, bf16[192,1024]{1,0:T(8,128)(2,1)} %copy-done.5, bf16[128,1024]{1,0:T(8,128)(2,1)} %copy-done.6, bf16[32,1024]{1,0:T(8,128)(2,1)} %copy-done.13, ...), custom_call_target="tpu_custom_call" | custom-call | bytes 2950144 | tf_op jit(solution)/shard_map/final/pallas_call | solution.py:30
  (66 shorter events, 0.1 us)
Async XLA Ops:
  3.7 13.6 %copy-start.16 = (bf16[192,1152]{1,0:T(8,128)(2,1)S(1)}, bf16[192,1152]{1,0:T(8,128)(2,1)}, u32[]{:S(2)}) copy-start(bf16[192,1152]{1,0:T(8,128)(2,1)} %get-tuple-element.31.sib) | copy-start | bytes 1327108
  3.7 16.8 %copy-start.11 = (bf16[32,1152]{1,0:T(8,128)(2,1)S(1)}, bf16[32,1152]{1,0:T(8,128)(2,1)}, u32[]{:S(2)}) copy-start(bf16[32,1152]{1,0:T(8,128)(2,1)} %get-tuple-element.33.pair) | copy-start | bytes 221188
  3.7 38.7 %all-to-all-start = ((bf16[32,8,1152]{2,1,0:T(8,128)(2,1)}), bf16[32,8,1152]{2,1,0:T(8,128)(2,1)S(1)}, u32[]{:S(2)}, u32[]{:S(2)}) async-start(bf16[32,8,1152]{2,1,0:T(8,128)(2,1)} %get-tuple-element.34), calls=%async_computation | async-start | bytes 1179648 | tf_op jit(solution)/shard_map/all_to_all | solution.py:476
  17.3 25.1 %collective-permute-start = (bf16[192,1152]{1,0:T(8,128)(2,1)S(1)}, bf16[192,1152]{1,0:T(8,128)(2,1)S(1)}, u32[]{:S(2)}, u32[]{:S(2)}) collective-permute-start(bf16[192,1152]{1,0:T(8,128)(2,1)S(1)} %copy-done.16), channel_id=1, source_target_pairs={{0,1},{1,0},{2,3},{3,2},{4,5},{5,4},{6,7},{7,6},{8,9},{9,8},{10,11... | collective-permute-start | bytes 1327112 | tf_op jit(solution)/shard_map/ppermute | solution.py:457
  20.5 21.9 %collective-permute-start.3 = (bf16[32,1152]{1,0:T(8,128)(2,1)S(1)}, bf16[32,1152]{1,0:T(8,128)(2,1)S(1)}, u32[]{:S(2)}, u32[]{:S(2)}) collective-permute-start(bf16[32,1152]{1,0:T(8,128)(2,1)S(1)} %copy-done.11), channel_id=1, source_target_pairs={{0,3},{1,2},{2,1},{3,0},{4,7},{5,6},{6,5},{7,4},{8,11},{9,10},{10,... | collective-permute-start | bytes 221192 | tf_op jit(solution)/shard_map/ppermute | solution.py:457
  24.5 17.9 %collective-permute-start.2 = (bf16[32,1152]{1,0:T(8,128)(2,1)S(1)}, bf16[32,1152]{1,0:T(8,128)(2,1)S(1)}, u32[]{:S(2)}, u32[]{:S(2)}) collective-permute-start(bf16[32,1152]{1,0:T(8,128)(2,1)S(1)} %copy-done.11), channel_id=1, source_target_pairs={{0,2},{1,3},{2,0},{3,1},{4,6},{5,7},{6,4},{7,5},{8,10},{9,11},{10,... | collective-permute-start | bytes 221192 | tf_op jit(solution)/shard_map/ppermute | solution.py:457
  42.4 0.8 copy-start.4
  42.4 1.0 copy-start
  46.3 11.9 %copy-start.18 = (bf16[128,1152]{1,0:T(8,128)(2,1)S(1)}, bf16[128,1152]{1,0:T(8,128)(2,1)}, u32[]{:S(2)}) copy-start(bf16[128,1152]{1,0:T(8,128)(2,1)} %get-tuple-element.32.oth) | copy-start | bytes 884740
  46.3 17.1 %copy-start.24 = (bf16[64,1152]{1,0:T(8,128)(2,1)S(1)}, bf16[64,1152]{1,0:T(8,128)(2,1)}, u32[]{:S(2)}) copy-start(bf16[64,1152]{1,0:T(8,128)(2,1)} %get-tuple-element.35) | copy-start | bytes 442372
  46.3 19.0 %copy-start.23 = (bf16[64,1152]{1,0:T(8,128)(2,1)S(1)}, bf16[64,1152]{1,0:T(8,128)(2,1)}, u32[]{:S(2)}) copy-start(bf16[64,1152]{1,0:T(8,128)(2,1)} %get-tuple-element.36) | copy-start | bytes 442372
  46.3 21.0 %copy-start.29 = (bf16[32,1152]{1,0:T(8,128)(2,1)S(1)}, bf16[32,1152]{1,0:T(8,128)(2,1)}, u32[]{:S(2)}) copy-start(bf16[32,1152]{1,0:T(8,128)(2,1)} %get-tuple-element.37) | copy-start | bytes 221188
  46.3 37.7 %all-to-all-start.1 = ((bf16[16,16,1152]{2,1,0:T(8,128)(2,1)}), bf16[16,16,1152]{2,1,0:T(8,128)(2,1)S(1)}, u32[]{:S(2)}, u32[]{:S(2)}) async-start(bf16[16,16,1152]{2,1,0:T(8,128)(2,1)} %get-tuple-element.38), calls=%async_computation.1 | async-start | bytes 1179648 | tf_op jit(solution)/shard_map/all_to_all | solution.py:493
  58.2 14.9 %collective-permute-start.1 = (bf16[128,1152]{1,0:T(8,128)(2,1)S(1)}, bf16[128,1152]{1,0:T(8,128)(2,1)S(1)}, u32[]{:S(2)}, u32[]{:S(2)}) collective-permute-start(bf16[128,1152]{1,0:T(8,128)(2,1)S(1)} %copy-done.18), channel_id=1, source_target_pairs={{1,2},{3,4},{5,6},{7,8},{9,10},{11,12},{13,14},{15,16},{17,18},{19... | collective-permute-start | bytes 884744 | tf_op jit(solution)/shard_map/ppermute | solution.py:475
  63.4 13.6 %collective-permute-start.4 = (bf16[64,1152]{1,0:T(8,128)(2,1)S(1)}, bf16[64,1152]{1,0:T(8,128)(2,1)S(1)}, u32[]{:S(2)}, u32[]{:S(2)}) collective-permute-start(bf16[64,1152]{1,0:T(8,128)(2,1)S(1)} %copy-done.24), channel_id=1, source_target_pairs={{0,4},{1,5},{2,6},{3,7},{4,0},{5,1},{6,2},{7,3},{8,12},{9,13},{10,... | collective-permute-start | bytes 442376 | tf_op jit(solution)/shard_map/ppermute | solution.py:457
  65.4 11.7 %collective-permute-start.5 = (bf16[64,1152]{1,0:T(8,128)(2,1)S(1)}, bf16[64,1152]{1,0:T(8,128)(2,1)S(1)}, u32[]{:S(2)}, u32[]{:S(2)}) collective-permute-start(bf16[64,1152]{1,0:T(8,128)(2,1)S(1)} %copy-done.23), channel_id=1, source_target_pairs={{0,32},{32,0},{64,96},{96,64},{128,160},{160,128},{192,224},{224,1... | collective-permute-start | bytes 442376 | tf_op jit(solution)/shard_map/ppermute | solution.py:460
  67.3 7.0 %collective-permute-start.7 = (bf16[32,1152]{1,0:T(8,128)(2,1)S(1)}, bf16[32,1152]{1,0:T(8,128)(2,1)S(1)}, u32[]{:S(2)}, u32[]{:S(2)}) collective-permute-start(bf16[32,1152]{1,0:T(8,128)(2,1)S(1)} %copy-done.29), channel_id=1, source_target_pairs={{0,96},{32,64},{64,32},{96,0},{128,224},{160,192},{192,160},{224,1... | collective-permute-start | bytes 221192 | tf_op jit(solution)/shard_map/ppermute | solution.py:460
  71.2 5.8 %collective-permute-start.6 = (bf16[32,1152]{1,0:T(8,128)(2,1)S(1)}, bf16[32,1152]{1,0:T(8,128)(2,1)S(1)}, u32[]{:S(2)}, u32[]{:S(2)}) collective-permute-start(bf16[32,1152]{1,0:T(8,128)(2,1)S(1)} %copy-done.29), channel_id=1, source_target_pairs={{0,64},{32,96},{64,0},{96,32},{128,192},{160,224},{192,128},{224,1... | collective-permute-start | bytes 221192 | tf_op jit(solution)/shard_map/ppermute | solution.py:460
  73.2 10.8 %copy-start.19 = (bf16[128,1152]{1,0:T(8,128)(2,1)}, bf16[128,1152]{1,0:T(8,128)(2,1)S(1)}, u32[]{:S(2)}) copy-start(bf16[128,1152]{1,0:T(8,128)(2,1)S(1)} %collective-permute-done.1.oth_in) | copy-start | bytes 884740
  74.3 9.7 %copy-start.27 = (bf16[32,1152]{1,0:T(8,128)(2,1)}, bf16[32,1152]{1,0:T(8,128)(2,1)S(1)}, u32[]{:S(2)}) copy-start(bf16[32,1152]{1,0:T(8,128)(2,1)S(1)} %collective-permute-done.7.seven_b) | copy-start | bytes 221188
  77.0 7.0 %copy-start.28 = (bf16[32,1152]{1,0:T(8,128)(2,1)}, bf16[32,1152]{1,0:T(8,128)(2,1)S(1)}, u32[]{:S(2)}) copy-start(bf16[32,1152]{1,0:T(8,128)(2,1)S(1)} %collective-permute-done.6.seven_a) | copy-start | bytes 221188
  77.0 7.0 %copy-start.21 = (bf16[64,1152]{1,0:T(8,128)(2,1)}, bf16[64,1152]{1,0:T(8,128)(2,1)S(1)}, u32[]{:S(2)}) copy-start(bf16[64,1152]{1,0:T(8,128)(2,1)S(1)} %collective-permute-done.4.three_in) | copy-start | bytes 442372
  77.0 7.0 %copy-start.22 = (bf16[64,1152]{1,0:T(8,128)(2,1)}, bf16[64,1152]{1,0:T(8,128)(2,1)S(1)}, u32[]{:S(2)}) copy-start(bf16[64,1152]{1,0:T(8,128)(2,1)S(1)} %collective-permute-done.5.six_in) | copy-start | bytes 442372
  84.0 0.8 copy-start.3
  95.6 4.6 %copy-start.26 = (bf16[64,1024]{1,0:T(8,128)(2,1)S(1)}, bf16[64,1024]{1,0:T(8,128)(2,1)}, u32[]{:S(2)}) copy-start(bf16[64,1024]{1,0:T(8,128)(2,1)} %get-tuple-element.43) | copy-start | bytes 393220
  95.6 6.6 %copy-start.25 = (bf16[64,1024]{1,0:T(8,128)(2,1)S(1)}, bf16[64,1024]{1,0:T(8,128)(2,1)}, u32[]{:S(2)}) copy-start(bf16[64,1024]{1,0:T(8,128)(2,1)} %get-tuple-element.47) | copy-start | bytes 393220
  95.6 9.7 %copy-start.31 = (bf16[32,1024]{1,0:T(8,128)(2,1)S(1)}, bf16[32,1024]{1,0:T(8,128)(2,1)}, u32[]{:S(2)}) copy-start(bf16[32,1024]{1,0:T(8,128)(2,1)} %get-tuple-element.44) | copy-start | bytes 196612
  95.6 13.2 %copy-start.30 = (bf16[32,1024]{1,0:T(8,128)(2,1)S(1)}, bf16[32,1024]{1,0:T(8,128)(2,1)}, u32[]{:S(2)}) copy-start(bf16[32,1024]{1,0:T(8,128)(2,1)} %get-tuple-element.45) | copy-start | bytes 196612
  95.6 19.8 %all-to-all-start.2 = ((bf16[16,16,1024]{2,1,0:T(8,128)(2,1)}), bf16[16,16,1024]{2,1,0:T(8,128)(2,1)S(1)}, u32[]{:S(2)}, u32[]{:S(2)}) async-start(bf16[16,16,1024]{2,1,0:T(8,128)(2,1)} %bitcast.18), calls=%async_computation.2 | async-start | bytes 1048576 | tf_op jit(solution)/shard_map/all_to_all | solution.py:508
  100.2 15.2 %collective-permute-start.8 = (bf16[64,1024]{1,0:T(8,128)(2,1)S(1)}, bf16[64,1024]{1,0:T(8,128)(2,1)S(1)}, u32[]{:S(2)}, u32[]{:S(2)}) collective-permute-start(bf16[64,1024]{1,0:T(8,128)(2,1)S(1)} %copy-done.26), channel_id=1, source_target_pairs={{0,32},{32,0},{64,96},{96,64},{128,160},{160,128},{192,224},{224,1... | collective-permute-start | bytes 393224 | tf_op jit(solution)/shard_map/ppermute | solution.py:460
  102.2 13.2 %collective-permute-start.11 = (bf16[64,1024]{1,0:T(8,128)(2,1)S(1)}, bf16[64,1024]{1,0:T(8,128)(2,1)S(1)}, u32[]{:S(2)}, u32[]{:S(2)}) collective-permute-start(bf16[64,1024]{1,0:T(8,128)(2,1)S(1)} %copy-done.25), channel_id=1, source_target_pairs={{0,4},{1,5},{2,6},{3,7},{4,0},{5,1},{6,2},{7,3},{8,12},{9,13},{10,... | collective-permute-start | bytes 393224 | tf_op jit(solution)/shard_map/ppermute | solution.py:457
  105.3 7.1 %collective-permute-start.9 = (bf16[32,1024]{1,0:T(8,128)(2,1)S(1)}, bf16[32,1024]{1,0:T(8,128)(2,1)S(1)}, u32[]{:S(2)}, u32[]{:S(2)}) collective-permute-start(bf16[32,1024]{1,0:T(8,128)(2,1)S(1)} %copy-done.31), channel_id=1, source_target_pairs={{0,64},{32,96},{64,0},{96,32},{128,192},{160,224},{192,128},{224,1... | collective-permute-start | bytes 196616 | tf_op jit(solution)/shard_map/ppermute | solution.py:460
  108.9 6.5 %collective-permute-start.10 = (bf16[32,1024]{1,0:T(8,128)(2,1)S(1)}, bf16[32,1024]{1,0:T(8,128)(2,1)S(1)}, u32[]{:S(2)}, u32[]{:S(2)}) collective-permute-start(bf16[32,1024]{1,0:T(8,128)(2,1)S(1)} %copy-done.30), channel_id=1, source_target_pairs={{0,96},{32,64},{64,32},{96,0},{128,224},{160,192},{192,160},{224,1... | collective-permute-start | bytes 196616 | tf_op jit(solution)/shard_map/ppermute | solution.py:460
  112.4 3.1 %copy-start.12 = (bf16[32,1024]{1,0:T(8,128)(2,1)}, bf16[32,1024]{1,0:T(8,128)(2,1)S(1)}, u32[]{:S(2)}) copy-start(bf16[32,1024]{1,0:T(8,128)(2,1)S(1)} %collective-permute-done.9.seven_a) | copy-start | bytes 196612
  115.4 0.7 copy-start.8
  115.4 0.9 copy-start.1
  119.8 13.7 %copy-start.17 = (bf16[192,1024]{1,0:T(8,128)(2,1)S(1)}, bf16[192,1024]{1,0:T(8,128)(2,1)}, u32[]{:S(2)}) copy-start(bf16[192,1024]{1,0:T(8,128)(2,1)} %get-tuple-element.50) | copy-start | bytes 1179652
  119.8 16.8 %copy-start.20 = (bf16[128,1024]{1,0:T(8,128)(2,1)S(1)}, bf16[128,1024]{1,0:T(8,128)(2,1)}, u32[]{:S(2)}) copy-start(bf16[128,1024]{1,0:T(8,128)(2,1)} %get-tuple-element.51) | copy-start | bytes 786436
  119.8 24.2 %copy-start.33 = (bf16[32,1024]{1,0:T(8,128)(2,1)S(1)}, bf16[32,1024]{1,0:T(8,128)(2,1)}, u32[]{:S(2)}) copy-start(bf16[32,1024]{1,0:T(8,128)(2,1)} %get-tuple-element.52) | copy-start | bytes 196612
  119.8 26.1 %copy-start.32 = (bf16[32,1024]{1,0:T(8,128)(2,1)S(1)}, bf16[32,1024]{1,0:T(8,128)(2,1)}, u32[]{:S(2)}) copy-start(bf16[32,1024]{1,0:T(8,128)(2,1)} %get-tuple-element.53) | copy-start | bytes 196612
  119.8 44.9 %all-to-all-start.3 = ((bf16[32,8,1024]{2,1,0:T(8,128)(2,1)}), bf16[32,8,1024]{2,1,0:T(8,128)(2,1)S(1)}, u32[]{:S(2)}, u32[]{:S(2)}) async-start(bf16[32,8,1024]{2,1,0:T(8,128)(2,1)} %bitcast.19), calls=%async_computation.3 | async-start | bytes 1048576 | tf_op jit(solution)/shard_map/all_to_all | solution.py:522
  133.5 31.2 %collective-permute-start.12 = (bf16[192,1024]{1,0:T(8,128)(2,1)S(1)}, bf16[192,1024]{1,0:T(8,128)(2,1)S(1)}, u32[]{:S(2)}, u32[]{:S(2)}) collective-permute-start(bf16[192,1024]{1,0:T(8,128)(2,1)S(1)} %copy-done.17), channel_id=1, source_target_pairs={{0,1},{1,0},{2,3},{3,2},{4,5},{5,4},{6,7},{7,6},{8,9},{9,8},{10,11... | collective-permute-start | bytes 1179656 | tf_op jit(solution)/shard_map/ppermute | solution.py:457
  136.7 20.1 %collective-permute-start.13 = (bf16[128,1024]{1,0:T(8,128)(2,1)S(1)}, bf16[128,1024]{1,0:T(8,128)(2,1)S(1)}, u32[]{:S(2)}, u32[]{:S(2)}) collective-permute-start(bf16[128,1024]{1,0:T(8,128)(2,1)S(1)} %copy-done.20), channel_id=1, source_target_pairs={{1,2},{3,4},{5,6},{7,8},{9,10},{11,12},{13,14},{15,16},{17,18},{19... | collective-permute-start | bytes 786440 | tf_op jit(solution)/shard_map/ppermute | solution.py:507
  144.0 20.7 %collective-permute-start.14 = (bf16[32,1024]{1,0:T(8,128)(2,1)S(1)}, bf16[32,1024]{1,0:T(8,128)(2,1)S(1)}, u32[]{:S(2)}, u32[]{:S(2)}) collective-permute-start(bf16[32,1024]{1,0:T(8,128)(2,1)S(1)} %copy-done.33), channel_id=1, source_target_pairs={{0,2},{1,3},{2,0},{3,1},{4,6},{5,7},{6,4},{7,5},{8,10},{9,11},{10,... | collective-permute-start | bytes 196616 | tf_op jit(solution)/shard_map/ppermute | solution.py:457
  145.9 18.7 %collective-permute-start.15 = (bf16[32,1024]{1,0:T(8,128)(2,1)S(1)}, bf16[32,1024]{1,0:T(8,128)(2,1)S(1)}, u32[]{:S(2)}, u32[]{:S(2)}) collective-permute-start(bf16[32,1024]{1,0:T(8,128)(2,1)S(1)} %copy-done.32), channel_id=1, source_target_pairs={{0,3},{1,2},{2,1},{3,0},{4,7},{5,6},{6,5},{7,4},{8,11},{9,10},{10,... | collective-permute-start | bytes 196616 | tf_op jit(solution)/shard_map/ppermute | solution.py:457
  156.8 7.9 %copy-start.6 = (bf16[128,1024]{1,0:T(8,128)(2,1)}, bf16[128,1024]{1,0:T(8,128)(2,1)S(1)}, u32[]{:S(2)}) copy-start(bf16[128,1024]{1,0:T(8,128)(2,1)S(1)} %collective-permute-done.13.oth_back) | copy-start | bytes 786436
  164.7 0.8 copy-start.5
  164.7 0.9 copy-start.2
  (6 other events, 3.9 us)

commit v3 on v2

--- a/solution.py
+++ b/solution.py
@@ -47,18 +47,6 @@
     return jnp.concatenate([column] * (width // LANES), axis=1)
 
 
-def decode_count(code):
-    lane = lax.broadcasted_iota(jnp.int32, code.shape, 1)
-    part = jnp.where(lane < LANES // 2, 8.0 * code, code)
-    return part + pltpu.roll(part, LANES // 2, 1)
-
-
-def encode_count(count):
-    lane = lax.broadcasted_iota(jnp.int32, count.shape, 1)
-    high = jnp.floor(count * 0.125)
-    return jnp.where(lane < LANES // 2, high, count - 8.0 * high)
-
-
 def local_kernel(width, peers):
     def kernel(index, mask, key, value, sib, oth, pair, gather):
         parity = index[0]
@@ -109,11 +97,9 @@
     out[pl.ds(first, rows), pl.ds(scale_width, LANES)] = count.astype(bf16)
 
 
-def load_sums(ref, first, rows, sums, counts, at, coded=False):
+def load_sums(ref, first, rows, sums, counts, at):
     width = sums.shape[0] * LANES
     count = ref[pl.ds(first, rows), pl.ds(width, LANES)].astype(f32)
-    if coded:
-        count = decode_count(count)
     counts[pl.ds(at, rows)] = count
     for tile in range(sums.shape[0]):
         mean = ref[pl.ds(first, rows), pl.ds(tile * LANES, LANES)].astype(f32)
@@ -138,7 +124,7 @@
 
 def climb_kernel(groups):
     def kernel(
-        index, sib_in, pair, pair_a, pair_b, recv, three, six, seven, wide, sums, counts
+        index, sib_in, pair, pair_a, pair_b, recv, three, six, seven, wide, shares, sums, counts
     ):
         width = sums.shape[0] * LANES
         total = recv.shape[0]
@@ -149,15 +135,19 @@
         store_means(
             seven, 0, pooled(sums, half, 2 * quarter), pooled(counts, half, 2 * quarter), width
         )
-        few = wide.shape[1]
-        step = total // few
-        count = pooled(counts, few, step)
-        inverse = by_lanes(1.0 / jnp.maximum(count, 1.0), width)
-        mean = (pooled(sums, few, step) * inverse).astype(bf16)
-        code = encode_count(count).astype(bf16)
-        for peer in range(groups):
-            wide[peer, :, pl.ds(0, width)] = mean
-            wide[peer, :, pl.ds(width, LANES)] = code
+        far_half = index[7]
+        held = wide.shape[1]
+        for side, rows in ((1 - far_half, held), (far_half, held // 2)):
+            count = pooled(counts, rows, total // rows)
+            share = 1.0 / jnp.maximum(count, 1.0)
+            mean = pooled(sums, rows, total // rows) * by_lanes(share, width)
+            if rows < held:
+                shares[pl.ds(held, rows)] = share
+                mean = jnp.concatenate([mean, jnp.zeros_like(mean)], axis=0)
+            else:
+                shares[pl.ds(0, rows)] = share
+            for i in range(groups // 2):
+                wide[side * (groups // 2) + i] = mean.astype(bf16)
         few = COARSE // 4
         for ref, first, rows, bits in (
             (pair, 0, half, 0), (sib_in, BLOCK, COARSE, 1), (pair_a, 0, half, 2), (pair_b, 0, half, 3)
@@ -221,12 +211,12 @@
         take(6 * COARSE, seven_a, 0, half)
         take(6 * COARSE + half, seven_b, 0, half)
         at = 7 * COARSE
-        keys[pl.ds(at, COARSE)] = group_in[pl.ds(quad_at, COARSE), pl.ds(0, packed)]
-        count = decode_count(group_in[pl.ds(quad_at, COARSE), pl.ds(packed, LANES)].astype(f32))
-        bias[pl.ds(at, COARSE)] = jnp.where(count > 0, 0.0, MASKED)
-        inverse[pl.ds(at, COARSE)] = 1.0 / jnp.maximum(count, 1.0)
-        load_sums(group_in, half_group_at, 2 * COARSE, sums, counts, 0, coded=True)
-        take_pooled(8 * COARSE)
+        keys[pl.ds(at, COARSE)] = group_in[pl.ds(quad_at, COARSE)]
+        nine = group_in[pl.ds(half_group_at, 2 * COARSE)].astype(f32)
+        nine = nine.reshape(8, 2 * COARSE // 8, packed)[:, : COARSE // 8].reshape(COARSE, packed)
+        keys[pl.ds(at + COARSE, COARSE)] = nine.astype(bf16)
+        bias[pl.ds(at, 2 * COARSE)] = jnp.zeros((2 * COARSE, LANES), f32)
+        inverse[pl.ds(at, 2 * COARSE)] = jnp.ones((2 * COARSE, LANES), f32)
         take(far_rows, sib, 0, BLOCK)
         take(far_rows + BLOCK, oth, 0, BLOCK)
         take(main_rows, sib_in, 0, BLOCK)
@@ -242,8 +232,8 @@
         halo_segments = [(at, 64) for at in range(0, BLOCK, 64)]
 
         def one_head(head):
-            key_cols = pl.ds(pl.multiple_of(head * HEAD_DIM, HEAD_DIM), HEAD_DIM)
-            value_cols = pl.ds(pl.multiple_of(width + head * HEAD_DIM, HEAD_DIM), HEAD_DIM)
+            key_cols = pl.ds(head * HEAD_DIM, HEAD_DIM)
+            value_cols = pl.ds(width + head * HEAD_DIM, HEAD_DIM)
             q = jnp.concatenate([query[r, key_cols] for r in own_rows], axis=0)
             c = jnp.concatenate([cot[r, key_cols] for r in own_rows], axis=0)
 
@@ -340,16 +330,14 @@
                         near = near * factor
                     out_ref[:, cols] = near.astype(bf16)
 
-        def step(head, carry):
+        for head in range(HEADS):
             one_head(head)
-            return carry
-
-        lax.fori_loop(0, HEADS, step, 0)
         group_out[...] = jnp.zeros_like(group_out)
         for tile in range(sums.shape[0]):
             cols = pl.ds(tile * LANES, LANES)
             group_out[pl.ds(quad_at, COARSE), cols] = sums[tile, pl.ds(0, COARSE)].astype(bf16)
-            wide = widen(sums[tile, pl.ds(COARSE, COARSE)], 2)
+            nine = sums[tile, pl.ds(COARSE, COARSE)].reshape(8, COARSE // 8, LANES)
+            wide = jnp.concatenate([nine, jnp.zeros_like(nine)], axis=1).reshape(2 * COARSE, LANES)
             group_out[pl.ds(half_group_at, 2 * COARSE), cols] = wide.astype(bf16)
 
     scratch = [
@@ -377,16 +365,19 @@
 
 
 def back_kernel(
-    index, part, six, seven_a, seven_b, group, three, low, sib_grad,
+    index, part, six, seven_a, seven_b, group, shares, three, low, sib_grad,
     out, sib_out, pair_a, pair_b, mine, acc,
 ):
     octet, half_shard = index[4], index[5]
     tile = six[...].astype(f32) + widen(seven_a[...].astype(f32) + seven_b[...].astype(f32), 2)
     few = COARSE // 4
-    total = group[pl.ds(0, few)].astype(f32)
-    for i in range(1, group.shape[0] // few):
-        total = total + group[pl.ds(i * few, few)].astype(f32)
-    tile = tile + widen(total, 4)
+    quad_at = pl.multiple_of(index[6] * COARSE, COARSE)
+    half_at = pl.multiple_of(index[7] * 2 * COARSE, 2 * COARSE)
+    eight = jnp.sum(group[pl.ds(quad_at, COARSE)].astype(f32).reshape(4, few, -1), axis=0)
+    nine = group[pl.ds(half_at, 2 * COARSE)].astype(f32).reshape(8, few, -1)[:, : few // 2]
+    nine = jnp.sum(nine, axis=0)
+    share = by_lanes(shares[...], tile.shape[1])
+    tile = tile + widen(eight * share[:few], 4) + widen(nine * share[few : few + few // 2], 8)
     acc[...] = widen(tile, out.shape[0] // COARSE)
     octet_at = pl.ds(pl.multiple_of(octet * COARSE, COARSE), COARSE)
     half_at = pl.ds(pl.multiple_of(half_shard * 2 * COARSE, 2 * COARSE), 2 * COARSE)
@@ -474,11 +465,12 @@
     pair_b = on_shard(pair, 3)
     oth_in = lax.ppermute(oth, ("grp", "shard"), pairs)
     shard_in = lax.all_to_all(gather, "shard", 0, 0, tiled=True).reshape(shards * few_shard, row)
-    three, six, seven, wide = call(
+    three, six, seven, wide, shares = call(
         climb_kernel(groups),
         [
             shape(COARSE, row), shape(COARSE, row), shape(half, row),
-            jax.ShapeDtypeStruct((groups, few_group, row), bf16),
+            jax.ShapeDtypeStruct((groups, few_group, packed), bf16),
+            shape(few_group + few_group // 2, LANES, f32),
         ],
         [
             pltpu.VMEM((packed // LANES, shards * few_shard, LANES), f32),
@@ -490,7 +482,7 @@
     seven_a = on_group(seven, 2)
     seven_b = on_group(seven, 3)
     three_in = on_shard(three, 4)
-    group_in = lax.all_to_all(wide, "grp", 0, 0, tiled=True).reshape(groups * few_group, row)
+    group_in = lax.all_to_all(wide, "grp", 0, 0, tiled=True).reshape(groups * few_group, packed)
     kernel, outs, scratch = attention_kernel(width, shards * few_shard, groups * few_group)
     (
         attended, query_grad, own_grad, sib_grad, oth_grad, low_grad, three_out, shard_part,
@@ -506,6 +498,7 @@
     three_back = on_shard(three_out, 4)
     oth_back = lax.ppermute(oth_grad, ("grp", "shard"), pairs)
     group_back = lax.all_to_all(group_out, "grp", 0, 0, tiled=True)
+    oth_back, group_back = lax.optimization_barrier((oth_back, group_back))
     shard_out, sib_out, pair_a_out, pair_b_out, mine = call(
         back_kernel,
         [
@@ -513,7 +506,7 @@
             shape(half, packed), shape(half, packed), shape(few_group, packed, f32),
         ],
         [pltpu.VMEM((shards * few_shard, packed), f32)],
-        index, shard_part, six_back, seven_a_back, seven_b_back, group_back, three_back,
+        index, shard_part, six_back, seven_a_back, seven_b_back, group_back, shares, three_back,
         low_grad, sib_grad, name="back",
     )
     sib_back = on_shard(sib_out, 1)

time: 170 us -> 166 us (0.976)
  waiting for transfers between devices: 47.5 us -> 45 us
    ppermute x1, waiting for transfers between devices: 8.92 us -> 0.01 us  [body(): oth_back = lax.ppermute(oth_grad, ('grp', 'shard'), pairs)]
    ppermute x8, waiting for transfers between devices: 23.9 us -> 30.9 us  [on_shard(): return lax.ppermute(x, 'shard', flip(shards, bits))]
    all_to_all x1, waiting for transfers between devices: 0.01 us -> 4.95 us  [body(): group_back = lax.all_to_all(group_out, 'grp', 0, 0, tiled=True)]
    ppermute x6, waiting for transfers between devices: 7.79 us -> 3.68 us  [on_group(): return lax.ppermute(x, 'grp', flip(groups, bits))]
    ppermute x1, starting transfers between devices: 7.33 us -> 4.82 us  [body(): oth_back = lax.ppermute(oth_grad, ('grp', 'shard'), pairs)]
where the time goes in v3:
time: 166 us; the launch traced here: 165 us
  starting transfers between devices  92.7 us (56%)
  waiting for transfers between devices  45 us (27%)
  Pallas kernels  22.1 us (13%)
  local copies, waits for them, and re-layouts  4.3 us (3%)
    ppermute x8, waiting for transfers between devices, on_shard(): return lax.ppermute(x, 'shard', flip(shards, bits))  30.9 us
    ppermute x8, starting transfers between devices, on_shard(): return lax.ppermute(x, 'shard', flip(shards, bits))  22.2 us
    pallas_call x5, Pallas kernels, call(): pl.pallas_call(kernel, out_shape=outs, in_specs=in_specs, out_specs=[pl.B...  22.1 us
    ppermute x6, starting transfers between devices, on_group(): return lax.ppermute(x, 'grp', flip(groups, bits))  15.6 us
    all_to_all x1, starting transfers between devices, body(): shard_back = lax.all_to_all(shard_out, 'shard', 0, 0, tiled=True)  14.3 us
    all_to_all x1, starting transfers between devices, body(): lax.all_to_all(gather, 'shard', 0, 0, tiled=True)  13.6 us
    all_to_all x1, starting transfers between devices, body(): lax.all_to_all(wide, 'grp', 0, 0, tiled=True)  11.9 us
    all_to_all x1, waiting for transfers between devices, body(): lax.all_to_all(wide, 'grp', 0, 0, tiled=True)  5.3 us
  transfers between devices with their start and end apart: 20, of which 8 were waited for; matrix products, arithmetic and copies ran while one was open for 0% of the time, Pallas kernels for 0%

profile of v3, /device:TPU:1, one launch (start us, length us, event | category | flops | bytes accessed | tf_op | source)
XLA Modules:
  0.0 165.3 jit_solution(18330227274343501262)
XLA Ops:
  0.6 0.7 stack.35.index
  1.3 2.5 %local.1 = (bf16[192,1152]{1,0:T(8,128)(2,1)}, bf16[128,1152]{1,0:T(8,128)(2,1)}, bf16[32,1152]{1,0:T(8,128)(2,1)}, bf16[32,8,1152]{2,1,0:T(8,128)(2,1)}) custom-call(s32[8]{0:T(128)} %stack.35.index, s32[1,256]{1,0:T(1,128)} %bitcast.20, bf16[256,512]{1,0:T(8,128)(2,1)} %key.1, bf16[256,512]{1,0:T(8,128)(2,1)} %value.1), custom_call_target="tpu_custom_call" | custom-call | bytes 1926144 | tf_op jit(solution)/shard_map/local/pallas_call | solution.py:30
  3.8 13.6 %all-to-all-start = ((bf16[32,8,1152]{2,1,0:T(8,128)(2,1)}), bf16[32,8,1152]{2,1,0:T(8,128)(2,1)S(1)}, u32[]{:S(2)}, u32[]{:S(2)}) async-start(bf16[32,8,1152]{2,1,0:T(8,128)(2,1)} %get-tuple-element.37), calls=%async_computation | async-start | bytes 1179648 | tf_op jit(solution)/shard_map/all_to_all | solution.py:467
  17.4 3.1 %collective-permute-start = (bf16[192,1152]{1,0:T(8,128)(2,1)S(1)}, bf16[192,1152]{1,0:T(8,128)(2,1)S(1)}, u32[]{:S(2)}, u32[]{:S(2)}) collective-permute-start(bf16[192,1152]{1,0:T(8,128)(2,1)S(1)} %copy-done.16), channel_id=1, source_target_pairs={{0,1},{1,0},{2,3},{3,2},{4,5},{5,4},{6,7},{7,6},{8,9},{9,8},{10,11... | collective-permute-start | bytes 1327112 | tf_op jit(solution)/shard_map/ppermute | solution.py:448
  20.6 4.0 %collective-permute-start.3 = (bf16[32,1152]{1,0:T(8,128)(2,1)S(1)}, bf16[32,1152]{1,0:T(8,128)(2,1)S(1)}, u32[]{:S(2)}, u32[]{:S(2)}) collective-permute-start(bf16[32,1152]{1,0:T(8,128)(2,1)S(1)} %copy-done.11), channel_id=1, source_target_pairs={{0,3},{1,2},{2,1},{3,0},{4,7},{5,6},{6,5},{7,4},{8,11},{9,10},{10,... | collective-permute-start | bytes 221192 | tf_op jit(solution)/shard_map/ppermute | solution.py:448
  24.6 1.9 %collective-permute-start.2 = (bf16[32,1152]{1,0:T(8,128)(2,1)S(1)}, bf16[32,1152]{1,0:T(8,128)(2,1)S(1)}, u32[]{:S(2)}, u32[]{:S(2)}) collective-permute-start(bf16[32,1152]{1,0:T(8,128)(2,1)S(1)} %copy-done.11), channel_id=1, source_target_pairs={{0,2},{1,3},{2,0},{3,1},{4,6},{5,7},{6,4},{7,5},{8,10},{9,11},{10,... | collective-permute-start | bytes 221192 | tf_op jit(solution)/shard_map/ppermute | solution.py:448
  26.5 16.0 %collective-permute-done.3.pair_b = bf16[32,1152]{1,0:T(8,128)(2,1)S(1)} collective-permute-done((bf16[32,1152]{1,0:T(8,128)(2,1)S(1)}, bf16[32,1152]{1,0:T(8,128)(2,1)S(1)}, u32[]{:S(2)}, u32[]{:S(2)}) %collective-permute-start.3) | collective-permute-done | bytes 73760 | tf_op jit(solution)/shard_map/ppermute | solution.py:448
  42.5 0.6 copy-done.9
  43.1 0.0 copy-done.10
  43.2 0.2 copy-done.4
  43.3 0.2 copy-done
  43.5 3.4 %climb.1 = (bf16[64,1152]{1,0:T(8,128)(2,1)}, bf16[64,1152]{1,0:T(8,128)(2,1)}, bf16[32,1152]{1,0:T(8,128)(2,1)}, bf16[16,16,1024]{2,1,0:T(8,128)(2,1)}, f32[24,128]{1,0:T(8,128)}) custom-call(s32[8]{0:T(128)} %stack.35.index, bf16[192,1152]{1,0:T(8,128)(2,1)} %copy-done.4, bf16[32,1152]{1,0:T(8,128)(2,1)} %get-tuple-element.36.pair, ...), custom_call_target="tpu_custom_call" | custom-call | bytes 2158592 | tf_op jit(solution)/shard_map/climb/pallas_call | solution.py:30
  46.9 0.0 copy-start.29
  46.9 11.9 %all-to-all-start.1 = ((bf16[16,16,1024]{2,1,0:T(8,128)(2,1)}), bf16[16,16,1024]{2,1,0:T(8,128)(2,1)S(1)}, u32[]{:S(2)}, u32[]{:S(2)}) async-start(bf16[16,16,1024]{2,1,0:T(8,128)(2,1)} %get-tuple-element.41), calls=%async_computation.1 | async-start | bytes 1048576 | tf_op jit(solution)/shard_map/all_to_all | solution.py:485
  58.8 5.2 %collective-permute-start.1 = (bf16[128,1152]{1,0:T(8,128)(2,1)S(1)}, bf16[128,1152]{1,0:T(8,128)(2,1)S(1)}, u32[]{:S(2)}, u32[]{:S(2)}) collective-permute-start(bf16[128,1152]{1,0:T(8,128)(2,1)S(1)} %copy-done.18), channel_id=1, source_target_pairs={{1,2},{3,4},{5,6},{7,8},{9,10},{11,12},{13,14},{15,16},{17,18},{19... | collective-permute-start | bytes 884744 | tf_op jit(solution)/shard_map/ppermute | solution.py:466
  64.0 1.9 %collective-permute-start.4 = (bf16[64,1152]{1,0:T(8,128)(2,1)S(1)}, bf16[64,1152]{1,0:T(8,128)(2,1)S(1)}, u32[]{:S(2)}, u32[]{:S(2)}) collective-permute-start(bf16[64,1152]{1,0:T(8,128)(2,1)S(1)} %copy-done.24), channel_id=1, source_target_pairs={{0,4},{1,5},{2,6},{3,7},{4,0},{5,1},{6,2},{7,3},{8,12},{9,13},{10,... | collective-permute-start | bytes 442376 | tf_op jit(solution)/shard_map/ppermute | solution.py:448
  66.0 1.9 %collective-permute-start.5 = (bf16[64,1152]{1,0:T(8,128)(2,1)S(1)}, bf16[64,1152]{1,0:T(8,128)(2,1)S(1)}, u32[]{:S(2)}, u32[]{:S(2)}) collective-permute-start(bf16[64,1152]{1,0:T(8,128)(2,1)S(1)} %copy-done.23), channel_id=1, source_target_pairs={{0,32},{32,0},{64,96},{96,64},{128,160},{160,128},{192,224},{224,1... | collective-permute-start | bytes 442376 | tf_op jit(solution)/shard_map/ppermute | solution.py:451
  67.9 3.9 %collective-permute-start.7 = (bf16[32,1152]{1,0:T(8,128)(2,1)S(1)}, bf16[32,1152]{1,0:T(8,128)(2,1)S(1)}, u32[]{:S(2)}, u32[]{:S(2)}) collective-permute-start(bf16[32,1152]{1,0:T(8,128)(2,1)S(1)} %copy-done.29), channel_id=1, source_target_pairs={{0,96},{32,64},{64,32},{96,0},{128,224},{160,192},{192,160},{224,1... | collective-permute-start | bytes 221192 | tf_op jit(solution)/shard_map/ppermute | solution.py:451
  71.8 1.9 %collective-permute-start.6 = (bf16[32,1152]{1,0:T(8,128)(2,1)S(1)}, bf16[32,1152]{1,0:T(8,128)(2,1)S(1)}, u32[]{:S(2)}, u32[]{:S(2)}) collective-permute-start(bf16[32,1152]{1,0:T(8,128)(2,1)S(1)} %copy-done.29), channel_id=1, source_target_pairs={{0,64},{32,96},{64,0},{96,32},{128,192},{160,224},{192,128},{224,1... | collective-permute-start | bytes 221192 | tf_op jit(solution)/shard_map/ppermute | solution.py:451
  73.8 0.2 collective-permute-done.1.oth_in
  74.0 0.8 collective-permute-done.7.seven_b
  74.7 2.9 %collective-permute-done.6.seven_a = bf16[32,1152]{1,0:T(8,128)(2,1)S(1)} collective-permute-done((bf16[32,1152]{1,0:T(8,128)(2,1)S(1)}, bf16[32,1152]{1,0:T(8,128)(2,1)S(1)}, u32[]{:S(2)}, u32[]{:S(2)}) %collective-permute-start.6) | collective-permute-done | bytes 73760 | tf_op jit(solution)/shard_map/ppermute | solution.py:451
  77.7 5.3 %all-to-all-done.1 = bf16[16,16,1024]{2,1,0:T(8,128)(2,1)S(1)} async-done(((bf16[16,16,1024]{2,1,0:T(8,128)(2,1)}), bf16[16,16,1024]{2,1,0:T(8,128)(2,1)S(1)}, u32[]{:S(2)}, u32[]{:S(2)}) %all-to-all-start.1) | async-done | bytes 524320 | tf_op jit(solution)/shard_map/all_to_all | solution.py:485
  83.0 0.8 copy-done.3
  83.7 9.6 %attention.1 = (bf16[256,512]{1,0:T(8,128)(2,1)}, bf16[256,512]{1,0:T(8,128)(2,1)}, f32[256,1024]{1,0:T(8,128)}, bf16[128,1024]{1,0:T(8,128)(2,1)}, bf16[128,102...) custom-call(s32[8]{0:T(128)} %stack.35.index, ...), custom_call_target="tpu_custom_call" | custom-call | flops 1600000000 | bytes 7766016 | tf_op jit(solution)/shard_map/attention/pallas_call | solution.py:30
  93.4 5.2 %all-to-all-start.2 = ((bf16[16,16,1024]{2,1,0:T(8,128)(2,1)}), bf16[16,16,1024]{2,1,0:T(8,128)(2,1)S(1)}, u32[]{:S(2)}, u32[]{:S(2)}) async-start(bf16[16,16,1024]{2,1,0:T(8,128)(2,1)} %bitcast.18), calls=%async_computation.2 | async-start | bytes 1048576 | tf_op jit(solution)/shard_map/all_to_all | solution.py:500
  98.6 4.8 %collective-permute-start.11 = (bf16[128,1024]{1,0:T(8,128)(2,1)S(1)}, bf16[128,1024]{1,0:T(8,128)(2,1)S(1)}, u32[]{:S(2)}, u32[]{:S(2)}) collective-permute-start(bf16[128,1024]{1,0:T(8,128)(2,1)S(1)} %copy-done.20), channel_id=1, source_target_pairs={{1,2},{3,4},{5,6},{7,8},{9,10},{11,12},{13,14},{15,16},{17,18},{19... | collective-permute-start | bytes 786440 | tf_op jit(solution)/shard_map/ppermute | solution.py:499
  103.4 1.9 %collective-permute-start.8 = (bf16[64,1024]{1,0:T(8,128)(2,1)S(1)}, bf16[64,1024]{1,0:T(8,128)(2,1)S(1)}, u32[]{:S(2)}, u32[]{:S(2)}) collective-permute-start(bf16[64,1024]{1,0:T(8,128)(2,1)S(1)} %copy-done.26), channel_id=1, source_target_pairs={{0,32},{32,0},{64,96},{96,64},{128,160},{160,128},{192,224},{224,1... | collective-permute-start | bytes 393224 | tf_op jit(solution)/shard_map/ppermute | solution.py:451
  105.4 1.9 %collective-permute-start.12 = (bf16[64,1024]{1,0:T(8,128)(2,1)S(1)}, bf16[64,1024]{1,0:T(8,128)(2,1)S(1)}, u32[]{:S(2)}, u32[]{:S(2)}) collective-permute-start(bf16[64,1024]{1,0:T(8,128)(2,1)S(1)} %copy-done.25), channel_id=1, source_target_pairs={{0,4},{1,5},{2,6},{3,7},{4,0},{5,1},{6,2},{7,3},{8,12},{9,13},{10,... | collective-permute-start | bytes 393224 | tf_op jit(solution)/shard_map/ppermute | solution.py:448
  107.3 3.5 %collective-permute-start.9 = (bf16[32,1024]{1,0:T(8,128)(2,1)S(1)}, bf16[32,1024]{1,0:T(8,128)(2,1)S(1)}, u32[]{:S(2)}, u32[]{:S(2)}) collective-permute-start(bf16[32,1024]{1,0:T(8,128)(2,1)S(1)} %copy-done.31), channel_id=1, source_target_pairs={{0,64},{32,96},{64,0},{96,32},{128,192},{160,224},{192,128},{224,1... | collective-permute-start | bytes 196616 | tf_op jit(solution)/shard_map/ppermute | solution.py:451
  110.9 2.4 %collective-permute-start.10 = (bf16[32,1024]{1,0:T(8,128)(2,1)S(1)}, bf16[32,1024]{1,0:T(8,128)(2,1)S(1)}, u32[]{:S(2)}, u32[]{:S(2)}) collective-permute-start(bf16[32,1024]{1,0:T(8,128)(2,1)S(1)} %copy-done.30), channel_id=1, source_target_pairs={{0,96},{32,64},{64,32},{96,0},{128,224},{160,192},{192,160},{224,1... | collective-permute-start | bytes 196616 | tf_op jit(solution)/shard_map/ppermute | solution.py:451
  113.3 4.9 %all-to-all-done.2 = bf16[16,16,1024]{2,1,0:T(8,128)(2,1)S(1)} async-done(((bf16[16,16,1024]{2,1,0:T(8,128)(2,1)}), bf16[16,16,1024]{2,1,0:T(8,128)(2,1)S(1)}, u32[]{:S(2)}, u32[]{:S(2)}) %all-to-all-start.2) | async-done | bytes 524320 | tf_op jit(solution)/shard_map/all_to_all | solution.py:500
  118.3 0.7 copy-done.1
  119.0 0.0 copy-done.12
  119.1 0.0 copy-done.13
  119.1 0.0 copy-done.7
  119.1 0.0 copy-done.8
  119.1 3.4 %back.1 = (bf16[256,1024]{1,0:T(8,128)(2,1)}, bf16[192,1024]{1,0:T(8,128)(2,1)}, bf16[32,1024]{1,0:T(8,128)(2,1)}, bf16[32,1024]{1,0:T(8,128)(2,1)}, f32[16,1024]{1,0:T(8,128)}) custom-call(s32[8]{0:T(128)} %stack.35.index, f32[128,1024]{1,0:T(8,128)} %get-tuple-element.45.part, bf16[64,1024]{1,0:T(8,128)(2,1)} %copy-done.7, bf16[32,1024]{1,0:T(8,128)(2,1)} %copy-done.12, ...), custom_call_target="tpu_custom_call" | custom-call | bytes 3354624 | tf_op jit(solution)/shard_map/back/pallas_call | solution.py:30
  122.6 14.3 %all-to-all-start.3 = ((bf16[32,8,1024]{2,1,0:T(8,128)(2,1)}), bf16[32,8,1024]{2,1,0:T(8,128)(2,1)S(1)}, u32[]{:S(2)}, u32[]{:S(2)}) async-start(bf16[32,8,1024]{2,1,0:T(8,128)(2,1)} %bitcast.19), calls=%async_computation.3 | async-start | bytes 1048576 | tf_op jit(solution)/shard_map/all_to_all | solution.py:515
  136.9 3.1 %collective-permute-start.13 = (bf16[192,1024]{1,0:T(8,128)(2,1)S(1)}, bf16[192,1024]{1,0:T(8,128)(2,1)S(1)}, u32[]{:S(2)}, u32[]{:S(2)}) collective-permute-start(bf16[192,1024]{1,0:T(8,128)(2,1)S(1)} %copy-done.17), channel_id=1, source_target_pairs={{0,1},{1,0},{2,3},{3,2},{4,5},{5,4},{6,7},{7,6},{8,9},{9,8},{10,11... | collective-permute-start | bytes 1179656 | tf_op jit(solution)/shard_map/ppermute | solution.py:448
  140.1 4.0 %collective-permute-start.14 = (bf16[32,1024]{1,0:T(8,128)(2,1)S(1)}, bf16[32,1024]{1,0:T(8,128)(2,1)S(1)}, u32[]{:S(2)}, u32[]{:S(2)}) collective-permute-start(bf16[32,1024]{1,0:T(8,128)(2,1)S(1)} %copy-done.33), channel_id=1, source_target_pairs={{0,2},{1,3},{2,0},{3,1},{4,6},{5,7},{6,4},{7,5},{8,10},{9,11},{10,... | collective-permute-start | bytes 196616 | tf_op jit(solution)/shard_map/ppermute | solution.py:448
  144.1 2.1 %collective-permute-start.15 = (bf16[32,1024]{1,0:T(8,128)(2,1)S(1)}, bf16[32,1024]{1,0:T(8,128)(2,1)S(1)}, u32[]{:S(2)}, u32[]{:S(2)}) collective-permute-start(bf16[32,1024]{1,0:T(8,128)(2,1)S(1)} %copy-done.32), channel_id=1, source_target_pairs={{0,3},{1,2},{2,1},{3,0},{4,7},{5,6},{6,5},{7,4},{8,11},{9,10},{10,... | collective-permute-start | bytes 196616 | tf_op jit(solution)/shard_map/ppermute | solution.py:448
  146.2 10.1 %collective-permute-done.14.pair_a = bf16[32,1024]{1,0:T(8,128)(2,1)S(1)} collective-permute-done((bf16[32,1024]{1,0:T(8,128)(2,1)S(1)}, bf16[32,1024]{1,0:T(8,128)(2,1)S(1)}, u32[]{:S(2)}, u32[]{:S(2)}) %collective-permute-start.14) | collective-permute-done | bytes 65568 | tf_op jit(solution)/shard_map/ppermute | solution.py:448
  156.3 4.8 %collective-permute-done.15.pair_b = bf16[32,1024]{1,0:T(8,128)(2,1)S(1)} collective-permute-done((bf16[32,1024]{1,0:T(8,128)(2,1)S(1)}, bf16[32,1024]{1,0:T(8,128)(2,1)S(1)}, u32[]{:S(2)}, u32[]{:S(2)}) %collective-permute-start.15) | collective-permute-done | bytes 65568 | tf_op jit(solution)/shard_map/ppermute | solution.py:448
  161.1 0.6 copy-done.15
  161.7 0.2 copy-done.5
  161.9 0.2 copy-done.2
  162.1 3.2 %final.1 = (bf16[256,512]{1,0:T(8,128)(2,1)}, bf16[256,512]{1,0:T(8,128)(2,1)}) custom-call(s32[8]{0:T(128)} %stack.35.index, s32[1,256]{1,0:T(1,128)} %bitcast.21, f32[256,1024]{1,0:T(8,128)} %get-tuple-element.44.own, bf16[192,1024]{1,0:T(8,128)(2,1)} %copy-done.5, bf16[128,1024]{1,0:T(8,128)(2,1)} %copy-done.6, bf16[32,1024]{1,0:T(8,128)(2,1)} %copy-done.14, ...), custom_call_target="tpu_custom_call" | custom-call | bytes 2950144 | tf_op jit(solution)/shard_map/final/pallas_call | solution.py:30
  (66 shorter events, 0.1 us)
Async XLA Ops:
  3.8 13.6 %copy-start.16 = (bf16[192,1152]{1,0:T(8,128)(2,1)S(1)}, bf16[192,1152]{1,0:T(8,128)(2,1)}, u32[]{:S(2)}) copy-start(bf16[192,1152]{1,0:T(8,128)(2,1)} %get-tuple-element.34.sib) | copy-start | bytes 1327108
  3.8 16.8 %copy-start.11 = (bf16[32,1152]{1,0:T(8,128)(2,1)S(1)}, bf16[32,1152]{1,0:T(8,128)(2,1)}, u32[]{:S(2)}) copy-start(bf16[32,1152]{1,0:T(8,128)(2,1)} %get-tuple-element.36.pair) | copy-start | bytes 221188
  3.8 38.7 %all-to-all-start = ((bf16[32,8,1152]{2,1,0:T(8,128)(2,1)}), bf16[32,8,1152]{2,1,0:T(8,128)(2,1)S(1)}, u32[]{:S(2)}, u32[]{:S(2)}) async-start(bf16[32,8,1152]{2,1,0:T(8,128)(2,1)} %get-tuple-element.37), calls=%async_computation | async-start | bytes 1179648 | tf_op jit(solution)/shard_map/all_to_all | solution.py:467
  17.4 25.1 %collective-permute-start = (bf16[192,1152]{1,0:T(8,128)(2,1)S(1)}, bf16[192,1152]{1,0:T(8,128)(2,1)S(1)}, u32[]{:S(2)}, u32[]{:S(2)}) collective-permute-start(bf16[192,1152]{1,0:T(8,128)(2,1)S(1)} %copy-done.16), channel_id=1, source_target_pairs={{0,1},{1,0},{2,3},{3,2},{4,5},{5,4},{6,7},{7,6},{8,9},{9,8},{10,11... | collective-permute-start | bytes 1327112 | tf_op jit(solution)/shard_map/ppermute | solution.py:448
  20.6 21.9 %collective-permute-start.3 = (bf16[32,1152]{1,0:T(8,128)(2,1)S(1)}, bf16[32,1152]{1,0:T(8,128)(2,1)S(1)}, u32[]{:S(2)}, u32[]{:S(2)}) collective-permute-start(bf16[32,1152]{1,0:T(8,128)(2,1)S(1)} %copy-done.11), channel_id=1, source_target_pairs={{0,3},{1,2},{2,1},{3,0},{4,7},{5,6},{6,5},{7,4},{8,11},{9,10},{10,... | collective-permute-start | bytes 221192 | tf_op jit(solution)/shard_map/ppermute | solution.py:448
  24.6 17.9 %collective-permute-start.2 = (bf16[32,1152]{1,0:T(8,128)(2,1)S(1)}, bf16[32,1152]{1,0:T(8,128)(2,1)S(1)}, u32[]{:S(2)}, u32[]{:S(2)}) collective-permute-start(bf16[32,1152]{1,0:T(8,128)(2,1)S(1)} %copy-done.11), channel_id=1, source_target_pairs={{0,2},{1,3},{2,0},{3,1},{4,6},{5,7},{6,4},{7,5},{8,10},{9,11},{10,... | collective-permute-start | bytes 221192 | tf_op jit(solution)/shard_map/ppermute | solution.py:448
  42.5 0.8 copy-start.4
  42.5 1.0 copy-start
  46.9 11.9 %copy-start.18 = (bf16[128,1152]{1,0:T(8,128)(2,1)S(1)}, bf16[128,1152]{1,0:T(8,128)(2,1)}, u32[]{:S(2)}) copy-start(bf16[128,1152]{1,0:T(8,128)(2,1)} %get-tuple-element.35.oth) | copy-start | bytes 884740
  46.9 17.1 %copy-start.24 = (bf16[64,1152]{1,0:T(8,128)(2,1)S(1)}, bf16[64,1152]{1,0:T(8,128)(2,1)}, u32[]{:S(2)}) copy-start(bf16[64,1152]{1,0:T(8,128)(2,1)} %get-tuple-element.38) | copy-start | bytes 442372
  46.9 19.0 %copy-start.23 = (bf16[64,1152]{1,0:T(8,128)(2,1)S(1)}, bf16[64,1152]{1,0:T(8,128)(2,1)}, u32[]{:S(2)}) copy-start(bf16[64,1152]{1,0:T(8,128)(2,1)} %get-tuple-element.39) | copy-start | bytes 442372
  46.9 21.0 %copy-start.29 = (bf16[32,1152]{1,0:T(8,128)(2,1)S(1)}, bf16[32,1152]{1,0:T(8,128)(2,1)}, u32[]{:S(2)}) copy-start(bf16[32,1152]{1,0:T(8,128)(2,1)} %get-tuple-element.40) | copy-start | bytes 221188
  46.9 36.0 %all-to-all-start.1 = ((bf16[16,16,1024]{2,1,0:T(8,128)(2,1)}), bf16[16,16,1024]{2,1,0:T(8,128)(2,1)S(1)}, u32[]{:S(2)}, u32[]{:S(2)}) async-start(bf16[16,16,1024]{2,1,0:T(8,128)(2,1)} %get-tuple-element.41), calls=%async_computation.1 | async-start | bytes 1048576 | tf_op jit(solution)/shard_map/all_to_all | solution.py:485
  58.8 15.1 %collective-permute-start.1 = (bf16[128,1152]{1,0:T(8,128)(2,1)S(1)}, bf16[128,1152]{1,0:T(8,128)(2,1)S(1)}, u32[]{:S(2)}, u32[]{:S(2)}) collective-permute-start(bf16[128,1152]{1,0:T(8,128)(2,1)S(1)} %copy-done.18), channel_id=1, source_target_pairs={{1,2},{3,4},{5,6},{7,8},{9,10},{11,12},{13,14},{15,16},{17,18},{19... | collective-permute-start | bytes 884744 | tf_op jit(solution)/shard_map/ppermute | solution.py:466
  64.0 13.6 %collective-permute-start.4 = (bf16[64,1152]{1,0:T(8,128)(2,1)S(1)}, bf16[64,1152]{1,0:T(8,128)(2,1)S(1)}, u32[]{:S(2)}, u32[]{:S(2)}) collective-permute-start(bf16[64,1152]{1,0:T(8,128)(2,1)S(1)} %copy-done.24), channel_id=1, source_target_pairs={{0,4},{1,5},{2,6},{3,7},{4,0},{5,1},{6,2},{7,3},{8,12},{9,13},{10,... | collective-permute-start | bytes 442376 | tf_op jit(solution)/shard_map/ppermute | solution.py:448
  66.0 11.7 %collective-permute-start.5 = (bf16[64,1152]{1,0:T(8,128)(2,1)S(1)}, bf16[64,1152]{1,0:T(8,128)(2,1)S(1)}, u32[]{:S(2)}, u32[]{:S(2)}) collective-permute-start(bf16[64,1152]{1,0:T(8,128)(2,1)S(1)} %copy-done.23), channel_id=1, source_target_pairs={{0,32},{32,0},{64,96},{96,64},{128,160},{160,128},{192,224},{224,1... | collective-permute-start | bytes 442376 | tf_op jit(solution)/shard_map/ppermute | solution.py:451
  67.9 6.8 %collective-permute-start.7 = (bf16[32,1152]{1,0:T(8,128)(2,1)S(1)}, bf16[32,1152]{1,0:T(8,128)(2,1)S(1)}, u32[]{:S(2)}, u32[]{:S(2)}) collective-permute-start(bf16[32,1152]{1,0:T(8,128)(2,1)S(1)} %copy-done.29), channel_id=1, source_target_pairs={{0,96},{32,64},{64,32},{96,0},{128,224},{160,192},{192,160},{224,1... | collective-permute-start | bytes 221192 | tf_op jit(solution)/shard_map/ppermute | solution.py:451
  71.8 5.8 %collective-permute-start.6 = (bf16[32,1152]{1,0:T(8,128)(2,1)S(1)}, bf16[32,1152]{1,0:T(8,128)(2,1)S(1)}, u32[]{:S(2)}, u32[]{:S(2)}) collective-permute-start(bf16[32,1152]{1,0:T(8,128)(2,1)S(1)} %copy-done.29), channel_id=1, source_target_pairs={{0,64},{32,96},{64,0},{96,32},{128,192},{160,224},{192,128},{224,1... | collective-permute-start | bytes 221192 | tf_op jit(solution)/shard_map/ppermute | solution.py:451
  74.0 9.0 %copy-start.19 = (bf16[128,1152]{1,0:T(8,128)(2,1)}, bf16[128,1152]{1,0:T(8,128)(2,1)S(1)}, u32[]{:S(2)}) copy-start(bf16[128,1152]{1,0:T(8,128)(2,1)S(1)} %collective-permute-done.1.oth_in) | copy-start | bytes 884740
  74.7 8.2 %copy-start.27 = (bf16[32,1152]{1,0:T(8,128)(2,1)}, bf16[32,1152]{1,0:T(8,128)(2,1)S(1)}, u32[]{:S(2)}) copy-start(bf16[32,1152]{1,0:T(8,128)(2,1)S(1)} %collective-permute-done.7.seven_b) | copy-start | bytes 221188
  77.6 5.3 %copy-start.28 = (bf16[32,1152]{1,0:T(8,128)(2,1)}, bf16[32,1152]{1,0:T(8,128)(2,1)S(1)}, u32[]{:S(2)}) copy-start(bf16[32,1152]{1,0:T(8,128)(2,1)S(1)} %collective-permute-done.6.seven_a) | copy-start | bytes 221188
  77.6 5.3 %copy-start.21 = (bf16[64,1152]{1,0:T(8,128)(2,1)}, bf16[64,1152]{1,0:T(8,128)(2,1)S(1)}, u32[]{:S(2)}) copy-start(bf16[64,1152]{1,0:T(8,128)(2,1)S(1)} %collective-permute-done.4.three_in) | copy-start | bytes 442372
  77.6 5.3 %copy-start.22 = (bf16[64,1152]{1,0:T(8,128)(2,1)}, bf16[64,1152]{1,0:T(8,128)(2,1)S(1)}, u32[]{:S(2)}) copy-start(bf16[64,1152]{1,0:T(8,128)(2,1)S(1)} %collective-permute-done.5.six_in) | copy-start | bytes 442372
  93.3 5.2 %copy-start.20 = (bf16[128,1024]{1,0:T(8,128)(2,1)S(1)}, bf16[128,1024]{1,0:T(8,128)(2,1)}, u32[]{:S(2)}) copy-start(bf16[128,1024]{1,0:T(8,128)(2,1)} %get-tuple-element.49) | copy-start | bytes 786436
  93.4 10.1 %copy-start.26 = (bf16[64,1024]{1,0:T(8,128)(2,1)S(1)}, bf16[64,1024]{1,0:T(8,128)(2,1)}, u32[]{:S(2)}) copy-start(bf16[64,1024]{1,0:T(8,128)(2,1)} %get-tuple-element.46) | copy-start | bytes 393220
  93.4 12.0 %copy-start.25 = (bf16[64,1024]{1,0:T(8,128)(2,1)S(1)}, bf16[64,1024]{1,0:T(8,128)(2,1)}, u32[]{:S(2)}) copy-start(bf16[64,1024]{1,0:T(8,128)(2,1)} %get-tuple-element.53) | copy-start | bytes 393220
  93.4 13.9 %copy-start.31 = (bf16[32,1024]{1,0:T(8,128)(2,1)S(1)}, bf16[32,1024]{1,0:T(8,128)(2,1)}, u32[]{:S(2)}) copy-start(bf16[32,1024]{1,0:T(8,128)(2,1)} %get-tuple-element.47) | copy-start | bytes 196612
  93.4 17.5 %copy-start.30 = (bf16[32,1024]{1,0:T(8,128)(2,1)S(1)}, bf16[32,1024]{1,0:T(8,128)(2,1)}, u32[]{:S(2)}) copy-start(bf16[32,1024]{1,0:T(8,128)(2,1)} %get-tuple-element.48) | copy-start | bytes 196612
  93.4 24.8 %all-to-all-start.2 = ((bf16[16,16,1024]{2,1,0:T(8,128)(2,1)}), bf16[16,16,1024]{2,1,0:T(8,128)(2,1)S(1)}, u32[]{:S(2)}, u32[]{:S(2)}) async-start(bf16[16,16,1024]{2,1,0:T(8,128)(2,1)} %bitcast.18), calls=%async_computation.2 | async-start | bytes 1048576 | tf_op jit(solution)/shard_map/all_to_all | solution.py:500
  98.6 14.7 %collective-permute-start.11 = (bf16[128,1024]{1,0:T(8,128)(2,1)S(1)}, bf16[128,1024]{1,0:T(8,128)(2,1)S(1)}, u32[]{:S(2)}, u32[]{:S(2)}) collective-permute-start(bf16[128,1024]{1,0:T(8,128)(2,1)S(1)} %copy-done.20), channel_id=1, source_target_pairs={{1,2},{3,4},{5,6},{7,8},{9,10},{11,12},{13,14},{15,16},{17,18},{19... | collective-permute-start | bytes 786440 | tf_op jit(solution)/shard_map/ppermute | solution.py:499
  103.4 14.8 %collective-permute-start.8 = (bf16[64,1024]{1,0:T(8,128)(2,1)S(1)}, bf16[64,1024]{1,0:T(8,128)(2,1)S(1)}, u32[]{:S(2)}, u32[]{:S(2)}) collective-permute-start(bf16[64,1024]{1,0:T(8,128)(2,1)S(1)} %copy-done.26), channel_id=1, source_target_pairs={{0,32},{32,0},{64,96},{96,64},{128,160},{160,128},{192,224},{224,1... | collective-permute-start | bytes 393224 | tf_op jit(solution)/shard_map/ppermute | solution.py:451
  105.4 12.9 %collective-permute-start.12 = (bf16[64,1024]{1,0:T(8,128)(2,1)S(1)}, bf16[64,1024]{1,0:T(8,128)(2,1)S(1)}, u32[]{:S(2)}, u32[]{:S(2)}) collective-permute-start(bf16[64,1024]{1,0:T(8,128)(2,1)S(1)} %copy-done.25), channel_id=1, source_target_pairs={{0,4},{1,5},{2,6},{3,7},{4,0},{5,1},{6,2},{7,3},{8,12},{9,13},{10,... | collective-permute-start | bytes 393224 | tf_op jit(solution)/shard_map/ppermute | solution.py:448
  107.3 10.9 %collective-permute-start.9 = (bf16[32,1024]{1,0:T(8,128)(2,1)S(1)}, bf16[32,1024]{1,0:T(8,128)(2,1)S(1)}, u32[]{:S(2)}, u32[]{:S(2)}) collective-permute-start(bf16[32,1024]{1,0:T(8,128)(2,1)S(1)} %copy-done.31), channel_id=1, source_target_pairs={{0,64},{32,96},{64,0},{96,32},{128,192},{160,224},{192,128},{224,1... | collective-permute-start | bytes 196616 | tf_op jit(solution)/shard_map/ppermute | solution.py:451
  110.9 7.4 %collective-permute-start.10 = (bf16[32,1024]{1,0:T(8,128)(2,1)S(1)}, bf16[32,1024]{1,0:T(8,128)(2,1)S(1)}, u32[]{:S(2)}, u32[]{:S(2)}) collective-permute-start(bf16[32,1024]{1,0:T(8,128)(2,1)S(1)} %copy-done.30), channel_id=1, source_target_pairs={{0,96},{32,64},{64,32},{96,0},{128,224},{160,192},{192,160},{224,1... | collective-permute-start | bytes 196616 | tf_op jit(solution)/shard_map/ppermute | solution.py:451
  113.3 9.3 %copy-start.6 = (bf16[128,1024]{1,0:T(8,128)(2,1)}, bf16[128,1024]{1,0:T(8,128)(2,1)S(1)}, u32[]{:S(2)}) copy-start(bf16[128,1024]{1,0:T(8,128)(2,1)S(1)} %collective-permute-done.11.oth_back) | copy-start | bytes 786436
  118.2 0.8 copy-start.12
  118.3 0.8 copy-start.13
  118.3 0.8 copy-start.7
  118.3 0.8 copy-start.8
  122.6 14.3 %copy-start.17 = (bf16[192,1024]{1,0:T(8,128)(2,1)S(1)}, bf16[192,1024]{1,0:T(8,128)(2,1)}, u32[]{:S(2)}) copy-start(bf16[192,1024]{1,0:T(8,128)(2,1)} %get-tuple-element.56) | copy-start | bytes 1179652
  122.6 17.5 %copy-start.33 = (bf16[32,1024]{1,0:T(8,128)(2,1)S(1)}, bf16[32,1024]{1,0:T(8,128)(2,1)}, u32[]{:S(2)}) copy-start(bf16[32,1024]{1,0:T(8,128)(2,1)} %get-tuple-element.58) | copy-start | bytes 196612
  122.6 21.5 %copy-start.32 = (bf16[32,1024]{1,0:T(8,128)(2,1)S(1)}, bf16[32,1024]{1,0:T(8,128)(2,1)}, u32[]{:S(2)}) copy-start(bf16[32,1024]{1,0:T(8,128)(2,1)} %get-tuple-element.59) | copy-start | bytes 196612
  122.6 38.5 %all-to-all-start.3 = ((bf16[32,8,1024]{2,1,0:T(8,128)(2,1)}), bf16[32,8,1024]{2,1,0:T(8,128)(2,1)S(1)}, u32[]{:S(2)}, u32[]{:S(2)}) async-start(bf16[32,8,1024]{2,1,0:T(8,128)(2,1)} %bitcast.19), calls=%async_computation.3 | async-start | bytes 1048576 | tf_op jit(solution)/shard_map/all_to_all | solution.py:515
  136.9 24.2 %collective-permute-start.13 = (bf16[192,1024]{1,0:T(8,128)(2,1)S(1)}, bf16[192,1024]{1,0:T(8,128)(2,1)S(1)}, u32[]{:S(2)}, u32[]{:S(2)}) collective-permute-start(bf16[192,1024]{1,0:T(8,128)(2,1)S(1)} %copy-done.17), channel_id=1, source_target_pairs={{0,1},{1,0},{2,3},{3,2},{4,5},{5,4},{6,7},{7,6},{8,9},{9,8},{10,11... | collective-permute-start | bytes 1179656 | tf_op jit(solution)/shard_map/ppermute | solution.py:448
  140.1 16.2 %collective-permute-start.14 = (bf16[32,1024]{1,0:T(8,128)(2,1)S(1)}, bf16[32,1024]{1,0:T(8,128)(2,1)S(1)}, u32[]{:S(2)}, u32[]{:S(2)}) collective-permute-start(bf16[32,1024]{1,0:T(8,128)(2,1)S(1)} %copy-done.33), channel_id=1, source_target_pairs={{0,2},{1,3},{2,0},{3,1},{4,6},{5,7},{6,4},{7,5},{8,10},{9,11},{10,... | collective-permute-start | bytes 196616 | tf_op jit(solution)/shard_map/ppermute | solution.py:448
  144.1 17.0 %collective-permute-start.15 = (bf16[32,1024]{1,0:T(8,128)(2,1)S(1)}, bf16[32,1024]{1,0:T(8,128)(2,1)S(1)}, u32[]{:S(2)}, u32[]{:S(2)}) collective-permute-start(bf16[32,1024]{1,0:T(8,128)(2,1)S(1)} %copy-done.32), channel_id=1, source_target_pairs={{0,3},{1,2},{2,1},{3,0},{4,7},{5,6},{6,5},{7,4},{8,11},{9,10},{10,... | collective-permute-start | bytes 196616 | tf_op jit(solution)/shard_map/ppermute | solution.py:448
  156.3 4.8 %copy-start.14 = (bf16[32,1024]{1,0:T(8,128)(2,1)}, bf16[32,1024]{1,0:T(8,128)(2,1)S(1)}, u32[]{:S(2)}) copy-start(bf16[32,1024]{1,0:T(8,128)(2,1)S(1)} %collective-permute-done.14.pair_a) | copy-start | bytes 196612
  161.1 0.9 copy-start.2
  (6 other events, 4.3 us)

commit v4 on v3

--- a/solution.py
+++ b/solution.py
@@ -18,11 +18,24 @@
 bf16 = jnp.bfloat16
 
 
+def coordinate(index, item):
+    device = index[0]
+    shard = device & 31
+    group = device >> 5
+    if item == 3:
+        return shard
+    if item < 3:
+        return shard >> item & 1
+    if item < 6:
+        return shard >> (item - 1) ^ 1
+    return group >> (item - 4) ^ 1
+
+
 def rows_of(shape):
     return lax.broadcasted_iota(jnp.int32, shape, 0)
 
 
-def call(kernel, outs, scratch, index, *operands, flops=0, name=None):
+def call(kernel, outs, scratch, index, *operands, flops=0, name=None, room=8):
     size = sum(o.size * o.dtype.itemsize for o in operands)
     size += sum(o.size * o.dtype.itemsize for o in outs)
     in_specs = [pl.BlockSpec(memory_space=pltpu.SMEM)]
@@ -33,7 +46,7 @@
         in_specs=in_specs,
         out_specs=[pl.BlockSpec(memory_space=pltpu.VMEM) for _ in outs],
         scratch_shapes=scratch,
-        compiler_params=pltpu.CompilerParams(vmem_limit_bytes=VMEM_BYTES),
+        compiler_params=pltpu.CompilerParams(vmem_limit_bytes=room * 1024 * 1024),
         cost_estimate=pl.CostEstimate(flops=flops, bytes_accessed=size, transcendentals=0),
         name=name,
     )(index, *operands)
@@ -49,7 +62,7 @@
 
 def local_kernel(width, peers):
     def kernel(index, mask, key, value, sib, oth, pair, gather):
-        parity = index[0]
+        parity = coordinate(index, 0)
         tokens = key.shape[0]
         length = jnp.sum(mask[...], axis=1, keepdims=True)
         for ref, block in ((sib, 1 - parity), (oth, parity)):
@@ -119,7 +132,7 @@
 
 def quarter_at(index, flip_bits):
     few = COARSE // 4
-    return pl.multiple_of(((index[3] & 3) ^ flip_bits) * few, few)
+    return pl.multiple_of(((coordinate(index, 3) & 3) ^ flip_bits) * few, few)
 
 
 def climb_kernel(groups):
@@ -135,7 +148,7 @@
         store_means(
             seven, 0, pooled(sums, half, 2 * quarter), pooled(counts, half, 2 * quarter), width
         )
-        far_half = index[7]
+        far_half = coordinate(index, 7)
         held = wide.shape[1]
         for side, rows in ((1 - far_half, held), (far_half, held // 2)):
             count = pooled(counts, rows, total // rows)
@@ -178,7 +191,7 @@
         keys, bias, inverse, sums, counts, score, weight, grads,
     ):
         parity, octet, half_shard, quad_group, half_group = (
-            index[0], index[4], index[5], index[6], index[7]
+            coordinate(index, 0), coordinate(index, 4), coordinate(index, 5), coordinate(index, 6), coordinate(index, 7)
         )
         packed = 2 * width
 
@@ -314,9 +327,9 @@
                     res = res * factor
                 far = res[:far_rows] * inverse[...]
                 own_grad[:, cols] = res[far_rows:]
-                low_grad[:, cols] = far[: 2 * COARSE]
+                low_grad[:, cols] = far[: 2 * COARSE].astype(bf16)
                 three_out[:, cols] = far[2 * COARSE : 3 * COARSE].astype(bf16)
-                shard_part[pl.ds(0, 2 * COARSE), cols] = far[3 * COARSE : 5 * COARSE]
+                shard_part[:, cols] = far[3 * COARSE : 5 * COARSE].astype(bf16)
                 six_out[:, cols] = far[5 * COARSE : 6 * COARSE].astype(bf16)
                 seven_a_out[:, cols] = far[6 * COARSE : 6 * COARSE + half].astype(bf16)
                 seven_b_out[:, cols] = far[6 * COARSE + half : 7 * COARSE].astype(bf16)
@@ -352,8 +365,8 @@
     ]
     outs = [
         shape(2 * BLOCK, width), shape(2 * BLOCK, width), shape(2 * BLOCK, 2 * width, f32),
-        shape(BLOCK, 2 * width), shape(BLOCK, 2 * width), shape(2 * COARSE, 2 * width, f32),
-        shape(COARSE, 2 * width), shape(2 * COARSE, 2 * width, f32), shape(COARSE, 2 * width),
+        shape(BLOCK, 2 * width), shape(BLOCK, 2 * width), shape(2 * COARSE, 2 * width),
+        shape(COARSE, 2 * width), shape(2 * COARSE, 2 * width), shape(COARSE, 2 * width),
         shape(half, 2 * width), shape(half, 2 * width), shape(group_rows, 2 * width),
     ]
     return kernel, outs, scratch
@@ -368,11 +381,11 @@
     index, part, six, seven_a, seven_b, group, shares, three, low, sib_grad,
     out, sib_out, pair_a, pair_b, mine, acc,
 ):
-    octet, half_shard = index[4], index[5]
+    octet, half_shard = coordinate(index, 4), coordinate(index, 5)
     tile = six[...].astype(f32) + widen(seven_a[...].astype(f32) + seven_b[...].astype(f32), 2)
     few = COARSE // 4
-    quad_at = pl.multiple_of(index[6] * COARSE, COARSE)
-    half_at = pl.multiple_of(index[7] * 2 * COARSE, 2 * COARSE)
+    quad_at = pl.multiple_of(coordinate(index, 6) * COARSE, COARSE)
+    half_at = pl.multiple_of(coordinate(index, 7) * 2 * COARSE, 2 * COARSE)
     eight = jnp.sum(group[pl.ds(quad_at, COARSE)].astype(f32).reshape(4, few, -1), axis=0)
     nine = group[pl.ds(half_at, 2 * COARSE)].astype(f32).reshape(8, few, -1)[:, : few // 2]
     nine = jnp.sum(nine, axis=0)
@@ -381,8 +394,8 @@
     acc[...] = widen(tile, out.shape[0] // COARSE)
     octet_at = pl.ds(pl.multiple_of(octet * COARSE, COARSE), COARSE)
     half_at = pl.ds(pl.multiple_of(half_shard * 2 * COARSE, 2 * COARSE), 2 * COARSE)
-    acc[octet_at] = acc[octet_at] + part[pl.ds(0, COARSE)]
-    acc[half_at] = acc[half_at] + widen(part[pl.ds(COARSE, COARSE)], 2)
+    acc[octet_at] = acc[octet_at] + part[pl.ds(0, COARSE)].astype(f32)
+    acc[half_at] = acc[half_at] + widen(part[pl.ds(COARSE, COARSE)].astype(f32), 2)
     out[...] = acc[...].astype(bf16)
     half = COARSE // 2
 
@@ -390,9 +403,9 @@
         return three[pl.ds(quarter_at(index, bits), few)].astype(f32)
 
     sib_out[pl.ds(0, BLOCK)] = sib_grad[...]
-    sib_out[pl.ds(BLOCK, COARSE)] = (low[pl.ds(0, COARSE)] + widen(quarter(1), 4)).astype(bf16)
-    pair_a[...] = (low[pl.ds(COARSE, half)] + widen(quarter(2), 2)).astype(bf16)
-    pair_b[...] = (low[pl.ds(COARSE + half, half)] + widen(quarter(3), 2)).astype(bf16)
+    sib_out[pl.ds(BLOCK, COARSE)] = (low[pl.ds(0, COARSE)].astype(f32) + widen(quarter(1), 4)).astype(bf16)
+    pair_a[...] = (low[pl.ds(COARSE, half)].astype(f32) + widen(quarter(2), 2)).astype(bf16)
+    pair_b[...] = (low[pl.ds(COARSE + half, half)].astype(f32) + widen(quarter(3), 2)).astype(bf16)
     mine[...] = quarter(0)
 
 
@@ -401,7 +414,7 @@
         index, mask, own, sib_back, oth_back, pair_a, pair_b, mine, shard,
         key_grad, value_grad, spread,
     ):
-        parity = index[0]
+        parity = coordinate(index, 0)
         tokens = key_grad.shape[0]
         length = jnp.sum(mask[...], axis=1, keepdims=True)
         few = shard.shape[1]
@@ -435,11 +448,7 @@
     packed = 2 * width
     row = packed + LANES
     half = COARSE // 2
-    s = lax.axis_index("shard")
-    g = lax.axis_index("grp")
-    index = jnp.stack(
-        [s & 1, s >> 1 & 1, s >> 2 & 1, s, s >> 3 ^ 1, s >> 4 ^ 1, g >> 2 ^ 1, g >> 3 ^ 1]
-    ).astype(jnp.int32)
+    index = lax.axis_index(("grp", "shard")).astype(jnp.int32).reshape(1)
     mask = valid_mask.reshape(1, tokens)
     pairs = [(2 * i - 1, 2 * i) for i in range(1, total // 2)]
     pairs = pairs + [(high, low) for low, high in pairs]
@@ -458,7 +467,7 @@
             shape(BLOCK + COARSE, row), shape(BLOCK, row), shape(half, row),
             jax.ShapeDtypeStruct((shards, few_shard, row), bf16),
         ],
-        [], index, mask, key_states, value_states, name="local",
+        [], index, mask, key_states, value_states, name="local", room=62,
     )
     sib_in = on_shard(sib, 1)
     pair_a = on_shard(pair, 2)
@@ -490,7 +499,7 @@
     ) = call(
         kernel, outs, scratch, index, query_states, attended_grad, sib, oth, sib_in, oth_in,
         pair_a, pair_b, three_in, shard_in, six_in, seven_a, seven_b, group_in,
-        flops=1_600_000_000, name="attention",
+        flops=1_600_000_000, name="attention", room=62,
     )
     six_back = on_group(six_out, 1)
     seven_a_back = on_group(seven_a_out, 2)

time: 166 us -> 159 us (0.958)
  Pallas kernels: 22.1 us -> 17.5 us
  local copies, waits for them, and re-layouts: 4.3 us -> 2.13 us
    pallas_call x5, Pallas kernels: 22.1 us -> 17.5 us  [call(): pl.pallas_call(kernel, out_shape=outs, in_specs=in_specs, out_specs=[pl.B...]
    unnamed x68 -> x42, local copies, waits for them, and re-layouts: 3.63 us -> 2.13 us
where the time goes in v4:
time: 159 us; the launch traced here: 158 us
  starting transfers between devices  92.7 us (58%)
  waiting for transfers between devices  44.8 us (28%)
  Pallas kernels  17.5 us (11%)
  local copies, waits for them, and re-layouts  2.13 us (1%)
    ppermute x8, waiting for transfers between devices, on_shard(): return lax.ppermute(x, 'shard', flip(shards, bits))  30.6 us
    ppermute x8, starting transfers between devices, on_shard(): return lax.ppermute(x, 'shard', flip(shards, bits))  22.2 us
    pallas_call x5, Pallas kernels, call(): pl.pallas_call(kernel, out_shape=outs, in_specs=in_specs, out_specs=[pl.B...  17.5 us
    ppermute x6, starting transfers between devices, on_group(): return lax.ppermute(x, 'grp', flip(groups, bits))  15.6 us
    all_to_all x1, starting transfers between devices, body(): shard_back = lax.all_to_all(shard_out, 'shard', 0, 0, tiled=True)  14.2 us
    all_to_all x1, starting transfers between devices, body(): lax.all_to_all(gather, 'shard', 0, 0, tiled=True)  13.6 us
    all_to_all x1, starting transfers between devices, body(): lax.all_to_all(wide, 'grp', 0, 0, tiled=True)  11.9 us
    all_to_all x1, waiting for transfers between devices, body(): lax.all_to_all(wide, 'grp', 0, 0, tiled=True)  5.33 us
  transfers between devices with their start and end apart: 20, of which 8 were waited for; matrix products, arithmetic and copies ran while one was open for 0% of the time, Pallas kernels for 0%

profile of v4, /device:TPU:1, one launch (start us, length us, event | category | flops | bytes accessed | tf_op | source)
XLA Modules:
  0.0 158.1 jit_solution(9621950370734979600)
XLA Ops:
  0.6 2.5 %local.1 = (bf16[192,1152]{1,0:T(8,128)(2,1)}, bf16[128,1152]{1,0:T(8,128)(2,1)}, bf16[32,1152]{1,0:T(8,128)(2,1)}, bf16[32,8,1152]{2,1,0:T(8,128)(2,1)}) custom-call(s32[1]{0:T(128)} %bitcast.index, s32[1,256]{1,0:T(1,128)} %bitcast.10, bf16[256,512]{1,0:T(8,128)(2,1)} %key.1, bf16[256,512]{1,0:T(8,128)(2,1)} %value.1), custom_call_target="tpu_custom_call" | custom-call | bytes 1926144 | tf_op jit(solution)/shard_map/local/pallas_call | solution.py:43
  3.1 13.6 %all-to-all-start = ((bf16[32,8,1152]{2,1,0:T(8,128)(2,1)}), bf16[32,8,1152]{2,1,0:T(8,128)(2,1)S(1)}, u32[]{:S(2)}, u32[]{:S(2)}) async-start(bf16[32,8,1152]{2,1,0:T(8,128)(2,1)} %get-tuple-element.37), calls=%async_computation | async-start | bytes 1179648 | tf_op jit(solution)/shard_map/all_to_all | solution.py:476
  16.7 3.1 %collective-permute-start = (bf16[192,1152]{1,0:T(8,128)(2,1)S(1)}, bf16[192,1152]{1,0:T(8,128)(2,1)S(1)}, u32[]{:S(2)}, u32[]{:S(2)}) collective-permute-start(bf16[192,1152]{1,0:T(8,128)(2,1)S(1)} %copy-done.13), channel_id=1, source_target_pairs={{0,1},{1,0},{2,3},{3,2},{4,5},{5,4},{6,7},{7,6},{8,9},{9,8},{10,11... | collective-permute-start | bytes 1327112 | tf_op jit(solution)/shard_map/ppermute | solution.py:457
  19.9 4.0 %collective-permute-start.3 = (bf16[32,1152]{1,0:T(8,128)(2,1)S(1)}, bf16[32,1152]{1,0:T(8,128)(2,1)S(1)}, u32[]{:S(2)}, u32[]{:S(2)}) collective-permute-start(bf16[32,1152]{1,0:T(8,128)(2,1)S(1)} %copy-done.8), channel_id=1, source_target_pairs={{0,3},{1,2},{2,1},{3,0},{4,7},{5,6},{6,5},{7,4},{8,11},{9,10},{10,... | collective-permute-start | bytes 221192 | tf_op jit(solution)/shard_map/ppermute | solution.py:457
  23.9 1.9 %collective-permute-start.2 = (bf16[32,1152]{1,0:T(8,128)(2,1)S(1)}, bf16[32,1152]{1,0:T(8,128)(2,1)S(1)}, u32[]{:S(2)}, u32[]{:S(2)}) collective-permute-start(bf16[32,1152]{1,0:T(8,128)(2,1)S(1)} %copy-done.8), channel_id=1, source_target_pairs={{0,2},{1,3},{2,0},{3,1},{4,6},{5,7},{6,4},{7,5},{8,10},{9,11},{10,... | collective-permute-start | bytes 221192 | tf_op jit(solution)/shard_map/ppermute | solution.py:457
  25.8 16.0 %collective-permute-done.3.pair_b = bf16[32,1152]{1,0:T(8,128)(2,1)S(1)} collective-permute-done((bf16[32,1152]{1,0:T(8,128)(2,1)S(1)}, bf16[32,1152]{1,0:T(8,128)(2,1)S(1)}, u32[]{:S(2)}, u32[]{:S(2)}) %collective-permute-start.3) | collective-permute-done | bytes 73760 | tf_op jit(solution)/shard_map/ppermute | solution.py:457
  41.8 0.0 collective-permute-done.2.pair_a
  41.8 0.0 collective-permute-done.sib_in
  41.8 0.0 all-to-all-done
  41.9 2.1 %climb.1 = (bf16[64,1152]{1,0:T(8,128)(2,1)S(1)}, bf16[64,1152]{1,0:T(8,128)(2,1)S(1)}, bf16[32,1152]{1,0:T(8,128)(2,1)S(1)}, bf16[16,16,1024]{2,1,0:T(8,128)(2,1)}, f32[24,128]{1,0:T(8,128)S(1)}) custom-call(s32[1]{0:T(128)} %bitcast.index, bf16[192,1152]{1,0:T(8,128)(2,1)S(1)} %collective-permute-done.sib_in, bf16[32,1152]{1,0:T(8,128)(2,1)S(1)} %copy-done.8, ...), custom_call_target="tpu_custom_call" | custom-call | bytes 2158592 | tf_op jit(solution)/shard_map/climb/pallas_call | solution.py:43
  44.0 11.9 %all-to-all-start.1 = ((bf16[16,16,1024]{2,1,0:T(8,128)(2,1)}), bf16[16,16,1024]{2,1,0:T(8,128)(2,1)S(1)}, u32[]{:S(2)}, u32[]{:S(2)}) async-start(bf16[16,16,1024]{2,1,0:T(8,128)(2,1)} %get-tuple-element.41), calls=%async_computation.1 | async-start | bytes 1048576 | tf_op jit(solution)/shard_map/all_to_all | solution.py:494
  55.9 5.2 %collective-permute-start.1 = (bf16[128,1152]{1,0:T(8,128)(2,1)S(1)}, bf16[128,1152]{1,0:T(8,128)(2,1)S(1)}, u32[]{:S(2)}, u32[]{:S(2)}) collective-permute-start(bf16[128,1152]{1,0:T(8,128)(2,1)S(1)} %copy-done.14), channel_id=1, source_target_pairs={{1,2},{3,4},{5,6},{7,8},{9,10},{11,12},{13,14},{15,16},{17,18},{19... | collective-permute-start | bytes 884744 | tf_op jit(solution)/shard_map/ppermute | solution.py:475
  61.1 1.9 %collective-permute-start.4 = (bf16[64,1152]{1,0:T(8,128)(2,1)S(1)}, bf16[64,1152]{1,0:T(8,128)(2,1)S(1)}, u32[]{:S(2)}, u32[]{:S(2)}) collective-permute-start(bf16[64,1152]{1,0:T(8,128)(2,1)S(1)} %get-tuple-element.38), channel_id=1, source_target_pairs={{0,4},{1,5},{2,6},{3,7},{4,0},{5,1},{6,2},{7,3},{8,12},{9,13},{10,... | collective-permute-start | bytes 442376 | tf_op jit(solution)/shard_map/ppermute | solution.py:457
  63.0 1.9 %collective-permute-start.5 = (bf16[64,1152]{1,0:T(8,128)(2,1)S(1)}, bf16[64,1152]{1,0:T(8,128)(2,1)S(1)}, u32[]{:S(2)}, u32[]{:S(2)}) collective-permute-start(bf16[64,1152]{1,0:T(8,128)(2,1)S(1)} %get-tuple-element.39), channel_id=1, source_target_pairs={{0,32},{32,0},{64,96},{96,64},{128,160},{160,128},{192,224},{224,1... | collective-permute-start | bytes 442376 | tf_op jit(solution)/shard_map/ppermute | solution.py:460
  65.0 3.9 %collective-permute-start.7 = (bf16[32,1152]{1,0:T(8,128)(2,1)S(1)}, bf16[32,1152]{1,0:T(8,128)(2,1)S(1)}, u32[]{:S(2)}, u32[]{:S(2)}) collective-permute-start(bf16[32,1152]{1,0:T(8,128)(2,1)S(1)} %get-tuple-element.40), channel_id=1, source_target_pairs={{0,96},{32,64},{64,32},{96,0},{128,224},{160,192},{192,160},{224,1... | collective-permute-start | bytes 221192 | tf_op jit(solution)/shard_map/ppermute | solution.py:460
  68.9 1.9 %collective-permute-start.6 = (bf16[32,1152]{1,0:T(8,128)(2,1)S(1)}, bf16[32,1152]{1,0:T(8,128)(2,1)S(1)}, u32[]{:S(2)}, u32[]{:S(2)}) collective-permute-start(bf16[32,1152]{1,0:T(8,128)(2,1)S(1)} %get-tuple-element.40), channel_id=1, source_target_pairs={{0,64},{32,96},{64,0},{96,32},{128,192},{160,224},{192,128},{224,1... | collective-permute-start | bytes 221192 | tf_op jit(solution)/shard_map/ppermute | solution.py:460
  70.8 0.2 collective-permute-done.1.oth_in
  71.0 0.8 collective-permute-done.7.seven_b
  71.8 2.9 %collective-permute-done.6.seven_a = bf16[32,1152]{1,0:T(8,128)(2,1)S(1)} collective-permute-done((bf16[32,1152]{1,0:T(8,128)(2,1)S(1)}, bf16[32,1152]{1,0:T(8,128)(2,1)S(1)}, u32[]{:S(2)}, u32[]{:S(2)}) %collective-permute-start.6) | collective-permute-done | bytes 73760 | tf_op jit(solution)/shard_map/ppermute | solution.py:460
  74.7 0.0 collective-permute-done.4.three_in
  74.7 0.0 collective-permute-done.5.six_in
  74.7 5.3 %all-to-all-done.1 = bf16[16,16,1024]{2,1,0:T(8,128)(2,1)S(1)} async-done(((bf16[16,16,1024]{2,1,0:T(8,128)(2,1)}), bf16[16,16,1024]{2,1,0:T(8,128)(2,1)S(1)}, u32[]{:S(2)}, u32[]{:S(2)}) %all-to-all-start.1) | async-done | bytes 524320 | tf_op jit(solution)/shard_map/all_to_all | solution.py:494
  80.1 0.8 copy-done.12
  80.8 9.5 %attention.1 = (bf16[256,512]{1,0:T(8,128)(2,1)}, bf16[256,512]{1,0:T(8,128)(2,1)}, f32[256,1024]{1,0:T(8,128)}, bf16[128,1024]{1,0:T(8,128)(2,1)}, bf16[128,102...) custom-call(s32[1]{0:T(128)} %bitcast.index, ...), custom_call_target="tpu_custom_call" | custom-call | flops 1600000000 | bytes 7241728 | tf_op jit(solution)/shard_map/attention/pallas_call | solution.py:43
  90.3 0.0 copy-start.16
  90.3 0.0 copy-start.3
  90.3 5.2 %all-to-all-start.2 = ((bf16[16,16,1024]{2,1,0:T(8,128)(2,1)}), bf16[16,16,1024]{2,1,0:T(8,128)(2,1)S(1)}, u32[]{:S(2)}, u32[]{:S(2)}) async-start(bf16[16,16,1024]{2,1,0:T(8,128)(2,1)} %bitcast.13), calls=%async_computation.2 | async-start | bytes 1048576 | tf_op jit(solution)/shard_map/all_to_all | solution.py:509
  95.5 4.8 %collective-permute-start.11 = (bf16[128,1024]{1,0:T(8,128)(2,1)S(1)}, bf16[128,1024]{1,0:T(8,128)(2,1)S(1)}, u32[]{:S(2)}, u32[]{:S(2)}) collective-permute-start(bf16[128,1024]{1,0:T(8,128)(2,1)S(1)} %copy-done.16), channel_id=1, source_target_pairs={{1,2},{3,4},{5,6},{7,8},{9,10},{11,12},{13,14},{15,16},{17,18},{19... | collective-permute-start | bytes 786440 | tf_op jit(solution)/shard_map/ppermute | solution.py:508
  100.3 1.9 %collective-permute-start.8 = (bf16[64,1024]{1,0:T(8,128)(2,1)}, bf16[64,1024]{1,0:T(8,128)(2,1)S(1)}, u32[]{:S(2)}, u32[]{:S(2)}) collective-permute-start(bf16[64,1024]{1,0:T(8,128)(2,1)} %get-tuple-element.46), channel_id=1, source_target_pairs={{0,32},{32,0},{64,96},{96,64},{128,160},{160,128},{192,224},{224,1... | collective-permute-start | bytes 393224 | tf_op jit(solution)/shard_map/ppermute | solution.py:460
  102.3 1.9 %collective-permute-start.12 = (bf16[64,1024]{1,0:T(8,128)(2,1)}, bf16[64,1024]{1,0:T(8,128)(2,1)S(1)}, u32[]{:S(2)}, u32[]{:S(2)}) collective-permute-start(bf16[64,1024]{1,0:T(8,128)(2,1)} %get-tuple-element.53), channel_id=1, source_target_pairs={{0,4},{1,5},{2,6},{3,7},{4,0},{5,1},{6,2},{7,3},{8,12},{9,13},{10,... | collective-permute-start | bytes 393224 | tf_op jit(solution)/shard_map/ppermute | solution.py:457
  104.2 3.5 %collective-permute-start.9 = (bf16[32,1024]{1,0:T(8,128)(2,1)}, bf16[32,1024]{1,0:T(8,128)(2,1)S(1)}, u32[]{:S(2)}, u32[]{:S(2)}) collective-permute-start(bf16[32,1024]{1,0:T(8,128)(2,1)} %get-tuple-element.47), channel_id=1, source_target_pairs={{0,64},{32,96},{64,0},{96,32},{128,192},{160,224},{192,128},{224,1... | collective-permute-start | bytes 196616 | tf_op jit(solution)/shard_map/ppermute | solution.py:460
  107.8 2.4 %collective-permute-start.10 = (bf16[32,1024]{1,0:T(8,128)(2,1)}, bf16[32,1024]{1,0:T(8,128)(2,1)S(1)}, u32[]{:S(2)}, u32[]{:S(2)}) collective-permute-start(bf16[32,1024]{1,0:T(8,128)(2,1)} %get-tuple-element.48), channel_id=1, source_target_pairs={{0,96},{32,64},{64,32},{96,0},{128,224},{160,192},{192,160},{224,1... | collective-permute-start | bytes 196616 | tf_op jit(solution)/shard_map/ppermute | solution.py:460
  110.2 0.0 collective-permute-done.11.oth_back
  110.2 5.0 %all-to-all-done.2 = bf16[16,16,1024]{2,1,0:T(8,128)(2,1)S(1)} async-done(((bf16[16,16,1024]{2,1,0:T(8,128)(2,1)}), bf16[16,16,1024]{2,1,0:T(8,128)(2,1)S(1)}, u32[]{:S(2)}, u32[]{:S(2)}) %all-to-all-start.2) | async-done | bytes 524320 | tf_op jit(solution)/shard_map/all_to_all | solution.py:509
  115.2 0.0 collective-permute-done.9.seven_a
  115.2 0.0 collective-permute-done.10.seven_b
  115.3 1.8 %back.1 = (bf16[256,1024]{1,0:T(8,128)(2,1)}, bf16[192,1024]{1,0:T(8,128)(2,1)S(1)}, bf16[32,1024]{1,0:T(8,128)(2,1)S(1)}, bf16[32,1024]{1,0:T(8,128)(2,1)S(1)}, f32[16,1024]{1,0:T(8,128)S(1)}) custom-call(s32[1]{0:T(128)} %bitcast.index, bf16[128,1024]{1,0:T(8,128)(2,1)S(1)} %copy-done.5, bf16[64,1024]{1,0:T(8,128)(2,1)S(1)} %collective-permute-done.8.six, ...), custom_call_target="tpu_custom_call" | custom-call | bytes 2830336 | tf_op jit(solution)/shard_map/back/pallas_call | solution.py:43
  117.1 0.6 copy-done.10
  117.7 14.2 %all-to-all-start.3 = ((bf16[32,8,1024]{2,1,0:T(8,128)(2,1)}), bf16[32,8,1024]{2,1,0:T(8,128)(2,1)S(1)}, u32[]{:S(2)}, u32[]{:S(2)}) async-start(bf16[32,8,1024]{2,1,0:T(8,128)(2,1)} %bitcast.6), calls=%async_computation.3 | async-start | bytes 1048576 | tf_op jit(solution)/shard_map/all_to_all | solution.py:524
  132.0 3.1 %collective-permute-start.13 = (bf16[192,1024]{1,0:T(8,128)(2,1)S(1)}, bf16[192,1024]{1,0:T(8,128)(2,1)S(1)}, u32[]{:S(2)}, u32[]{:S(2)}) collective-permute-start(bf16[192,1024]{1,0:T(8,128)(2,1)S(1)} %get-tuple-element.56), channel_id=1, source_target_pairs={{0,1},{1,0},{2,3},{3,2},{4,5},{5,4},{6,7},{7,6},{8,9},{9,8},{10,11... | collective-permute-start | bytes 1179656 | tf_op jit(solution)/shard_map/ppermute | solution.py:457
  135.1 4.0 %collective-permute-start.14 = (bf16[32,1024]{1,0:T(8,128)(2,1)S(1)}, bf16[32,1024]{1,0:T(8,128)(2,1)S(1)}, u32[]{:S(2)}, u32[]{:S(2)}) collective-permute-start(bf16[32,1024]{1,0:T(8,128)(2,1)S(1)} %copy-done.11), channel_id=1, source_target_pairs={{0,2},{1,3},{2,0},{3,1},{4,6},{5,7},{6,4},{7,5},{8,10},{9,11},{10,... | collective-permute-start | bytes 196616 | tf_op jit(solution)/shard_map/ppermute | solution.py:457
  139.1 2.1 %collective-permute-start.15 = (bf16[32,1024]{1,0:T(8,128)(2,1)S(1)}, bf16[32,1024]{1,0:T(8,128)(2,1)S(1)}, u32[]{:S(2)}, u32[]{:S(2)}) collective-permute-start(bf16[32,1024]{1,0:T(8,128)(2,1)S(1)} %get-tuple-element.59), channel_id=1, source_target_pairs={{0,3},{1,2},{2,1},{3,0},{4,7},{5,6},{6,5},{7,4},{8,11},{9,10},{10,... | collective-permute-start | bytes 196616 | tf_op jit(solution)/shard_map/ppermute | solution.py:457
  141.3 10.1 %collective-permute-done.14.pair_a = bf16[32,1024]{1,0:T(8,128)(2,1)S(1)} collective-permute-done((bf16[32,1024]{1,0:T(8,128)(2,1)S(1)}, bf16[32,1024]{1,0:T(8,128)(2,1)S(1)}, u32[]{:S(2)}, u32[]{:S(2)}) %collective-permute-start.14) | collective-permute-done | bytes 65568 | tf_op jit(solution)/shard_map/ppermute | solution.py:457
  151.4 4.5 %collective-permute-done.15.pair_b = bf16[32,1024]{1,0:T(8,128)(2,1)S(1)} collective-permute-done((bf16[32,1024]{1,0:T(8,128)(2,1)S(1)}, bf16[32,1024]{1,0:T(8,128)(2,1)S(1)}, u32[]{:S(2)}, u32[]{:S(2)}) %collective-permute-start.15) | collective-permute-done | bytes 65568 | tf_op jit(solution)/shard_map/ppermute | solution.py:457
  155.9 0.0 collective-permute-done.13.sib_back
  155.9 0.0 all-to-all-done.3.shard
  155.9 0.7 copy-done.9
  156.6 1.6 %final.1 = (bf16[256,512]{1,0:T(8,128)(2,1)}, bf16[256,512]{1,0:T(8,128)(2,1)}) custom-call(s32[1]{0:T(128)} %bitcast.index, s32[1,256]{1,0:T(1,128)S(1)} %bitcast.11, f32[256,1024]{1,0:T(8,128)S(1)} %copy-done.1, bf16[192,1024]{1,0:T(8,128)(2,1)S(1)} %collective-permute-done.13.sib_back, bf16[128,1024]{1,0:T(8,128)(2,1)S(1)} %collective-permute-done.11.oth_back, ...), custom_call_target="tpu_custom_call" | custom-call | bytes 2950144 | tf_op jit(solution)/shard_map/final/pallas_call | solution.py:43
  (39 shorter events, 0.1 us)
Async XLA Ops:
  3.1 13.6 %copy-start.13 = (bf16[192,1152]{1,0:T(8,128)(2,1)S(1)}, bf16[192,1152]{1,0:T(8,128)(2,1)}, u32[]{:S(2)}) copy-start(bf16[192,1152]{1,0:T(8,128)(2,1)} %get-tuple-element.34.sib) | copy-start | bytes 1327108
  3.1 16.8 %copy-start.8 = (bf16[32,1152]{1,0:T(8,128)(2,1)S(1)}, bf16[32,1152]{1,0:T(8,128)(2,1)}, u32[]{:S(2)}) copy-start(bf16[32,1152]{1,0:T(8,128)(2,1)} %get-tuple-element.36.pair) | copy-start | bytes 221188
  3.1 38.7 %all-to-all-start = ((bf16[32,8,1152]{2,1,0:T(8,128)(2,1)}), bf16[32,8,1152]{2,1,0:T(8,128)(2,1)S(1)}, u32[]{:S(2)}, u32[]{:S(2)}) async-start(bf16[32,8,1152]{2,1,0:T(8,128)(2,1)} %get-tuple-element.37), calls=%async_computation | async-start | bytes 1179648 | tf_op jit(solution)/shard_map/all_to_all | solution.py:476
  16.7 25.1 %collective-permute-start = (bf16[192,1152]{1,0:T(8,128)(2,1)S(1)}, bf16[192,1152]{1,0:T(8,128)(2,1)S(1)}, u32[]{:S(2)}, u32[]{:S(2)}) collective-permute-start(bf16[192,1152]{1,0:T(8,128)(2,1)S(1)} %copy-done.13), channel_id=1, source_target_pairs={{0,1},{1,0},{2,3},{3,2},{4,5},{5,4},{6,7},{7,6},{8,9},{9,8},{10,11... | collective-permute-start | bytes 1327112 | tf_op jit(solution)/shard_map/ppermute | solution.py:457
  19.9 21.9 %collective-permute-start.3 = (bf16[32,1152]{1,0:T(8,128)(2,1)S(1)}, bf16[32,1152]{1,0:T(8,128)(2,1)S(1)}, u32[]{:S(2)}, u32[]{:S(2)}) collective-permute-start(bf16[32,1152]{1,0:T(8,128)(2,1)S(1)} %copy-done.8), channel_id=1, source_target_pairs={{0,3},{1,2},{2,1},{3,0},{4,7},{5,6},{6,5},{7,4},{8,11},{9,10},{10,... | collective-permute-start | bytes 221192 | tf_op jit(solution)/shard_map/ppermute | solution.py:457
  23.9 17.9 %collective-permute-start.2 = (bf16[32,1152]{1,0:T(8,128)(2,1)S(1)}, bf16[32,1152]{1,0:T(8,128)(2,1)S(1)}, u32[]{:S(2)}, u32[]{:S(2)}) collective-permute-start(bf16[32,1152]{1,0:T(8,128)(2,1)S(1)} %copy-done.8), channel_id=1, source_target_pairs={{0,2},{1,3},{2,0},{3,1},{4,6},{5,7},{6,4},{7,5},{8,10},{9,11},{10,... | collective-permute-start | bytes 221192 | tf_op jit(solution)/shard_map/ppermute | solution.py:457
  41.8 2.2 %copy-start.6 = (bf16[32,1152]{1,0:T(8,128)(2,1)}, bf16[32,1152]{1,0:T(8,128)(2,1)S(1)}, u32[]{:S(2)}) copy-start(bf16[32,1152]{1,0:T(8,128)(2,1)S(1)} %collective-permute-done.3.pair_b) | copy-start | bytes 221188
  41.8 2.2 %copy-start.7 = (bf16[32,1152]{1,0:T(8,128)(2,1)}, bf16[32,1152]{1,0:T(8,128)(2,1)S(1)}, u32[]{:S(2)}) copy-start(bf16[32,1152]{1,0:T(8,128)(2,1)S(1)} %collective-permute-done.2.pair_a) | copy-start | bytes 221188
  41.8 2.2 %copy-start.2 = (bf16[192,1152]{1,0:T(8,128)(2,1)}, bf16[192,1152]{1,0:T(8,128)(2,1)S(1)}, u32[]{:S(2)}) copy-start(bf16[192,1152]{1,0:T(8,128)(2,1)S(1)} %collective-permute-done.sib_in) | copy-start | bytes 1327108
  41.8 2.2 %copy-start = (bf16[32,8,1152]{2,1,0:T(8,128)(2,1)}, bf16[32,8,1152]{2,1,0:T(8,128)(2,1)S(1)}, u32[]{:S(2)}) copy-start(bf16[32,8,1152]{2,1,0:T(8,128)(2,1)S(1)} %all-to-all-done) | copy-start | bytes 1769476
  44.0 11.9 %copy-start.14 = (bf16[128,1152]{1,0:T(8,128)(2,1)S(1)}, bf16[128,1152]{1,0:T(8,128)(2,1)}, u32[]{:S(2)}) copy-start(bf16[128,1152]{1,0:T(8,128)(2,1)} %get-tuple-element.35.oth) | copy-start | bytes 884740
  44.0 36.0 %all-to-all-start.1 = ((bf16[16,16,1024]{2,1,0:T(8,128)(2,1)}), bf16[16,16,1024]{2,1,0:T(8,128)(2,1)S(1)}, u32[]{:S(2)}, u32[]{:S(2)}) async-start(bf16[16,16,1024]{2,1,0:T(8,128)(2,1)} %get-tuple-element.41), calls=%async_computation.1 | async-start | bytes 1048576 | tf_op jit(solution)/shard_map/all_to_all | solution.py:494
  55.9 15.1 %collective-permute-start.1 = (bf16[128,1152]{1,0:T(8,128)(2,1)S(1)}, bf16[128,1152]{1,0:T(8,128)(2,1)S(1)}, u32[]{:S(2)}, u32[]{:S(2)}) collective-permute-start(bf16[128,1152]{1,0:T(8,128)(2,1)S(1)} %copy-done.14), channel_id=1, source_target_pairs={{1,2},{3,4},{5,6},{7,8},{9,10},{11,12},{13,14},{15,16},{17,18},{19... | collective-permute-start | bytes 884744 | tf_op jit(solution)/shard_map/ppermute | solution.py:475
  61.1 13.6 %collective-permute-start.4 = (bf16[64,1152]{1,0:T(8,128)(2,1)S(1)}, bf16[64,1152]{1,0:T(8,128)(2,1)S(1)}, u32[]{:S(2)}, u32[]{:S(2)}) collective-permute-start(bf16[64,1152]{1,0:T(8,128)(2,1)S(1)} %get-tuple-element.38), channel_id=1, source_target_pairs={{0,4},{1,5},{2,6},{3,7},{4,0},{5,1},{6,2},{7,3},{8,12},{9,13},{10,... | collective-permute-start | bytes 442376 | tf_op jit(solution)/shard_map/ppermute | solution.py:457
  63.0 11.7 %collective-permute-start.5 = (bf16[64,1152]{1,0:T(8,128)(2,1)S(1)}, bf16[64,1152]{1,0:T(8,128)(2,1)S(1)}, u32[]{:S(2)}, u32[]{:S(2)}) collective-permute-start(bf16[64,1152]{1,0:T(8,128)(2,1)S(1)} %get-tuple-element.39), channel_id=1, source_target_pairs={{0,32},{32,0},{64,96},{96,64},{128,160},{160,128},{192,224},{224,1... | collective-permute-start | bytes 442376 | tf_op jit(solution)/shard_map/ppermute | solution.py:460
  65.0 6.8 %collective-permute-start.7 = (bf16[32,1152]{1,0:T(8,128)(2,1)S(1)}, bf16[32,1152]{1,0:T(8,128)(2,1)S(1)}, u32[]{:S(2)}, u32[]{:S(2)}) collective-permute-start(bf16[32,1152]{1,0:T(8,128)(2,1)S(1)} %get-tuple-element.40), channel_id=1, source_target_pairs={{0,96},{32,64},{64,32},{96,0},{128,224},{160,192},{192,160},{224,1... | collective-permute-start | bytes 221192 | tf_op jit(solution)/shard_map/ppermute | solution.py:460
  68.9 5.8 %collective-permute-start.6 = (bf16[32,1152]{1,0:T(8,128)(2,1)S(1)}, bf16[32,1152]{1,0:T(8,128)(2,1)S(1)}, u32[]{:S(2)}, u32[]{:S(2)}) collective-permute-start(bf16[32,1152]{1,0:T(8,128)(2,1)S(1)} %get-tuple-element.40), channel_id=1, source_target_pairs={{0,64},{32,96},{64,0},{96,32},{128,192},{160,224},{192,128},{224,1... | collective-permute-start | bytes 221192 | tf_op jit(solution)/shard_map/ppermute | solution.py:460
  71.0 9.0 %copy-start.15 = (bf16[128,1152]{1,0:T(8,128)(2,1)}, bf16[128,1152]{1,0:T(8,128)(2,1)S(1)}, u32[]{:S(2)}) copy-start(bf16[128,1152]{1,0:T(8,128)(2,1)S(1)} %collective-permute-done.1.oth_in) | copy-start | bytes 884740
  71.8 8.3 %copy-start.19 = (bf16[32,1152]{1,0:T(8,128)(2,1)}, bf16[32,1152]{1,0:T(8,128)(2,1)S(1)}, u32[]{:S(2)}) copy-start(bf16[32,1152]{1,0:T(8,128)(2,1)S(1)} %collective-permute-done.7.seven_b) | copy-start | bytes 221188
  74.7 5.4 %copy-start.20 = (bf16[32,1152]{1,0:T(8,128)(2,1)}, bf16[32,1152]{1,0:T(8,128)(2,1)S(1)}, u32[]{:S(2)}) copy-start(bf16[32,1152]{1,0:T(8,128)(2,1)S(1)} %collective-permute-done.6.seven_a) | copy-start | bytes 221188
  74.7 5.4 %copy-start.17 = (bf16[64,1152]{1,0:T(8,128)(2,1)}, bf16[64,1152]{1,0:T(8,128)(2,1)S(1)}, u32[]{:S(2)}) copy-start(bf16[64,1152]{1,0:T(8,128)(2,1)S(1)} %collective-permute-done.4.three_in) | copy-start | bytes 442372
  74.7 5.4 %copy-start.18 = (bf16[64,1152]{1,0:T(8,128)(2,1)}, bf16[64,1152]{1,0:T(8,128)(2,1)S(1)}, u32[]{:S(2)}) copy-start(bf16[64,1152]{1,0:T(8,128)(2,1)S(1)} %collective-permute-done.5.six_in) | copy-start | bytes 442372
  80.0 0.8 copy-start.12
  90.3 5.2 %copy-start.16 = (bf16[128,1024]{1,0:T(8,128)(2,1)S(1)}, bf16[128,1024]{1,0:T(8,128)(2,1)}, u32[]{:S(2)}) copy-start(bf16[128,1024]{1,0:T(8,128)(2,1)} %get-tuple-element.49) | copy-start | bytes 786436
  90.3 24.9 %copy-start.3 = (bf16[128,1024]{1,0:T(8,128)(2,1)S(1)}, bf16[128,1024]{1,0:T(8,128)(2,1)}, u32[]{:S(2)}) copy-start(bf16[128,1024]{1,0:T(8,128)(2,1)} %get-tuple-element.55.sib_grad) | copy-start | bytes 786436
  90.3 24.9 %copy-start.4 = (bf16[128,1024]{1,0:T(8,128)(2,1)S(1)}, bf16[128,1024]{1,0:T(8,128)(2,1)}, u32[]{:S(2)}) copy-start(bf16[128,1024]{1,0:T(8,128)(2,1)} %get-tuple-element.54.low) | copy-start | bytes 786436
  90.3 24.9 %copy-start.5 = (bf16[128,1024]{1,0:T(8,128)(2,1)S(1)}, bf16[128,1024]{1,0:T(8,128)(2,1)}, u32[]{:S(2)}) copy-start(bf16[128,1024]{1,0:T(8,128)(2,1)} %get-tuple-element.45.part) | copy-start | bytes 786436
  90.3 24.9 %all-to-all-start.2 = ((bf16[16,16,1024]{2,1,0:T(8,128)(2,1)}), bf16[16,16,1024]{2,1,0:T(8,128)(2,1)S(1)}, u32[]{:S(2)}, u32[]{:S(2)}) async-start(bf16[16,16,1024]{2,1,0:T(8,128)(2,1)} %bitcast.13), calls=%async_computation.2 | async-start | bytes 1048576 | tf_op jit(solution)/shard_map/all_to_all | solution.py:509
  95.5 14.6 %collective-permute-start.11 = (bf16[128,1024]{1,0:T(8,128)(2,1)S(1)}, bf16[128,1024]{1,0:T(8,128)(2,1)S(1)}, u32[]{:S(2)}, u32[]{:S(2)}) collective-permute-start(bf16[128,1024]{1,0:T(8,128)(2,1)S(1)} %copy-done.16), channel_id=1, source_target_pairs={{1,2},{3,4},{5,6},{7,8},{9,10},{11,12},{13,14},{15,16},{17,18},{19... | collective-permute-start | bytes 786440 | tf_op jit(solution)/shard_map/ppermute | solution.py:508
  100.3 14.9 %collective-permute-start.8 = (bf16[64,1024]{1,0:T(8,128)(2,1)}, bf16[64,1024]{1,0:T(8,128)(2,1)S(1)}, u32[]{:S(2)}, u32[]{:S(2)}) collective-permute-start(bf16[64,1024]{1,0:T(8,128)(2,1)} %get-tuple-element.46), channel_id=1, source_target_pairs={{0,32},{32,0},{64,96},{96,64},{128,160},{160,128},{192,224},{224,1... | collective-permute-start | bytes 393224 | tf_op jit(solution)/shard_map/ppermute | solution.py:460
  102.3 12.9 %collective-permute-start.12 = (bf16[64,1024]{1,0:T(8,128)(2,1)}, bf16[64,1024]{1,0:T(8,128)(2,1)S(1)}, u32[]{:S(2)}, u32[]{:S(2)}) collective-permute-start(bf16[64,1024]{1,0:T(8,128)(2,1)} %get-tuple-element.53), channel_id=1, source_target_pairs={{0,4},{1,5},{2,6},{3,7},{4,0},{5,1},{6,2},{7,3},{8,12},{9,13},{10,... | collective-permute-start | bytes 393224 | tf_op jit(solution)/shard_map/ppermute | solution.py:457
  104.2 11.0 %collective-permute-start.9 = (bf16[32,1024]{1,0:T(8,128)(2,1)}, bf16[32,1024]{1,0:T(8,128)(2,1)S(1)}, u32[]{:S(2)}, u32[]{:S(2)}) collective-permute-start(bf16[32,1024]{1,0:T(8,128)(2,1)} %get-tuple-element.47), channel_id=1, source_target_pairs={{0,64},{32,96},{64,0},{96,32},{128,192},{160,224},{192,128},{224,1... | collective-permute-start | bytes 196616 | tf_op jit(solution)/shard_map/ppermute | solution.py:460
  107.8 7.4 %collective-permute-start.10 = (bf16[32,1024]{1,0:T(8,128)(2,1)}, bf16[32,1024]{1,0:T(8,128)(2,1)S(1)}, u32[]{:S(2)}, u32[]{:S(2)}) collective-permute-start(bf16[32,1024]{1,0:T(8,128)(2,1)} %get-tuple-element.48), channel_id=1, source_target_pairs={{0,96},{32,64},{64,32},{96,0},{128,224},{160,192},{192,160},{224,1... | collective-permute-start | bytes 196616 | tf_op jit(solution)/shard_map/ppermute | solution.py:460
  115.2 40.6 %copy-start.1 = (f32[256,1024]{1,0:T(8,128)S(1)}, f32[256,1024]{1,0:T(8,128)}, u32[]{:S(2)}) copy-start(f32[256,1024]{1,0:T(8,128)} %get-tuple-element.44.own) | copy-start | bytes 3145732
  117.1 0.6 copy-start.10
  117.7 17.4 %copy-start.11 = (bf16[32,1024]{1,0:T(8,128)(2,1)S(1)}, bf16[32,1024]{1,0:T(8,128)(2,1)}, u32[]{:S(2)}) copy-start(bf16[32,1024]{1,0:T(8,128)(2,1)} %copy-done.10) | copy-start | bytes 196612
  117.7 38.1 %all-to-all-start.3 = ((bf16[32,8,1024]{2,1,0:T(8,128)(2,1)}), bf16[32,8,1024]{2,1,0:T(8,128)(2,1)S(1)}, u32[]{:S(2)}, u32[]{:S(2)}) async-start(bf16[32,8,1024]{2,1,0:T(8,128)(2,1)} %bitcast.6), calls=%async_computation.3 | async-start | bytes 1048576 | tf_op jit(solution)/shard_map/all_to_all | solution.py:524
  132.0 23.9 %collective-permute-start.13 = (bf16[192,1024]{1,0:T(8,128)(2,1)S(1)}, bf16[192,1024]{1,0:T(8,128)(2,1)S(1)}, u32[]{:S(2)}, u32[]{:S(2)}) collective-permute-start(bf16[192,1024]{1,0:T(8,128)(2,1)S(1)} %get-tuple-element.56), channel_id=1, source_target_pairs={{0,1},{1,0},{2,3},{3,2},{4,5},{5,4},{6,7},{7,6},{8,9},{9,8},{10,11... | collective-permute-start | bytes 1179656 | tf_op jit(solution)/shard_map/ppermute | solution.py:457
  135.1 16.2 %collective-permute-start.14 = (bf16[32,1024]{1,0:T(8,128)(2,1)S(1)}, bf16[32,1024]{1,0:T(8,128)(2,1)S(1)}, u32[]{:S(2)}, u32[]{:S(2)}) collective-permute-start(bf16[32,1024]{1,0:T(8,128)(2,1)S(1)} %copy-done.11), channel_id=1, source_target_pairs={{0,2},{1,3},{2,0},{3,1},{4,6},{5,7},{6,4},{7,5},{8,10},{9,11},{10,... | collective-permute-start | bytes 196616 | tf_op jit(solution)/shard_map/ppermute | solution.py:457
  139.1 16.7 %collective-permute-start.15 = (bf16[32,1024]{1,0:T(8,128)(2,1)S(1)}, bf16[32,1024]{1,0:T(8,128)(2,1)S(1)}, u32[]{:S(2)}, u32[]{:S(2)}) collective-permute-start(bf16[32,1024]{1,0:T(8,128)(2,1)S(1)} %get-tuple-element.59), channel_id=1, source_target_pairs={{0,3},{1,2},{2,1},{3,0},{4,7},{5,6},{6,5},{7,4},{8,11},{9,10},{10,... | collective-permute-start | bytes 196616 | tf_op jit(solution)/shard_map/ppermute | solution.py:457
  155.9 0.7 copy-start.9

commit v5 on v4

--- a/solution.py
+++ b/solution.py
@@ -326,7 +326,7 @@
                 if factor is not None:
                     res = res * factor
                 far = res[:far_rows] * inverse[...]
-                own_grad[:, cols] = res[far_rows:]
+                own_grad[:, cols] = res[far_rows:].astype(bf16)
                 low_grad[:, cols] = far[: 2 * COARSE].astype(bf16)
                 three_out[:, cols] = far[2 * COARSE : 3 * COARSE].astype(bf16)
                 shard_part[:, cols] = far[3 * COARSE : 5 * COARSE].astype(bf16)
@@ -364,7 +364,7 @@
         pltpu.VMEM((key_rows, 2 * BLOCK), f32),
     ]
     outs = [
-        shape(2 * BLOCK, width), shape(2 * BLOCK, width), shape(2 * BLOCK, 2 * width, f32),
+        shape(2 * BLOCK, width), shape(2 * BLOCK, width), shape(2 * BLOCK, 2 * width),
         shape(BLOCK, 2 * width), shape(BLOCK, 2 * width), shape(2 * COARSE, 2 * width),
         shape(COARSE, 2 * width), shape(2 * COARSE, 2 * width), shape(COARSE, 2 * width),
         shape(half, 2 * width), shape(half, 2 * width), shape(group_rows, 2 * width),
@@ -428,7 +428,7 @@
         for i, (block, near) in enumerate(((1 - parity, sib_back), (parity, oth_back))):
             start = pl.multiple_of(block * BLOCK, BLOCK)
             live = (rows_of((BLOCK, LANES)) + start < length).astype(f32)
-            grad = own[pl.ds(i * BLOCK, BLOCK)] + near[pl.ds(0, BLOCK)].astype(f32)
+            grad = own[pl.ds(i * BLOCK, BLOCK)].astype(f32) + near[pl.ds(0, BLOCK)].astype(f32)
             grad = grad + spread[pl.ds(start, BLOCK)] * by_lanes(live, 2 * width)
             key_grad[pl.ds(start, BLOCK)] = grad[:, :width].astype(bf16)
             value_grad[pl.ds(start, BLOCK)] = grad[:, width:].astype(bf16)

time: 159 us -> 158 us (level)
  no operation moved by 1% of the time
where the time goes in v5:
time: 158 us; the launch traced here: 157 us
  starting transfers between devices  92.7 us (59%)
  waiting for transfers between devices  44.8 us (28%)
  Pallas kernels  17.4 us (11%)
    ppermute x8, waiting for transfers between devices, on_shard(): return lax.ppermute(x, 'shard', flip(shards, bits))  30.6 us
    ppermute x8, starting transfers between devices, on_shard(): return lax.ppermute(x, 'shard', flip(shards, bits))  22.2 us
    pallas_call x5, Pallas kernels, call(): pl.pallas_call(kernel, out_shape=outs, in_specs=in_specs, out_specs=[pl.B...  17.4 us
    ppermute x6, starting transfers between devices, on_group(): return lax.ppermute(x, 'grp', flip(groups, bits))  15.6 us
    all_to_all x1, starting transfers between devices, body(): shard_back = lax.all_to_all(shard_out, 'shard', 0, 0, tiled=True)  14.2 us
    all_to_all x1, starting transfers between devices, body(): lax.all_to_all(gather, 'shard', 0, 0, tiled=True)  13.6 us
    all_to_all x1, starting transfers between devices, body(): lax.all_to_all(wide, 'grp', 0, 0, tiled=True)  11.9 us
    all_to_all x1, waiting for transfers between devices, body(): lax.all_to_all(wide, 'grp', 0, 0, tiled=True)  5.33 us
  transfers between devices with their start and end apart: 20, of which 8 were waited for; matrix products, arithmetic and copies ran while one was open for 0% of the time, Pallas kernels for 0%

profile of v5, /device:TPU:1, one launch (start us, length us, event | category | flops | bytes accessed | tf_op | source)
XLA Modules:
  0.0 157.4 jit_solution(8352158721063721241)
XLA Ops:
  0.6 2.5 %local.1 = (bf16[192,1152]{1,0:T(8,128)(2,1)}, bf16[128,1152]{1,0:T(8,128)(2,1)}, bf16[32,1152]{1,0:T(8,128)(2,1)}, bf16[32,8,1152]{2,1,0:T(8,128)(2,1)}) custom-call(s32[1]{0:T(128)} %bitcast.index, s32[1,256]{1,0:T(1,128)} %bitcast.10, bf16[256,512]{1,0:T(8,128)(2,1)} %key.1, bf16[256,512]{1,0:T(8,128)(2,1)} %value.1), custom_call_target="tpu_custom_call" | custom-call | bytes 1926144 | tf_op jit(solution)/shard_map/local/pallas_call | solution.py:43
  3.1 13.6 %all-to-all-start = ((bf16[32,8,1152]{2,1,0:T(8,128)(2,1)}), bf16[32,8,1152]{2,1,0:T(8,128)(2,1)S(1)}, u32[]{:S(2)}, u32[]{:S(2)}) async-start(bf16[32,8,1152]{2,1,0:T(8,128)(2,1)} %get-tuple-element.37), calls=%async_computation | async-start | bytes 1179648 | tf_op jit(solution)/shard_map/all_to_all | solution.py:476
  16.7 3.1 %collective-permute-start = (bf16[192,1152]{1,0:T(8,128)(2,1)S(1)}, bf16[192,1152]{1,0:T(8,128)(2,1)S(1)}, u32[]{:S(2)}, u32[]{:S(2)}) collective-permute-start(bf16[192,1152]{1,0:T(8,128)(2,1)S(1)} %copy-done.11), channel_id=1, source_target_pairs={{0,1},{1,0},{2,3},{3,2},{4,5},{5,4},{6,7},{7,6},{8,9},{9,8},{10,11... | collective-permute-start | bytes 1327112 | tf_op jit(solution)/shard_map/ppermute | solution.py:457
  19.9 4.0 %collective-permute-start.3 = (bf16[32,1152]{1,0:T(8,128)(2,1)S(1)}, bf16[32,1152]{1,0:T(8,128)(2,1)S(1)}, u32[]{:S(2)}, u32[]{:S(2)}) collective-permute-start(bf16[32,1152]{1,0:T(8,128)(2,1)S(1)} %copy-done.8), channel_id=1, source_target_pairs={{0,3},{1,2},{2,1},{3,0},{4,7},{5,6},{6,5},{7,4},{8,11},{9,10},{10,... | collective-permute-start | bytes 221192 | tf_op jit(solution)/shard_map/ppermute | solution.py:457
  23.9 1.9 %collective-permute-start.2 = (bf16[32,1152]{1,0:T(8,128)(2,1)S(1)}, bf16[32,1152]{1,0:T(8,128)(2,1)S(1)}, u32[]{:S(2)}, u32[]{:S(2)}) collective-permute-start(bf16[32,1152]{1,0:T(8,128)(2,1)S(1)} %copy-done.8), channel_id=1, source_target_pairs={{0,2},{1,3},{2,0},{3,1},{4,6},{5,7},{6,4},{7,5},{8,10},{9,11},{10,... | collective-permute-start | bytes 221192 | tf_op jit(solution)/shard_map/ppermute | solution.py:457
  25.8 16.0 %collective-permute-done.3.pair_b = bf16[32,1152]{1,0:T(8,128)(2,1)S(1)} collective-permute-done((bf16[32,1152]{1,0:T(8,128)(2,1)S(1)}, bf16[32,1152]{1,0:T(8,128)(2,1)S(1)}, u32[]{:S(2)}, u32[]{:S(2)}) %collective-permute-start.3) | collective-permute-done | bytes 73760 | tf_op jit(solution)/shard_map/ppermute | solution.py:457
  41.8 0.0 collective-permute-done.2.pair_a
  41.8 0.0 collective-permute-done.sib_in
  41.8 0.0 all-to-all-done
  41.9 2.1 %climb.1 = (bf16[64,1152]{1,0:T(8,128)(2,1)S(1)}, bf16[64,1152]{1,0:T(8,128)(2,1)S(1)}, bf16[32,1152]{1,0:T(8,128)(2,1)S(1)}, bf16[16,16,1024]{2,1,0:T(8,128)(2,1)}, f32[24,128]{1,0:T(8,128)S(1)}) custom-call(s32[1]{0:T(128)} %bitcast.index, bf16[192,1152]{1,0:T(8,128)(2,1)S(1)} %collective-permute-done.sib_in, bf16[32,1152]{1,0:T(8,128)(2,1)S(1)} %copy-done.8, ...), custom_call_target="tpu_custom_call" | custom-call | bytes 2158592 | tf_op jit(solution)/shard_map/climb/pallas_call | solution.py:43
  44.0 11.9 %all-to-all-start.1 = ((bf16[16,16,1024]{2,1,0:T(8,128)(2,1)}), bf16[16,16,1024]{2,1,0:T(8,128)(2,1)S(1)}, u32[]{:S(2)}, u32[]{:S(2)}) async-start(bf16[16,16,1024]{2,1,0:T(8,128)(2,1)} %get-tuple-element.41), calls=%async_computation.1 | async-start | bytes 1048576 | tf_op jit(solution)/shard_map/all_to_all | solution.py:494
  55.9 5.2 %collective-permute-start.1 = (bf16[128,1152]{1,0:T(8,128)(2,1)S(1)}, bf16[128,1152]{1,0:T(8,128)(2,1)S(1)}, u32[]{:S(2)}, u32[]{:S(2)}) collective-permute-start(bf16[128,1152]{1,0:T(8,128)(2,1)S(1)} %copy-done.12), channel_id=1, source_target_pairs={{1,2},{3,4},{5,6},{7,8},{9,10},{11,12},{13,14},{15,16},{17,18},{19... | collective-permute-start | bytes 884744 | tf_op jit(solution)/shard_map/ppermute | solution.py:475
  61.1 1.9 %collective-permute-start.4 = (bf16[64,1152]{1,0:T(8,128)(2,1)S(1)}, bf16[64,1152]{1,0:T(8,128)(2,1)S(1)}, u32[]{:S(2)}, u32[]{:S(2)}) collective-permute-start(bf16[64,1152]{1,0:T(8,128)(2,1)S(1)} %get-tuple-element.38), channel_id=1, source_target_pairs={{0,4},{1,5},{2,6},{3,7},{4,0},{5,1},{6,2},{7,3},{8,12},{9,13},{10,... | collective-permute-start | bytes 442376 | tf_op jit(solution)/shard_map/ppermute | solution.py:457
  63.0 1.9 %collective-permute-start.5 = (bf16[64,1152]{1,0:T(8,128)(2,1)S(1)}, bf16[64,1152]{1,0:T(8,128)(2,1)S(1)}, u32[]{:S(2)}, u32[]{:S(2)}) collective-permute-start(bf16[64,1152]{1,0:T(8,128)(2,1)S(1)} %get-tuple-element.39), channel_id=1, source_target_pairs={{0,32},{32,0},{64,96},{96,64},{128,160},{160,128},{192,224},{224,1... | collective-permute-start | bytes 442376 | tf_op jit(solution)/shard_map/ppermute | solution.py:460
  65.0 3.9 %collective-permute-start.7 = (bf16[32,1152]{1,0:T(8,128)(2,1)S(1)}, bf16[32,1152]{1,0:T(8,128)(2,1)S(1)}, u32[]{:S(2)}, u32[]{:S(2)}) collective-permute-start(bf16[32,1152]{1,0:T(8,128)(2,1)S(1)} %get-tuple-element.40), channel_id=1, source_target_pairs={{0,96},{32,64},{64,32},{96,0},{128,224},{160,192},{192,160},{224,1... | collective-permute-start | bytes 221192 | tf_op jit(solution)/shard_map/ppermute | solution.py:460
  68.9 1.9 %collective-permute-start.6 = (bf16[32,1152]{1,0:T(8,128)(2,1)S(1)}, bf16[32,1152]{1,0:T(8,128)(2,1)S(1)}, u32[]{:S(2)}, u32[]{:S(2)}) collective-permute-start(bf16[32,1152]{1,0:T(8,128)(2,1)S(1)} %get-tuple-element.40), channel_id=1, source_target_pairs={{0,64},{32,96},{64,0},{96,32},{128,192},{160,224},{192,128},{224,1... | collective-permute-start | bytes 221192 | tf_op jit(solution)/shard_map/ppermute | solution.py:460
  70.8 0.2 collective-permute-done.1.oth_in
  71.0 0.8 collective-permute-done.7.seven_b
  71.8 2.9 %collective-permute-done.6.seven_a = bf16[32,1152]{1,0:T(8,128)(2,1)S(1)} collective-permute-done((bf16[32,1152]{1,0:T(8,128)(2,1)S(1)}, bf16[32,1152]{1,0:T(8,128)(2,1)S(1)}, u32[]{:S(2)}, u32[]{:S(2)}) %collective-permute-start.6) | collective-permute-done | bytes 73760 | tf_op jit(solution)/shard_map/ppermute | solution.py:460
  74.7 0.0 collective-permute-done.4.three_in
  74.7 0.0 collective-permute-done.5.six_in
  74.7 5.3 %all-to-all-done.1 = bf16[16,16,1024]{2,1,0:T(8,128)(2,1)S(1)} async-done(((bf16[16,16,1024]{2,1,0:T(8,128)(2,1)}), bf16[16,16,1024]{2,1,0:T(8,128)(2,1)S(1)}, u32[]{:S(2)}, u32[]{:S(2)}) %all-to-all-start.1) | async-done | bytes 524320 | tf_op jit(solution)/shard_map/all_to_all | solution.py:494
  80.1 0.8 copy-done.10
  80.9 9.3 %attention.1 = (bf16[256,512]{1,0:T(8,128)(2,1)}, bf16[256,512]{1,0:T(8,128)(2,1)}, bf16[256,1024]{1,0:T(8,128)(2,1)}, bf16[128,1024]{1,0:T(8,128)(2,1)}, bf16[1...) custom-call(s32[1]{0:T(128)} %bitcast.index, ...), custom_call_target="tpu_custom_call" | custom-call | flops 1600000000 | bytes 6717440 | tf_op jit(solution)/shard_map/attention/pallas_call | solution.py:43
  90.2 0.0 copy-start.14
  90.2 0.0 copy-start.3
  90.2 5.2 %all-to-all-start.2 = ((bf16[16,16,1024]{2,1,0:T(8,128)(2,1)}), bf16[16,16,1024]{2,1,0:T(8,128)(2,1)S(1)}, u32[]{:S(2)}, u32[]{:S(2)}) async-start(bf16[16,16,1024]{2,1,0:T(8,128)(2,1)} %bitcast.13), calls=%async_computation.2 | async-start | bytes 1048576 | tf_op jit(solution)/shard_map/all_to_all | solution.py:509
  95.4 4.8 %collective-permute-start.11 = (bf16[128,1024]{1,0:T(8,128)(2,1)S(1)}, bf16[128,1024]{1,0:T(8,128)(2,1)S(1)}, u32[]{:S(2)}, u32[]{:S(2)}) collective-permute-start(bf16[128,1024]{1,0:T(8,128)(2,1)S(1)} %copy-done.14), channel_id=1, source_target_pairs={{1,2},{3,4},{5,6},{7,8},{9,10},{11,12},{13,14},{15,16},{17,18},{19... | collective-permute-start | bytes 786440 | tf_op jit(solution)/shard_map/ppermute | solution.py:508
  100.2 1.9 %collective-permute-start.8 = (bf16[64,1024]{1,0:T(8,128)(2,1)}, bf16[64,1024]{1,0:T(8,128)(2,1)S(1)}, u32[]{:S(2)}, u32[]{:S(2)}) collective-permute-start(bf16[64,1024]{1,0:T(8,128)(2,1)} %get-tuple-element.46), channel_id=1, source_target_pairs={{0,32},{32,0},{64,96},{96,64},{128,160},{160,128},{192,224},{224,1... | collective-permute-start | bytes 393224 | tf_op jit(solution)/shard_map/ppermute | solution.py:460
  102.2 1.9 %collective-permute-start.12 = (bf16[64,1024]{1,0:T(8,128)(2,1)}, bf16[64,1024]{1,0:T(8,128)(2,1)S(1)}, u32[]{:S(2)}, u32[]{:S(2)}) collective-permute-start(bf16[64,1024]{1,0:T(8,128)(2,1)} %get-tuple-element.53), channel_id=1, source_target_pairs={{0,4},{1,5},{2,6},{3,7},{4,0},{5,1},{6,2},{7,3},{8,12},{9,13},{10,... | collective-permute-start | bytes 393224 | tf_op jit(solution)/shard_map/ppermute | solution.py:457
  104.1 3.5 %collective-permute-start.9 = (bf16[32,1024]{1,0:T(8,128)(2,1)}, bf16[32,1024]{1,0:T(8,128)(2,1)S(1)}, u32[]{:S(2)}, u32[]{:S(2)}) collective-permute-start(bf16[32,1024]{1,0:T(8,128)(2,1)} %get-tuple-element.47), channel_id=1, source_target_pairs={{0,64},{32,96},{64,0},{96,32},{128,192},{160,224},{192,128},{224,1... | collective-permute-start | bytes 196616 | tf_op jit(solution)/shard_map/ppermute | solution.py:460
  107.7 2.4 %collective-permute-start.10 = (bf16[32,1024]{1,0:T(8,128)(2,1)}, bf16[32,1024]{1,0:T(8,128)(2,1)S(1)}, u32[]{:S(2)}, u32[]{:S(2)}) collective-permute-start(bf16[32,1024]{1,0:T(8,128)(2,1)} %get-tuple-element.48), channel_id=1, source_target_pairs={{0,96},{32,64},{64,32},{96,0},{128,224},{160,192},{192,160},{224,1... | collective-permute-start | bytes 196616 | tf_op jit(solution)/shard_map/ppermute | solution.py:460
  110.1 0.0 collective-permute-done.11.oth_back
  110.1 5.0 %all-to-all-done.2 = bf16[16,16,1024]{2,1,0:T(8,128)(2,1)S(1)} async-done(((bf16[16,16,1024]{2,1,0:T(8,128)(2,1)}), bf16[16,16,1024]{2,1,0:T(8,128)(2,1)S(1)}, u32[]{:S(2)}, u32[]{:S(2)}) %all-to-all-start.2) | async-done | bytes 524320 | tf_op jit(solution)/shard_map/all_to_all | solution.py:509
  115.1 0.0 collective-permute-done.9.seven_a
  115.1 0.0 collective-permute-done.8.six
  115.1 0.0 collective-permute-done.12.three
  115.1 1.8 %back.1 = (bf16[256,1024]{1,0:T(8,128)(2,1)}, bf16[192,1024]{1,0:T(8,128)(2,1)S(1)}, bf16[32,1024]{1,0:T(8,128)(2,1)S(1)}, bf16[32,1024]{1,0:T(8,128)(2,1)S(1)}, f32[16,1024]{1,0:T(8,128)S(1)}) custom-call(s32[1]{0:T(128)} %bitcast.index, bf16[128,1024]{1,0:T(8,128)(2,1)S(1)} %copy-done.5, bf16[64,1024]{1,0:T(8,128)(2,1)S(1)} %collective-permute-done.8.six, ...), custom_call_target="tpu_custom_call" | custom-call | bytes 2830336 | tf_op jit(solution)/shard_map/back/pallas_call | solution.py:43
  117.0 14.2 %all-to-all-start.3 = ((bf16[32,8,1024]{2,1,0:T(8,128)(2,1)}), bf16[32,8,1024]{2,1,0:T(8,128)(2,1)S(1)}, u32[]{:S(2)}, u32[]{:S(2)}) async-start(bf16[32,8,1024]{2,1,0:T(8,128)(2,1)} %bitcast.6), calls=%async_computation.3 | async-start | bytes 1048576 | tf_op jit(solution)/shard_map/all_to_all | solution.py:524
  131.2 3.1 %collective-permute-start.13 = (bf16[192,1024]{1,0:T(8,128)(2,1)S(1)}, bf16[192,1024]{1,0:T(8,128)(2,1)S(1)}, u32[]{:S(2)}, u32[]{:S(2)}) collective-permute-start(bf16[192,1024]{1,0:T(8,128)(2,1)S(1)} %get-tuple-element.56), channel_id=1, source_target_pairs={{0,1},{1,0},{2,3},{3,2},{4,5},{5,4},{6,7},{7,6},{8,9},{9,8},{10,11... | collective-permute-start | bytes 1179656 | tf_op jit(solution)/shard_map/ppermute | solution.py:457
  134.4 4.0 %collective-permute-start.14 = (bf16[32,1024]{1,0:T(8,128)(2,1)S(1)}, bf16[32,1024]{1,0:T(8,128)(2,1)S(1)}, u32[]{:S(2)}, u32[]{:S(2)}) collective-permute-start(bf16[32,1024]{1,0:T(8,128)(2,1)S(1)} %get-tuple-element.58), channel_id=1, source_target_pairs={{0,2},{1,3},{2,0},{3,1},{4,6},{5,7},{6,4},{7,5},{8,10},{9,11},{10,... | collective-permute-start | bytes 196616 | tf_op jit(solution)/shard_map/ppermute | solution.py:457
  138.4 2.1 %collective-permute-start.15 = (bf16[32,1024]{1,0:T(8,128)(2,1)S(1)}, bf16[32,1024]{1,0:T(8,128)(2,1)S(1)}, u32[]{:S(2)}, u32[]{:S(2)}) collective-permute-start(bf16[32,1024]{1,0:T(8,128)(2,1)S(1)} %get-tuple-element.59), channel_id=1, source_target_pairs={{0,3},{1,2},{2,1},{3,0},{4,7},{5,6},{6,5},{7,4},{8,11},{9,10},{10,... | collective-permute-start | bytes 196616 | tf_op jit(solution)/shard_map/ppermute | solution.py:457
  140.5 10.1 %collective-permute-done.14.pair_a = bf16[32,1024]{1,0:T(8,128)(2,1)S(1)} collective-permute-done((bf16[32,1024]{1,0:T(8,128)(2,1)S(1)}, bf16[32,1024]{1,0:T(8,128)(2,1)S(1)}, u32[]{:S(2)}, u32[]{:S(2)}) %collective-permute-start.14) | collective-permute-done | bytes 65568 | tf_op jit(solution)/shard_map/ppermute | solution.py:457
  150.6 4.5 %collective-permute-done.15.pair_b = bf16[32,1024]{1,0:T(8,128)(2,1)S(1)} collective-permute-done((bf16[32,1024]{1,0:T(8,128)(2,1)S(1)}, bf16[32,1024]{1,0:T(8,128)(2,1)S(1)}, u32[]{:S(2)}, u32[]{:S(2)}) %collective-permute-start.15) | collective-permute-done | bytes 65568 | tf_op jit(solution)/shard_map/ppermute | solution.py:457
  155.1 0.0 collective-permute-done.13.sib_back
  155.1 0.0 all-to-all-done.3.shard
  155.1 0.7 copy-done.9
  155.8 1.6 %final.1 = (bf16[256,512]{1,0:T(8,128)(2,1)}, bf16[256,512]{1,0:T(8,128)(2,1)}) custom-call(s32[1]{0:T(128)} %bitcast.index, s32[1,256]{1,0:T(1,128)S(1)} %bitcast.11, bf16[256,1024]{1,0:T(8,128)(2,1)S(1)} %copy-done.1, bf16[192,1024]{1,0:T(8,128)(2,1)S(1)} %collective-permute-done.13.sib_back, bf16[128,1024]{1,0:T(8,128)(2,1)S(1)} %collective-permute-done.11.oth_back, ...), custom_call_target="tpu_custom_call" | custom-call | bytes 2425856 | tf_op jit(solution)/shard_map/final/pallas_call | solution.py:43
  (35 shorter events, 0.1 us)
Async XLA Ops:
  3.1 13.6 %copy-start.11 = (bf16[192,1152]{1,0:T(8,128)(2,1)S(1)}, bf16[192,1152]{1,0:T(8,128)(2,1)}, u32[]{:S(2)}) copy-start(bf16[192,1152]{1,0:T(8,128)(2,1)} %get-tuple-element.34.sib) | copy-start | bytes 1327108
  3.1 16.8 %copy-start.8 = (bf16[32,1152]{1,0:T(8,128)(2,1)S(1)}, bf16[32,1152]{1,0:T(8,128)(2,1)}, u32[]{:S(2)}) copy-start(bf16[32,1152]{1,0:T(8,128)(2,1)} %get-tuple-element.36.pair) | copy-start | bytes 221188
  3.1 38.7 %all-to-all-start = ((bf16[32,8,1152]{2,1,0:T(8,128)(2,1)}), bf16[32,8,1152]{2,1,0:T(8,128)(2,1)S(1)}, u32[]{:S(2)}, u32[]{:S(2)}) async-start(bf16[32,8,1152]{2,1,0:T(8,128)(2,1)} %get-tuple-element.37), calls=%async_computation | async-start | bytes 1179648 | tf_op jit(solution)/shard_map/all_to_all | solution.py:476
  16.7 25.1 %collective-permute-start = (bf16[192,1152]{1,0:T(8,128)(2,1)S(1)}, bf16[192,1152]{1,0:T(8,128)(2,1)S(1)}, u32[]{:S(2)}, u32[]{:S(2)}) collective-permute-start(bf16[192,1152]{1,0:T(8,128)(2,1)S(1)} %copy-done.11), channel_id=1, source_target_pairs={{0,1},{1,0},{2,3},{3,2},{4,5},{5,4},{6,7},{7,6},{8,9},{9,8},{10,11... | collective-permute-start | bytes 1327112 | tf_op jit(solution)/shard_map/ppermute | solution.py:457
  19.9 21.9 %collective-permute-start.3 = (bf16[32,1152]{1,0:T(8,128)(2,1)S(1)}, bf16[32,1152]{1,0:T(8,128)(2,1)S(1)}, u32[]{:S(2)}, u32[]{:S(2)}) collective-permute-start(bf16[32,1152]{1,0:T(8,128)(2,1)S(1)} %copy-done.8), channel_id=1, source_target_pairs={{0,3},{1,2},{2,1},{3,0},{4,7},{5,6},{6,5},{7,4},{8,11},{9,10},{10,... | collective-permute-start | bytes 221192 | tf_op jit(solution)/shard_map/ppermute | solution.py:457
  23.9 17.9 %collective-permute-start.2 = (bf16[32,1152]{1,0:T(8,128)(2,1)S(1)}, bf16[32,1152]{1,0:T(8,128)(2,1)S(1)}, u32[]{:S(2)}, u32[]{:S(2)}) collective-permute-start(bf16[32,1152]{1,0:T(8,128)(2,1)S(1)} %copy-done.8), channel_id=1, source_target_pairs={{0,2},{1,3},{2,0},{3,1},{4,6},{5,7},{6,4},{7,5},{8,10},{9,11},{10,... | collective-permute-start | bytes 221192 | tf_op jit(solution)/shard_map/ppermute | solution.py:457
  41.8 2.2 %copy-start.6 = (bf16[32,1152]{1,0:T(8,128)(2,1)}, bf16[32,1152]{1,0:T(8,128)(2,1)S(1)}, u32[]{:S(2)}) copy-start(bf16[32,1152]{1,0:T(8,128)(2,1)S(1)} %collective-permute-done.3.pair_b) | copy-start | bytes 221188
  41.8 2.2 %copy-start.7 = (bf16[32,1152]{1,0:T(8,128)(2,1)}, bf16[32,1152]{1,0:T(8,128)(2,1)S(1)}, u32[]{:S(2)}) copy-start(bf16[32,1152]{1,0:T(8,128)(2,1)S(1)} %collective-permute-done.2.pair_a) | copy-start | bytes 221188
  41.8 2.2 %copy-start.2 = (bf16[192,1152]{1,0:T(8,128)(2,1)}, bf16[192,1152]{1,0:T(8,128)(2,1)S(1)}, u32[]{:S(2)}) copy-start(bf16[192,1152]{1,0:T(8,128)(2,1)S(1)} %collective-permute-done.sib_in) | copy-start | bytes 1327108
  41.8 2.2 %copy-start = (bf16[32,8,1152]{2,1,0:T(8,128)(2,1)}, bf16[32,8,1152]{2,1,0:T(8,128)(2,1)S(1)}, u32[]{:S(2)}) copy-start(bf16[32,8,1152]{2,1,0:T(8,128)(2,1)S(1)} %all-to-all-done) | copy-start | bytes 1769476
  44.0 11.9 %copy-start.12 = (bf16[128,1152]{1,0:T(8,128)(2,1)S(1)}, bf16[128,1152]{1,0:T(8,128)(2,1)}, u32[]{:S(2)}) copy-start(bf16[128,1152]{1,0:T(8,128)(2,1)} %get-tuple-element.35.oth) | copy-start | bytes 884740
  44.0 36.0 %all-to-all-start.1 = ((bf16[16,16,1024]{2,1,0:T(8,128)(2,1)}), bf16[16,16,1024]{2,1,0:T(8,128)(2,1)S(1)}, u32[]{:S(2)}, u32[]{:S(2)}) async-start(bf16[16,16,1024]{2,1,0:T(8,128)(2,1)} %get-tuple-element.41), calls=%async_computation.1 | async-start | bytes 1048576 | tf_op jit(solution)/shard_map/all_to_all | solution.py:494
  55.9 15.1 %collective-permute-start.1 = (bf16[128,1152]{1,0:T(8,128)(2,1)S(1)}, bf16[128,1152]{1,0:T(8,128)(2,1)S(1)}, u32[]{:S(2)}, u32[]{:S(2)}) collective-permute-start(bf16[128,1152]{1,0:T(8,128)(2,1)S(1)} %copy-done.12), channel_id=1, source_target_pairs={{1,2},{3,4},{5,6},{7,8},{9,10},{11,12},{13,14},{15,16},{17,18},{19... | collective-permute-start | bytes 884744 | tf_op jit(solution)/shard_map/ppermute | solution.py:475
  61.1 13.6 %collective-permute-start.4 = (bf16[64,1152]{1,0:T(8,128)(2,1)S(1)}, bf16[64,1152]{1,0:T(8,128)(2,1)S(1)}, u32[]{:S(2)}, u32[]{:S(2)}) collective-permute-start(bf16[64,1152]{1,0:T(8,128)(2,1)S(1)} %get-tuple-element.38), channel_id=1, source_target_pairs={{0,4},{1,5},{2,6},{3,7},{4,0},{5,1},{6,2},{7,3},{8,12},{9,13},{10,... | collective-permute-start | bytes 442376 | tf_op jit(solution)/shard_map/ppermute | solution.py:457
  63.0 11.7 %collective-permute-start.5 = (bf16[64,1152]{1,0:T(8,128)(2,1)S(1)}, bf16[64,1152]{1,0:T(8,128)(2,1)S(1)}, u32[]{:S(2)}, u32[]{:S(2)}) collective-permute-start(bf16[64,1152]{1,0:T(8,128)(2,1)S(1)} %get-tuple-element.39), channel_id=1, source_target_pairs={{0,32},{32,0},{64,96},{96,64},{128,160},{160,128},{192,224},{224,1... | collective-permute-start | bytes 442376 | tf_op jit(solution)/shard_map/ppermute | solution.py:460
  65.0 6.8 %collective-permute-start.7 = (bf16[32,1152]{1,0:T(8,128)(2,1)S(1)}, bf16[32,1152]{1,0:T(8,128)(2,1)S(1)}, u32[]{:S(2)}, u32[]{:S(2)}) collective-permute-start(bf16[32,1152]{1,0:T(8,128)(2,1)S(1)} %get-tuple-element.40), channel_id=1, source_target_pairs={{0,96},{32,64},{64,32},{96,0},{128,224},{160,192},{192,160},{224,1... | collective-permute-start | bytes 221192 | tf_op jit(solution)/shard_map/ppermute | solution.py:460
  68.9 5.8 %collective-permute-start.6 = (bf16[32,1152]{1,0:T(8,128)(2,1)S(1)}, bf16[32,1152]{1,0:T(8,128)(2,1)S(1)}, u32[]{:S(2)}, u32[]{:S(2)}) collective-permute-start(bf16[32,1152]{1,0:T(8,128)(2,1)S(1)} %get-tuple-element.40), channel_id=1, source_target_pairs={{0,64},{32,96},{64,0},{96,32},{128,192},{160,224},{192,128},{224,1... | collective-permute-start | bytes 221192 | tf_op jit(solution)/shard_map/ppermute | solution.py:460
  71.0 9.0 %copy-start.13 = (bf16[128,1152]{1,0:T(8,128)(2,1)}, bf16[128,1152]{1,0:T(8,128)(2,1)S(1)}, u32[]{:S(2)}) copy-start(bf16[128,1152]{1,0:T(8,128)(2,1)S(1)} %collective-permute-done.1.oth_in) | copy-start | bytes 884740
  71.8 8.3 %copy-start.17 = (bf16[32,1152]{1,0:T(8,128)(2,1)}, bf16[32,1152]{1,0:T(8,128)(2,1)S(1)}, u32[]{:S(2)}) copy-start(bf16[32,1152]{1,0:T(8,128)(2,1)S(1)} %collective-permute-done.7.seven_b) | copy-start | bytes 221188
  74.7 5.4 %copy-start.18 = (bf16[32,1152]{1,0:T(8,128)(2,1)}, bf16[32,1152]{1,0:T(8,128)(2,1)S(1)}, u32[]{:S(2)}) copy-start(bf16[32,1152]{1,0:T(8,128)(2,1)S(1)} %collective-permute-done.6.seven_a) | copy-start | bytes 221188
  74.7 5.4 %copy-start.15 = (bf16[64,1152]{1,0:T(8,128)(2,1)}, bf16[64,1152]{1,0:T(8,128)(2,1)S(1)}, u32[]{:S(2)}) copy-start(bf16[64,1152]{1,0:T(8,128)(2,1)S(1)} %collective-permute-done.4.three_in) | copy-start | bytes 442372
  74.7 5.4 %copy-start.16 = (bf16[64,1152]{1,0:T(8,128)(2,1)}, bf16[64,1152]{1,0:T(8,128)(2,1)S(1)}, u32[]{:S(2)}) copy-start(bf16[64,1152]{1,0:T(8,128)(2,1)S(1)} %collective-permute-done.5.six_in) | copy-start | bytes 442372
  80.0 0.8 copy-start.10
  90.2 5.2 %copy-start.14 = (bf16[128,1024]{1,0:T(8,128)(2,1)S(1)}, bf16[128,1024]{1,0:T(8,128)(2,1)}, u32[]{:S(2)}) copy-start(bf16[128,1024]{1,0:T(8,128)(2,1)} %get-tuple-element.49) | copy-start | bytes 786436
  90.2 24.9 %copy-start.3 = (bf16[128,1024]{1,0:T(8,128)(2,1)S(1)}, bf16[128,1024]{1,0:T(8,128)(2,1)}, u32[]{:S(2)}) copy-start(bf16[128,1024]{1,0:T(8,128)(2,1)} %get-tuple-element.55.sib_grad) | copy-start | bytes 786436
  90.2 24.9 %copy-start.4 = (bf16[128,1024]{1,0:T(8,128)(2,1)S(1)}, bf16[128,1024]{1,0:T(8,128)(2,1)}, u32[]{:S(2)}) copy-start(bf16[128,1024]{1,0:T(8,128)(2,1)} %get-tuple-element.54.low) | copy-start | bytes 786436
  90.2 24.9 %copy-start.5 = (bf16[128,1024]{1,0:T(8,128)(2,1)S(1)}, bf16[128,1024]{1,0:T(8,128)(2,1)}, u32[]{:S(2)}) copy-start(bf16[128,1024]{1,0:T(8,128)(2,1)} %get-tuple-element.45.part) | copy-start | bytes 786436
  90.2 24.9 %all-to-all-start.2 = ((bf16[16,16,1024]{2,1,0:T(8,128)(2,1)}), bf16[16,16,1024]{2,1,0:T(8,128)(2,1)S(1)}, u32[]{:S(2)}, u32[]{:S(2)}) async-start(bf16[16,16,1024]{2,1,0:T(8,128)(2,1)} %bitcast.13), calls=%async_computation.2 | async-start | bytes 1048576 | tf_op jit(solution)/shard_map/all_to_all | solution.py:509
  95.4 14.6 %collective-permute-start.11 = (bf16[128,1024]{1,0:T(8,128)(2,1)S(1)}, bf16[128,1024]{1,0:T(8,128)(2,1)S(1)}, u32[]{:S(2)}, u32[]{:S(2)}) collective-permute-start(bf16[128,1024]{1,0:T(8,128)(2,1)S(1)} %copy-done.14), channel_id=1, source_target_pairs={{1,2},{3,4},{5,6},{7,8},{9,10},{11,12},{13,14},{15,16},{17,18},{19... | collective-permute-start | bytes 786440 | tf_op jit(solution)/shard_map/ppermute | solution.py:508
  100.2 14.8 %collective-permute-start.8 = (bf16[64,1024]{1,0:T(8,128)(2,1)}, bf16[64,1024]{1,0:T(8,128)(2,1)S(1)}, u32[]{:S(2)}, u32[]{:S(2)}) collective-permute-start(bf16[64,1024]{1,0:T(8,128)(2,1)} %get-tuple-element.46), channel_id=1, source_target_pairs={{0,32},{32,0},{64,96},{96,64},{128,160},{160,128},{192,224},{224,1... | collective-permute-start | bytes 393224 | tf_op jit(solution)/shard_map/ppermute | solution.py:460
  102.2 12.9 %collective-permute-start.12 = (bf16[64,1024]{1,0:T(8,128)(2,1)}, bf16[64,1024]{1,0:T(8,128)(2,1)S(1)}, u32[]{:S(2)}, u32[]{:S(2)}) collective-permute-start(bf16[64,1024]{1,0:T(8,128)(2,1)} %get-tuple-element.53), channel_id=1, source_target_pairs={{0,4},{1,5},{2,6},{3,7},{4,0},{5,1},{6,2},{7,3},{8,12},{9,13},{10,... | collective-permute-start | bytes 393224 | tf_op jit(solution)/shard_map/ppermute | solution.py:457
  104.1 11.0 %collective-permute-start.9 = (bf16[32,1024]{1,0:T(8,128)(2,1)}, bf16[32,1024]{1,0:T(8,128)(2,1)S(1)}, u32[]{:S(2)}, u32[]{:S(2)}) collective-permute-start(bf16[32,1024]{1,0:T(8,128)(2,1)} %get-tuple-element.47), channel_id=1, source_target_pairs={{0,64},{32,96},{64,0},{96,32},{128,192},{160,224},{192,128},{224,1... | collective-permute-start | bytes 196616 | tf_op jit(solution)/shard_map/ppermute | solution.py:460
  107.7 7.4 %collective-permute-start.10 = (bf16[32,1024]{1,0:T(8,128)(2,1)}, bf16[32,1024]{1,0:T(8,128)(2,1)S(1)}, u32[]{:S(2)}, u32[]{:S(2)}) collective-permute-start(bf16[32,1024]{1,0:T(8,128)(2,1)} %get-tuple-element.48), channel_id=1, source_target_pairs={{0,96},{32,64},{64,32},{96,0},{128,224},{160,192},{192,160},{224,1... | collective-permute-start | bytes 196616 | tf_op jit(solution)/shard_map/ppermute | solution.py:460
  117.0 38.2 %copy-start.1 = (bf16[256,1024]{1,0:T(8,128)(2,1)S(1)}, bf16[256,1024]{1,0:T(8,128)(2,1)}, u32[]{:S(2)}) copy-start(bf16[256,1024]{1,0:T(8,128)(2,1)} %get-tuple-element.44.own) | copy-start | bytes 1572868
  117.0 38.1 %all-to-all-start.3 = ((bf16[32,8,1024]{2,1,0:T(8,128)(2,1)}), bf16[32,8,1024]{2,1,0:T(8,128)(2,1)S(1)}, u32[]{:S(2)}, u32[]{:S(2)}) async-start(bf16[32,8,1024]{2,1,0:T(8,128)(2,1)} %bitcast.6), calls=%async_computation.3 | async-start | bytes 1048576 | tf_op jit(solution)/shard_map/all_to_all | solution.py:524
  131.2 23.9 %collective-permute-start.13 = (bf16[192,1024]{1,0:T(8,128)(2,1)S(1)}, bf16[192,1024]{1,0:T(8,128)(2,1)S(1)}, u32[]{:S(2)}, u32[]{:S(2)}) collective-permute-start(bf16[192,1024]{1,0:T(8,128)(2,1)S(1)} %get-tuple-element.56), channel_id=1, source_target_pairs={{0,1},{1,0},{2,3},{3,2},{4,5},{5,4},{6,7},{7,6},{8,9},{9,8},{10,11... | collective-permute-start | bytes 1179656 | tf_op jit(solution)/shard_map/ppermute | solution.py:457
  134.4 16.2 %collective-permute-start.14 = (bf16[32,1024]{1,0:T(8,128)(2,1)S(1)}, bf16[32,1024]{1,0:T(8,128)(2,1)S(1)}, u32[]{:S(2)}, u32[]{:S(2)}) collective-permute-start(bf16[32,1024]{1,0:T(8,128)(2,1)S(1)} %get-tuple-element.58), channel_id=1, source_target_pairs={{0,2},{1,3},{2,0},{3,1},{4,6},{5,7},{6,4},{7,5},{8,10},{9,11},{10,... | collective-permute-start | bytes 196616 | tf_op jit(solution)/shard_map/ppermute | solution.py:457
  138.4 16.7 %collective-permute-start.15 = (bf16[32,1024]{1,0:T(8,128)(2,1)S(1)}, bf16[32,1024]{1,0:T(8,128)(2,1)S(1)}, u32[]{:S(2)}, u32[]{:S(2)}) collective-permute-start(bf16[32,1024]{1,0:T(8,128)(2,1)S(1)} %get-tuple-element.59), channel_id=1, source_target_pairs={{0,3},{1,2},{2,1},{3,0},{4,7},{5,6},{6,5},{7,4},{8,11},{9,10},{10,... | collective-permute-start | bytes 196616 | tf_op jit(solution)/shard_map/ppermute | solution.py:457
  155.1 0.7 copy-start.9
